TPU v7x, 512 devices: a whole 4x8x8 slice. The times are simulated.
512 devices in a mesh: batch: 16 (over y, core), seq: 32 (over x, z).
Axes of the slice: x: 4, y: 8, z: 8, core: 2. Of those that a mesh axis runs over, the one named last changes fastest.
Arguments:
- values: bfloat16 [1024, 131072], P(None, ('batch', 'seq')), may hold values from -6 to 6
- gates: bfloat16 [1024, 131072], P(None, ('batch', 'seq')), may hold values from -6 to 6
- cotangent: bfloat16 [1024, 131072], P(None, ('batch', 'seq')), may hold values from -12 to 12
- taps_values: float32 [3, 1024], replicated, may hold values from -3 to 3
- taps_gates: float32 [3, 1024], replicated, may hold values from -3 to 3
- skip_gain: float32 [1024], replicated, may hold values from 0.5 to 1.5
- twiddle: float32 [128, 1024], P('batch'), may hold values from 0.5 to 1.5
- mixing: float32 [128, 128], replicated, may hold values from -2 to 3
- spectrum: bfloat16 [1024, 128, 1024], P('seq', None, 'batch'), may hold values from -4 to 4
Outputs:
- mixed: bfloat16 [1024, 131072], P(None, ('batch', 'seq'))
- grad_values: bfloat16 [1024, 131072], P(None, ('batch', 'seq'))
- grad_gates: bfloat16 [1024, 131072], P(None, ('batch', 'seq'))
- grad_spectrum: float32 [1024, 128, 1024], P('seq', None, 'batch')
- grad_taps_values: float32 [3, 1024], P(None, 'seq')
- grad_taps_gates: float32 [3, 1024], P(None, 'seq')
- grad_skip: float32 [1024], P('seq')
All inputs are finite; a program needn't handle non-finite values.
Results may differ from a plain program's by a relative error of at most 0.0085.
Values may be sent and summed in bfloat16 or wider, within the bound.
No kernel may reach another device: no remote copies, remote signals or barrier semaphores. Data moves between devices by JAX's collectives and lax.ppermute only.
A program may use at most 64 MiB of HBM per device.

v0:
```python
import functools
import math

import jax
import jax.numpy as jnp
import numpy as np
from jax import lax
from jax.experimental import pallas as pl
from jax.experimental.pallas import tpu as pltpu
from jax.sharding import PartitionSpec as P

BLOCK = 1024
F32, BF16 = jnp.float32, jnp.bfloat16


def cas_table():
    indices = np.arange(BLOCK, dtype=np.int32)
    products = indices[:, None] * indices[None, :] % BLOCK
    angles = products.astype(np.float32) * np.float32(2.0 * math.pi / BLOCK)
    table = (np.cos(angles) + np.sin(angles)) / np.float32(math.sqrt(BLOCK))
    return table.astype(jnp.bfloat16)


def lanes(shape=(32, 128)):
    return lax.broadcasted_iota(jnp.int32, shape, 1)


def back_in_time(now, before, steps, lane):
    return jnp.where(lane < steps, before, now)


def rolled(tile):
    return pltpu.roll(tile, 1, 1), pltpu.roll(tile, 2, 1)


def column(cols, at):
    return jnp.broadcast_to(cols[:, at : at + 1], (32, 128))


def spread_kernel(r_ref, rim_ref, cols_ref, tw_ref, cas_ref, out_ref, lhs):
    lane = lanes()
    cols = cols_ref[...]
    tv = [column(cols, k) for k in range(3)]
    tg = [column(cols, 3 + k) for k in range(3)]

    def block(i, carry):
        v1, v2, g1, g2 = carry
        rows = pl.multiple_of(i * 32, 32)
        for t in range(8):
            piece, at = i * 4 + t // 2, (t % 2) * 128
            v = r_ref[piece, 0:32, at : at + 128].astype(F32)
            g = r_ref[piece, 32:64, at : at + 128].astype(F32)
            c = r_ref[piece, 64:96, at : at + 128].astype(F32)
            nv1, nv2 = rolled(v)
            ng1, ng2 = rolled(g)
            short_v = tv[0] * v + tv[1] * back_in_time(nv1, v1, 1, lane) + tv[2] * back_in_time(nv2, v2, 2, lane)
            short_g = tg[0] * g + tg[1] * back_in_time(ng1, g1, 1, lane) + tg[2] * back_in_time(ng2, g2, 2, lane)
            lhs[pl.ds(rows, 32), t * 128 : t * 128 + 128] = short_v.astype(BF16)
            lhs[pl.ds(rows + 256, 32), t * 128 : t * 128 + 128] = (c * short_g).astype(BF16)
            v1, v2, g1, g2 = nv1, nv2, ng1, ng2
        return v1, v2, g1, g2

    start = rolled(rim_ref[0:32, :].astype(F32)) + rolled(rim_ref[32:64, :].astype(F32))
    lax.fori_loop(0, 8, block, start)

    low = lanes((16, 128)) < 64

    def strip(n, _):
        at = pl.multiple_of(n * 256, 256)
        sums = jnp.dot(lhs[...], cas_ref[:, pl.ds(at, 256)], preferred_element_type=F32)
        for h in range(2):
            tw = tw_ref[:, pl.ds(pl.multiple_of(at + h * 128, 128), 128)]
            d = 4 * n + 2 * h
            for m in range(16):
                part = sums[m * 32 : m * 32 + 32, h * 128 : h * 128 + 128] * tw[m % 8 : m % 8 + 1, :]
                a, b = part[:16], part[16:]
                even = jnp.where(low, a, pltpu.roll(b, 64, 1))
                odd = jnp.where(low, pltpu.roll(a, 64, 1), b)
                out_ref[d, m * 16 : m * 16 + 16, :] = even.astype(BF16)
                out_ref[d + 1, m * 16 : m * 16 + 16, :] = odd.astype(BF16)
        return 0

    lax.fori_loop(0, 4, strip, 0)


def mix_kernel(f_ref, spec_ref, mix_ref, gs_ref, out_ref, wide_v, wide_g):
    wide = (wide_v, wide_g)
    for f in range(2):
        for b in range(16):
            wide[f][b * 128 : b * 128 + 128, :] = f_ref[b, f * 128 : f * 128 + 128, :].astype(F32)
    mixing = mix_ref[...]
    turned = mixing.T
    high = turned.astype(BF16)
    low = (turned - high.astype(F32)).astype(BF16)
    ahead = jnp.concatenate([high, low], axis=1)
    again = jnp.concatenate([jnp.concatenate([high, high], axis=1), jnp.concatenate([low, low], axis=1)], axis=0)

    for c in range(16):
        slabs = [wide[f][pl.ds(c, 128, stride=16), :].T.astype(BF16) for f in range(2)]
        both = jnp.dot(jnp.concatenate(slabs, axis=0), ahead, preferred_element_type=F32)
        both = both[:, :128] + both[:, 128:]
        sv, sg = both[:128], both[128:]
        filters = jnp.concatenate([spec_ref[c], spec_ref[16 + c]], axis=0).astype(F32)
        grad = sv * sg
        gs_ref[c] = grad[:64]
        gs_ref[16 + c] = grad[64:]
        product = jnp.concatenate([sv * filters, sg * filters], axis=0)
        top = product.astype(BF16)
        rest = (product - top.astype(F32)).astype(BF16)
        product = jnp.concatenate([top, rest], axis=1)
        sums = lax.dot_general(again, product, (((1,), (1,)), ((), ())), preferred_element_type=F32)
        sums = sums[:128] + sums[128:]
        for f in range(2):
            wide[f][pl.ds(c, 128, stride=16), :] = sums[:, f * 128 : f * 128 + 128]
    for f in range(2):
        for b in range(16):
            out_ref[b, f * 128 : f * 128 + 128, :] = wide[f][b * 128 : b * 128 + 128, :].astype(BF16)


def back_kernel(y_ref, r_ref, rim_ref, cols_ref, tw_ref, cas_ref, out_ref, head_ref, lhs):
    low = lanes((16, 128)) < 64

    def unpack(y, _):
        at = pl.multiple_of(y * 128, 128)
        tw = tw_ref[:, pl.ds(at, 128)]
        for m in range(16):
            e = y_ref[2 * y, m * 16 : m * 16 + 16, :].astype(F32)
            o = y_ref[2 * y + 1, m * 16 : m * 16 + 16, :].astype(F32)
            row = tw[m % 8 : m % 8 + 1, :]
            a = jnp.where(low, e, pltpu.roll(o, 64, 1)) * row
            b = jnp.where(low, pltpu.roll(e, 64, 1), o) * row
            lhs[m * 32 : m * 32 + 16, pl.ds(at, 128)] = a.astype(BF16)
            lhs[m * 32 + 16 : m * 32 + 32, pl.ds(at, 128)] = b.astype(BF16)
        return 0

    lax.fori_loop(0, 8, unpack, 0)

    def strip(n, _):
        at = pl.multiple_of(n * 256, 256)
        sums = jnp.dot(lhs[...], cas_ref[:, pl.ds(at, 256)], preferred_element_type=F32)
        out_ref[:, pl.ds(at, 256)] = sums.astype(BF16)
        return 0

    lax.fori_loop(0, 4, strip, 0)

    lane = lanes()
    cols = cols_ref[...]
    v, g, c = (r_ref[0, k * 32 : k * 32 + 32, 0:128].astype(F32) for k in range(3))
    before_v, before_g = rim_ref[0:32, :].astype(F32), rim_ref[32:64, :].astype(F32)
    short_v, short_g = v * column(cols, 0), g * column(cols, 3)
    for k in (1, 2):
        short_v += column(cols, k) * back_in_time(pltpu.roll(v, k, 1), pltpu.roll(before_v, k, 1), k, lane)
        short_g += column(cols, 3 + k) * back_in_time(pltpu.roll(g, k, 1), pltpu.roll(before_g, k, 1), k, lane)
    short_v = short_v.astype(BF16).astype(F32)
    grad_long = (c * short_g).astype(BF16).astype(F32)
    skip = column(cols, 6)
    head_ref[0:32, :] = skip * grad_long + out_ref[256:288, 0:128].astype(F32)
    head_ref[32:64, :] = c * (out_ref[0:32, 0:128].astype(F32) + skip * short_v)


def final_kernel(d_ref, r_ref, rim_ref, next_ref, cols_ref, out_ref, sums_ref):
    lane = lanes()
    cols = cols_ref[...]
    tv = [column(cols, k) for k in range(3)]
    tg = [column(cols, 3 + k) for k in range(3)]
    skip = column(cols, 6)

    def ahead(tile):
        return pltpu.roll(tile, 127, 1), pltpu.roll(tile, 126, 1)

    def block(step, carry):
        i = 7 - step
        (v, v1, v2), (g, g1, g2), nv, ng, acc = carry
        rows = pl.multiple_of(i * 32, 32)
        for t in reversed(range(8)):
            piece, at = i * 4 + t // 2, (t % 2) * 128
            if t > 0:
                piece_b, at_b = i * 4 + (t - 1) // 2, ((t - 1) % 2) * 128
                pv = r_ref[piece_b, 0:32, at_b : at_b + 128].astype(F32)
                pg = r_ref[piece_b, 32:64, at_b : at_b + 128].astype(F32)
            else:
                inside = i > 0
                piece_b = jnp.maximum(i * 4 - 1, 0)
                pv = jnp.where(inside, r_ref[piece_b, 0:32, 128:256].astype(F32), rim_ref[0:32, :].astype(F32))
                pg = jnp.where(inside, r_ref[piece_b, 32:64, 128:256].astype(F32), rim_ref[32:64, :].astype(F32))
            pv1, pv2 = rolled(pv)
            pg1, pg2 = rolled(pg)
            vb1, vb2 = back_in_time(v1, pv1, 1, lane), back_in_time(v2, pv2, 2, lane)
            gb1, gb2 = back_in_time(g1, pg1, 1, lane), back_in_time(g2, pg2, 2, lane)
            short_v = (tv[0] * v + tv[1] * vb1 + tv[2] * vb2).astype(BF16).astype(F32)
            short_g = tg[0] * g + tg[1] * gb1 + tg[2] * gb2
            c = r_ref[piece, 64:96, at : at + 128].astype(F32)
            grad_long = (c * short_g).astype(BF16).astype(F32)
            long_v = d_ref[pl.ds(rows, 32), t * 128 : t * 128 + 128].astype(F32)
            back_g = d_ref[pl.ds(rows + 256, 32), t * 128 : t * 128 + 128].astype(F32)
            direct = long_v + skip * short_v
            gsg = c * direct
            gsv = skip * grad_long + back_g
            wv, wg = ahead(gsv), ahead(gsg)
            out_ref[piece, 0:32, at : at + 128] = (short_g * direct).astype(BF16)
            out_ref[piece, 32:64, at : at + 128] = (
                tv[0] * gsv + tv[1] * jnp.where(lane > 126, nv[0], wv[0]) + tv[2] * jnp.where(lane > 125, nv[1], wv[1])
            ).astype(BF16)
            out_ref[piece, 64:96, at : at + 128] = (
                tg[0] * gsg + tg[1] * jnp.where(lane > 126, ng[0], wg[0]) + tg[2] * jnp.where(lane > 125, ng[1], wg[1])
            ).astype(BF16)
            terms = (gsv * v, gsv * vb1, gsv * vb2, gsg * g, gsg * gb1, gsg * gb2, grad_long * short_v)
            acc = tuple(a + b for a, b in zip(acc, terms))
            v, v1, v2, g, g1, g2, nv, ng = pv, pv1, pv2, pg, pg1, pg2, wv, wg
        return (v, v1, v2), (g, g1, g2), nv, ng, acc

    last_v = r_ref[31, 0:32, 128:256].astype(F32)
    last_g = r_ref[31, 32:64, 128:256].astype(F32)
    zero = jnp.zeros((32, 128), F32)
    start = (
        (last_v, *rolled(last_v)),
        (last_g, *rolled(last_g)),
        ahead(next_ref[0:32, :]),
        ahead(next_ref[32:64, :]),
        (zero,) * 7,
    )
    acc = lax.fori_loop(0, 8, block, start)[4]
    total = zero
    for k in range(7):
        total = jnp.where(lane == k, jnp.sum(acc[k], axis=1, keepdims=True), total)
    sums_ref[...] = total


def call(kernel, outs, scratch, flops, moved, *args):
    return pl.pallas_call(
        kernel,
        out_shape=[jax.ShapeDtypeStruct(s, d) for s, d in outs],
        scratch_shapes=[pltpu.VMEM(s, d) for s, d in scratch],
        cost_estimate=pl.CostEstimate(flops=flops, bytes_accessed=moved, transcendentals=0),
    )(*args)


def spread(r, rim, cols, twiddle, cas):
    return call(spread_kernel, [((16, 256, 128), BF16)], [((512, 1024), BF16)], 1 << 30, 5 << 20, r, rim, cols, twiddle, cas)[0]


def mix(by_freq, spectrum, mixing):
    return call(
        mix_kernel,
        [((32, 64, 128), F32), ((16, 256, 128), BF16)],
        [((2048, 128), F32), ((2048, 128), F32)],
        1 << 30,
        5 << 20,
        by_freq,
        spectrum,
        mixing,
    )


def back(returned, r, rim, cols, twiddle, cas):
    return call(
        back_kernel,
        [((512, 1024), BF16), ((64, 128), F32)],
        [((512, 1024), BF16)],
        1 << 30,
        5 << 20,
        returned,
        r,
        rim,
        cols,
        twiddle,
        cas,
    )


def final(d, r, rim, following, cols):
    return call(
        final_kernel, [((32, 96, 256), BF16), ((32, 128), F32)], [], 1 << 24, 5 << 20, d, r, rim, following, cols
    )


def exchange(array, axis):
    return lax.all_to_all(array, axis, 0, 0, tiled=True)


def per_device(values, gates, cotangent, taps_values, taps_gates, skip_gain, twiddle, mixing, spectrum):
    batch = lax.axis_size("batch")
    cas = jnp.asarray(cas_table())
    raw = jnp.concatenate([x.reshape(32, 32, 256) for x in (values, gates, cotangent)], axis=1)
    r = exchange(raw, "seq")
    gains = jnp.concatenate([taps_values, taps_gates, skip_gain[None]], axis=0)
    cols = lax.dynamic_slice(gains, (0, lax.axis_index("seq") * 32), (7, 32))
    cols = jnp.pad(cols.T, ((0, 0), (0, 121)))
    rim = lax.ppermute(r[31, :64, 128:], "batch", [(i, i + 1) for i in range(batch - 1)])
    by_freq = exchange(spread(r, rim, cols, twiddle, cas), "batch")
    grad_spectrum, weighted = mix(by_freq, spectrum.transpose(0, 2, 1), mixing)
    d, head = back(exchange(weighted, "batch"), r, rim, cols, twiddle, cas)
    following = lax.ppermute(head, "batch", [(i + 1, i) for i in range(batch - 1)])
    done, sums = final(d, r, rim, following, cols)
    outs = exchange(done, "seq")
    step = 1
    while step < batch:
        sums = sums + lax.ppermute(sums, "batch", [(i, i ^ step) for i in range(batch)])
        step *= 2
    sums = sums[:, :7].T
    mixed, grad_values, grad_gates = (outs[:, k * 32 : k * 32 + 32].reshape(values.shape) for k in range(3))
    return mixed, grad_values, grad_gates, grad_spectrum.transpose(0, 2, 1), sums[0:3], sums[3:6], sums[6]


def solution(mesh):
    in_specs = (
        P(None, ("batch", "seq")),
        P(None, ("batch", "seq")),
        P(None, ("batch", "seq")),
        P(),
        P(),
        P(),
        P("batch", None),
        P(),
        P("seq", None, "batch"),
    )
    out_specs = (
        P(None, ("batch", "seq")),
        P(None, ("batch", "seq")),
        P(None, ("batch", "seq")),
        P("seq", None, "batch"),
        P(None, "seq"),
        P(None, "seq"),
        P("seq"),
    )
    return jax.shard_map(per_device, mesh=mesh, in_specs=in_specs, out_specs=out_specs, check_vma=False)
```

profile of v0, /device:TPU:1, one launch (start us, length us, event | category | flops | bytes accessed | tf_op | source)
XLA Modules:
  0.0 208.9 jit_solution(18267604098615833203)
XLA Ops:
  0.6 2.7 %pad_maximum_fusion = bf16[32,96,256]{2,1,0:T(8,128)(2,1)} fusion(bf16[32,32,256]{2,1,0:T(8,128)(2,1)} %bitcast.14, bf16[32,32,256]{2,1,0:T(8,128)(2,1)} %bitcast.15, bf16[32,32,256]{2,1,0:T(8,128)(2,1)} %bitcast.16), kind=kLoop, calls=%fused_computation | loop fusion | flops 4718592 | bytes 3145728 | tf_op jit(solution)/shard_map/concatenate | solution.py:284
  3.3 13.8 %all-to-all-start = ((bf16[32,96,256]{2,1,0:T(8,128)(2,1)}), bf16[32,96,256]{2,1,0:T(8,128)(2,1)S(1)}, u32[]{:S(2)}, u32[]{:S(2)}) async-start(bf16[32,96,256]{2,1,0:T(8,128)(2,1)} %pad_maximum_fusion), calls=%async_computation | async-start | bytes 3145728 | tf_op jit(solution)/shard_map/all_to_all | solution.py:278
  17.1 36.9 %all-to-all-done.r_ref = bf16[32,96,256]{2,1,0:T(8,128)(2,1)S(1)} async-done(((bf16[32,96,256]{2,1,0:T(8,128)(2,1)}), bf16[32,96,256]{2,1,0:T(8,128)(2,1)S(1)}, u32[]{:S(2)}, u32[]{:S(2)}) %all-to-all-start) | async-done | bytes 1572896 | tf_op jit(solution)/shard_map/all_to_all | solution.py:278
  54.1 6.5 %collective-permute-start = (bf16[64,128]{1,0:T(8,128)(2,1)S(1)}, bf16[64,128]{1,0:T(8,128)(2,1)S(1)}, u32[]{:S(2)}, u32[]{:S(2)}) collective-permute-start(bf16[64,128]{1,0:T(8,128)(2,1)S(1)} %slice_bitcast_fusion), channel_id=1, source_target_pairs={{0,32},{32,64},{64,96},{96,128},{128,160},{160,192},{192,224},{224... | collective-permute-start | bytes 49160 | tf_op jit(solution)/shard_map/ppermute | solution.py:289
  62.0 6.7 %shard_map.153 = bf16[16,256,128]{2,1,0:T(8,128)(2,1)} custom-call(bf16[32,96,256]{2,1,0:T(8,128)(2,1)} %copy-done, bf16[64,128]{1,0:T(8,128)(2,1)} %copy-done.1, f32[32,128]{1,0:T(8,128)} %pad.4.cols_ref, f32[8,1024]{1,0:T(8,128)} %tw_ref.3, bf16[1024,1024]{1,0:T(8,128)(2,1)} %constant.14.clone.cas_ref), custom_call_target="tpu_custom_call" | custom-call | flops 1073741824 | bytes 5242880 | tf_op jit(solution)/shard_map/pallas_call | solution.py:230
  68.7 38.0 %all_to_all.20.f_ref = bf16[16,256,128]{2,1,0:T(8,128)(2,1)} all-to-all(bf16[16,256,128]{2,1,0:T(8,128)(2,1)} %shard_map.153), channel_id=1, replica_groups=mesh['batch'=16,'seq'=32] {'batch'}, dimensions={0} | all-to-all | bytes 2097152 | tf_op jit(solution)/shard_map/all_to_all | solution.py:278
  106.7 4.7 %shard_map.154 = (f32[32,64,128]{2,1,0:T(8,128)}, bf16[16,256,128]{2,1,0:T(8,128)(2,1)}) custom-call(bf16[16,256,128]{2,1,0:T(8,128)(2,1)} %all_to_all.20.f_ref, bf16[32,64,128]{2,1,0:T(8,128)(2,1)} %bitcast.22, f32[128,128]{1,0:T(8,128)} %mix_ref.1), custom_call_target="tpu_custom_call" | custom-call | flops 1073741824 | bytes 5242880 | tf_op jit(solution)/shard_map/pallas_call | solution.py:230
  111.4 31.6 %all_to_all.21.y_ref = bf16[16,256,128]{2,1,0:T(8,128)(2,1)} all-to-all(bf16[16,256,128]{2,1,0:T(8,128)(2,1)} %get-tuple-element.13), channel_id=1, replica_groups=mesh['batch'=16,'seq'=32] {'batch'}, dimensions={0} | all-to-all | bytes 2097152 | tf_op jit(solution)/shard_map/all_to_all | solution.py:278
  143.0 6.2 %shard_map.155 = (bf16[512,1024]{1,0:T(8,128)(2,1)}, f32[64,128]{1,0:T(8,128)}) custom-call(bf16[16,256,128]{2,1,0:T(8,128)(2,1)} %all_to_all.21.y_ref, bf16[32,96,256]{2,1,0:T(8,128)(2,1)} %copy-done, bf16[64,128]{1,0:T(8,128)(2,1)} %copy-done.1, f32[32,128]{1,0:T(8,128)} %pad.4.cols_ref, f32[8,1024]{1,0:T(8,128)} %tw_ref.3, ...), custom_call_target="tpu_custom_call" | custom-call | flops 1073741824 | bytes 5242880 | tf_op jit(solution)/shard_map/pallas_call | solution.py:230
  149.2 1.9 collective-permute-start.1
  151.1 3.5 %collective-permute-done.1.next_ref = f32[64,128]{1,0:T(8,128)S(1)} collective-permute-done((f32[64,128]{1,0:T(8,128)}, f32[64,128]{1,0:T(8,128)S(1)}, u32[]{:S(2)}, u32[]{:S(2)}) %collective-permute-start.1) | collective-permute-done | bytes 32800 | tf_op jit(solution)/shard_map/ppermute | solution.py:293
  155.2 8.9 %shard_map.156 = (bf16[32,96,256]{2,1,0:T(8,128)(2,1)}, f32[32,128]{1,0:T(8,128)}) custom-call(bf16[512,1024]{1,0:T(8,128)(2,1)} %get-tuple-element.14.d_ref, bf16[32,96,256]{2,1,0:T(8,128)(2,1)} %copy-done, bf16[64,128]{1,0:T(8,128)(2,1)} %copy-done.1, f32[64,128]{1,0:T(8,128)} %copy-done.2, f32[32,128]{1,0:T(8,128)} %pad.4.cols_ref), custom_call_target="tpu_custom_call" | custom-call | flops 16777216 | bytes 5242880 | tf_op jit(solution)/shard_map/pallas_call | solution.py:230
  164.1 5.4 %all-to-all-start.3 = ((bf16[32,96,256]{2,1,0:T(8,128)(2,1)}), bf16[32,96,256]{2,1,0:T(8,128)(2,1)S(1)}, u32[]{:S(2)}, u32[]{:S(2)}) async-start(bf16[32,96,256]{2,1,0:T(8,128)(2,1)} %get-tuple-element.16), calls=%async_computation.3 | async-start | bytes 3145728 | tf_op jit(solution)/shard_map/all_to_all | solution.py:278
  169.6 1.9 collective-permute-start.2
  171.5 1.1 collective-permute-done.2
  172.6 2.1 collective-permute-start.3
  174.7 2.7 %collective-permute-done.3 = f32[32,128]{1,0:T(8,128)S(1)} collective-permute-done((f32[32,128]{1,0:T(8,128)S(1)}, f32[32,128]{1,0:T(8,128)S(1)}, u32[]{:S(2)}, u32[]{:S(2)}) %collective-permute-start.3) | collective-permute-done | bytes 16416 | tf_op jit(solution)/shard_map/ppermute | solution.py:298
  177.4 2.8 %collective-permute-start.4 = (f32[32,128]{1,0:T(8,128)S(1)}, f32[32,128]{1,0:T(8,128)S(1)}, u32[]{:S(2)}, u32[]{:S(2)}) collective-permute-start(f32[32,128]{1,0:T(8,128)S(1)} %add.19), channel_id=1, source_target_pairs={{0,128},{32,160},{64,192},{96,224},{128,0},{160,32},{192,64},{224,... | collective-permute-start | bytes 49160 | tf_op jit(solution)/shard_map/ppermute | solution.py:298
  180.2 2.9 %collective-permute-done.4 = f32[32,128]{1,0:T(8,128)S(1)} collective-permute-done((f32[32,128]{1,0:T(8,128)S(1)}, f32[32,128]{1,0:T(8,128)S(1)}, u32[]{:S(2)}, u32[]{:S(2)}) %collective-permute-start.4) | collective-permute-done | bytes 16416 | tf_op jit(solution)/shard_map/ppermute | solution.py:298
  183.1 3.8 %collective-permute-start.5 = (f32[32,128]{1,0:T(8,128)S(1)}, f32[32,128]{1,0:T(8,128)S(1)}, u32[]{:S(2)}, u32[]{:S(2)}) collective-permute-start(f32[32,128]{1,0:T(8,128)S(1)} %add.20), channel_id=1, source_target_pairs={{0,256},{32,288},{64,320},{96,352},{128,384},{160,416},{192,448},{... | collective-permute-start | bytes 49160 | tf_op jit(solution)/shard_map/ppermute | solution.py:298
  186.9 5.0 %collective-permute-done.5 = f32[32,128]{1,0:T(8,128)S(1)} collective-permute-done((f32[32,128]{1,0:T(8,128)S(1)}, f32[32,128]{1,0:T(8,128)S(1)}, u32[]{:S(2)}, u32[]{:S(2)}) %collective-permute-start.5) | collective-permute-done | bytes 16416 | tf_op jit(solution)/shard_map/ppermute | solution.py:298
  193.3 0.7 slice_reduce_fusion
  194.0 13.7 %all-to-all-done.3 = bf16[32,96,256]{2,1,0:T(8,128)(2,1)S(1)} async-done(((bf16[32,96,256]{2,1,0:T(8,128)(2,1)}), bf16[32,96,256]{2,1,0:T(8,128)(2,1)S(1)}, u32[]{:S(2)}, u32[]{:S(2)}) %all-to-all-start.3) | async-done | bytes 1572896 | tf_op jit(solution)/shard_map/all_to_all | solution.py:278
  207.8 1.2 fusion.3
  (26 shorter events, 3.5 us)
Async XLA Ops:
  3.3 57.2 %copy-start.4 = (f32[3,1024]{1,0:T(4,128)S(1)}, f32[3,1024]{1,0:T(4,128)}, u32[]{:S(2)}) copy-start(f32[3,1024]{1,0:T(4,128)} %param.13) | copy-start | bytes 36868
  3.3 57.2 %copy-start.5 = (f32[3,1024]{1,0:T(4,128)S(1)}, f32[3,1024]{1,0:T(4,128)}, u32[]{:S(2)}) copy-start(f32[3,1024]{1,0:T(4,128)} %param.14) | copy-start | bytes 36868
  3.3 57.2 %copy-start.6 = (f32[1024]{0:T(1024)S(1)}, f32[1024]{0:T(1024)}, u32[]{:S(2)}) copy-start(f32[1024]{0:T(1024)} %param.15) | copy-start | bytes 12292
  3.3 50.8 %all-to-all-start = ((bf16[32,96,256]{2,1,0:T(8,128)(2,1)}), bf16[32,96,256]{2,1,0:T(8,128)(2,1)S(1)}, u32[]{:S(2)}, u32[]{:S(2)}) async-start(bf16[32,96,256]{2,1,0:T(8,128)(2,1)} %pad_maximum_fusion), calls=%async_computation | async-start | bytes 3145728 | tf_op jit(solution)/shard_map/all_to_all | solution.py:278
  54.0 7.3 %copy-start = (bf16[32,96,256]{2,1,0:T(8,128)(2,1)}, bf16[32,96,256]{2,1,0:T(8,128)(2,1)S(1)}, u32[]{:S(2)}) copy-start(bf16[32,96,256]{2,1,0:T(8,128)(2,1)S(1)} %all-to-all-done.r_ref) | copy-start | bytes 4718596
  54.1 7.3 %collective-permute-start = (bf16[64,128]{1,0:T(8,128)(2,1)S(1)}, bf16[64,128]{1,0:T(8,128)(2,1)S(1)}, u32[]{:S(2)}, u32[]{:S(2)}) collective-permute-start(bf16[64,128]{1,0:T(8,128)(2,1)S(1)} %slice_bitcast_fusion), channel_id=1, source_target_pairs={{0,32},{32,64},{64,96},{96,128},{128,160},{160,192},{192,224},{224... | collective-permute-start | bytes 49160 | tf_op jit(solution)/shard_map/ppermute | solution.py:289
  61.4 0.6 copy-start.1
  149.2 5.4 %collective-permute-start.1 = (f32[64,128]{1,0:T(8,128)}, f32[64,128]{1,0:T(8,128)S(1)}, u32[]{:S(2)}, u32[]{:S(2)}) collective-permute-start(f32[64,128]{1,0:T(8,128)} %get-tuple-element.15), channel_id=1, source_target_pairs={{32,0},{64,32},{96,64},{128,96},{160,128},{192,160},{224,192},{256... | collective-permute-start | bytes 98312 | tf_op jit(solution)/shard_map/ppermute | solution.py:293
  154.6 0.6 copy-start.2
  164.1 5.5 %copy-start.3 = (f32[32,128]{1,0:T(8,128)S(1)}, f32[32,128]{1,0:T(8,128)}, u32[]{:S(2)}) copy-start(f32[32,128]{1,0:T(8,128)} %get-tuple-element.18) | copy-start | bytes 49156
  164.1 43.7 %all-to-all-start.3 = ((bf16[32,96,256]{2,1,0:T(8,128)(2,1)}), bf16[32,96,256]{2,1,0:T(8,128)(2,1)S(1)}, u32[]{:S(2)}, u32[]{:S(2)}) async-start(bf16[32,96,256]{2,1,0:T(8,128)(2,1)} %get-tuple-element.16), calls=%async_computation.3 | async-start | bytes 3145728 | tf_op jit(solution)/shard_map/all_to_all | solution.py:278
  169.6 3.1 %collective-permute-start.2 = (f32[32,128]{1,0:T(8,128)S(1)}, f32[32,128]{1,0:T(8,128)S(1)}, u32[]{:S(2)}, u32[]{:S(2)}) collective-permute-start(f32[32,128]{1,0:T(8,128)S(1)} %copy-done.3), channel_id=1, source_target_pairs={{0,32},{32,0},{64,96},{96,64},{128,160},{160,128},{192,224},{224,1... | collective-permute-start | bytes 49160 | tf_op jit(solution)/shard_map/ppermute | solution.py:298
  172.6 4.8 %collective-permute-start.3 = (f32[32,128]{1,0:T(8,128)S(1)}, f32[32,128]{1,0:T(8,128)S(1)}, u32[]{:S(2)}, u32[]{:S(2)}) collective-permute-start(f32[32,128]{1,0:T(8,128)S(1)} %add.18), channel_id=1, source_target_pairs={{0,64},{32,96},{64,0},{96,32},{128,192},{160,224},{192,128},{224,1... | collective-permute-start | bytes 49160 | tf_op jit(solution)/shard_map/ppermute | solution.py:298
  177.4 5.7 %collective-permute-start.4 = (f32[32,128]{1,0:T(8,128)S(1)}, f32[32,128]{1,0:T(8,128)S(1)}, u32[]{:S(2)}, u32[]{:S(2)}) collective-permute-start(f32[32,128]{1,0:T(8,128)S(1)} %add.19), channel_id=1, source_target_pairs={{0,128},{32,160},{64,192},{96,224},{128,0},{160,32},{192,64},{224,... | collective-permute-start | bytes 49160 | tf_op jit(solution)/shard_map/ppermute | solution.py:298
  183.1 8.8 %collective-permute-start.5 = (f32[32,128]{1,0:T(8,128)S(1)}, f32[32,128]{1,0:T(8,128)S(1)}, u32[]{:S(2)}, u32[]{:S(2)}) collective-permute-start(f32[32,128]{1,0:T(8,128)S(1)} %add.20), channel_id=1, source_target_pairs={{0,256},{32,288},{64,320},{96,352},{128,384},{160,416},{192,448},{... | collective-permute-start | bytes 49160 | tf_op jit(solution)/shard_map/ppermute | solution.py:298
where the time goes:
time: 210 us; the launch traced here: 209 us
  blocking collectives  69.6 us (33%)
  waiting for transfers between devices  66 us (31%)
  starting transfers between devices  38.2 us (18%)
  Pallas kernels  26.5 us (13%)
  local copies, waits for them, and re-layouts  5.19 us (2%)
  other arithmetic  2.76 us (1%)
    all_to_all x2, blocking collectives, exchange(): return lax.all_to_all(array, axis, 0, 0, tiled=True)  69.6 us
    all_to_all x2, waiting for transfers between devices, exchange(): return lax.all_to_all(array, axis, 0, 0, tiled=True)  50.6 us
    pallas_call x4, Pallas kernels, call(): pl.pallas_call(kernel, out_shape=[jax.ShapeDtypeStruct(s, d) for s, d in...  26.5 us
    all_to_all x2, starting transfers between devices, exchange(): return lax.all_to_all(array, axis, 0, 0, tiled=True)  19.3 us
    ppermute x4, waiting for transfers between devices, per_device(): lax.ppermute(sums, 'batch', [(i, i ^ step) for i in range(batch)])  11.8 us
    ppermute x4, starting transfers between devices, per_device(): lax.ppermute(sums, 'batch', [(i, i ^ step) for i in range(batch)])  10.5 us
    ppermute x1, starting transfers between devices, per_device(): lax.ppermute(r[31, :64, 128:], 'batch', [(i, i + 1) for i in range(batch...  6.46 us
  transfers between devices with their start and end apart: 8, of which 7 were waited for; matrix products, arithmetic and copies ran while one was open for 1% of the time, Pallas kernels for 0%

commit v1 on v0

--- a/solution.py
+++ b/solution.py
@@ -11,6 +11,7 @@
 
 BLOCK = 1024
 F32, BF16 = jnp.float32, jnp.bfloat16
+GRANT = 20 << 20
 
 
 def cas_table():
@@ -34,34 +35,47 @@
 
 
 def column(cols, at):
-    return jnp.broadcast_to(cols[:, at : at + 1], (32, 128))
+    return jnp.broadcast_to(cols[:, at : at + 1], (cols.shape[0], 128))
+
+
+def gather_kernel(a_ref, b_ref, c_ref, out_ref, sems):
+    copies = [
+        pltpu.make_async_copy(ref, out_ref.at[:, k * 32 : k * 32 + 32, :], sems.at[k])
+        for k, ref in enumerate((a_ref, b_ref, c_ref))
+    ]
+    for copy in copies:
+        copy.start()
+    for copy in copies:
+        copy.wait()
 
 
 def spread_kernel(r_ref, rim_ref, cols_ref, tw_ref, cas_ref, out_ref, lhs):
-    lane = lanes()
-    cols = cols_ref[...]
-    tv = [column(cols, k) for k in range(3)]
-    tg = [column(cols, 3 + k) for k in range(3)]
-
-    def block(i, carry):
-        v1, v2, g1, g2 = carry
-        rows = pl.multiple_of(i * 32, 32)
-        for t in range(8):
-            piece, at = i * 4 + t // 2, (t % 2) * 128
-            v = r_ref[piece, 0:32, at : at + 128].astype(F32)
-            g = r_ref[piece, 32:64, at : at + 128].astype(F32)
-            c = r_ref[piece, 64:96, at : at + 128].astype(F32)
-            nv1, nv2 = rolled(v)
-            ng1, ng2 = rolled(g)
-            short_v = tv[0] * v + tv[1] * back_in_time(nv1, v1, 1, lane) + tv[2] * back_in_time(nv2, v2, 2, lane)
-            short_g = tg[0] * g + tg[1] * back_in_time(ng1, g1, 1, lane) + tg[2] * back_in_time(ng2, g2, 2, lane)
-            lhs[pl.ds(rows, 32), t * 128 : t * 128 + 128] = short_v.astype(BF16)
-            lhs[pl.ds(rows + 256, 32), t * 128 : t * 128 + 128] = (c * short_g).astype(BF16)
-            v1, v2, g1, g2 = nv1, nv2, ng1, ng2
-        return v1, v2, g1, g2
-
-    start = rolled(rim_ref[0:32, :].astype(F32)) + rolled(rim_ref[32:64, :].astype(F32))
-    lax.fori_loop(0, 8, block, start)
+    lane = lanes((16, 128))
+    for h in range(2):
+        own = slice(h * 16, h * 16 + 16)
+        cols = cols_ref[own, :]
+        tv = [column(cols, k) for k in range(3)]
+        tg = [column(cols, 3 + k) for k in range(3)]
+
+        def block(i, carry):
+            v1, v2, g1, g2 = carry
+            rows = pl.multiple_of(i * 32, 32) + h * 16
+            for t in range(8):
+                piece, at = i * 4 + t // 2, slice((t % 2) * 128, (t % 2) * 128 + 128)
+                v = r_ref[piece, own, at].astype(F32)
+                g = r_ref[piece, h * 16 + 32 : h * 16 + 48, at].astype(F32)
+                c = r_ref[piece, h * 16 + 64 : h * 16 + 80, at].astype(F32)
+                nv1, nv2 = rolled(v)
+                ng1, ng2 = rolled(g)
+                short_v = tv[0] * v + tv[1] * back_in_time(nv1, v1, 1, lane) + tv[2] * back_in_time(nv2, v2, 2, lane)
+                short_g = tg[0] * g + tg[1] * back_in_time(ng1, g1, 1, lane) + tg[2] * back_in_time(ng2, g2, 2, lane)
+                lhs[pl.ds(rows, 16), t * 128 : t * 128 + 128] = short_v.astype(BF16)
+                lhs[pl.ds(rows + 256, 16), t * 128 : t * 128 + 128] = (c * short_g).astype(BF16)
+                v1, v2, g1, g2 = nv1, nv2, ng1, ng2
+            return v1, v2, g1, g2
+
+        start = rolled(rim_ref[own, :].astype(F32)) + rolled(rim_ref[h * 16 + 32 : h * 16 + 48, :].astype(F32))
+        lax.fori_loop(0, 8, block, start)
 
     low = lanes((16, 128)) < 64
 
@@ -159,76 +173,83 @@
 
 
 def final_kernel(d_ref, r_ref, rim_ref, next_ref, cols_ref, out_ref, sums_ref):
-    lane = lanes()
-    cols = cols_ref[...]
-    tv = [column(cols, k) for k in range(3)]
-    tg = [column(cols, 3 + k) for k in range(3)]
-    skip = column(cols, 6)
+    lane = lanes((16, 128))
 
     def ahead(tile):
         return pltpu.roll(tile, 127, 1), pltpu.roll(tile, 126, 1)
 
-    def block(step, carry):
-        i = 7 - step
-        (v, v1, v2), (g, g1, g2), nv, ng, acc = carry
-        rows = pl.multiple_of(i * 32, 32)
-        for t in reversed(range(8)):
-            piece, at = i * 4 + t // 2, (t % 2) * 128
-            if t > 0:
-                piece_b, at_b = i * 4 + (t - 1) // 2, ((t - 1) % 2) * 128
-                pv = r_ref[piece_b, 0:32, at_b : at_b + 128].astype(F32)
-                pg = r_ref[piece_b, 32:64, at_b : at_b + 128].astype(F32)
-            else:
-                inside = i > 0
-                piece_b = jnp.maximum(i * 4 - 1, 0)
-                pv = jnp.where(inside, r_ref[piece_b, 0:32, 128:256].astype(F32), rim_ref[0:32, :].astype(F32))
-                pg = jnp.where(inside, r_ref[piece_b, 32:64, 128:256].astype(F32), rim_ref[32:64, :].astype(F32))
-            pv1, pv2 = rolled(pv)
-            pg1, pg2 = rolled(pg)
-            vb1, vb2 = back_in_time(v1, pv1, 1, lane), back_in_time(v2, pv2, 2, lane)
-            gb1, gb2 = back_in_time(g1, pg1, 1, lane), back_in_time(g2, pg2, 2, lane)
-            short_v = (tv[0] * v + tv[1] * vb1 + tv[2] * vb2).astype(BF16).astype(F32)
-            short_g = tg[0] * g + tg[1] * gb1 + tg[2] * gb2
-            c = r_ref[piece, 64:96, at : at + 128].astype(F32)
-            grad_long = (c * short_g).astype(BF16).astype(F32)
-            long_v = d_ref[pl.ds(rows, 32), t * 128 : t * 128 + 128].astype(F32)
-            back_g = d_ref[pl.ds(rows + 256, 32), t * 128 : t * 128 + 128].astype(F32)
-            direct = long_v + skip * short_v
-            gsg = c * direct
-            gsv = skip * grad_long + back_g
-            wv, wg = ahead(gsv), ahead(gsg)
-            out_ref[piece, 0:32, at : at + 128] = (short_g * direct).astype(BF16)
-            out_ref[piece, 32:64, at : at + 128] = (
-                tv[0] * gsv + tv[1] * jnp.where(lane > 126, nv[0], wv[0]) + tv[2] * jnp.where(lane > 125, nv[1], wv[1])
-            ).astype(BF16)
-            out_ref[piece, 64:96, at : at + 128] = (
-                tg[0] * gsg + tg[1] * jnp.where(lane > 126, ng[0], wg[0]) + tg[2] * jnp.where(lane > 125, ng[1], wg[1])
-            ).astype(BF16)
-            terms = (gsv * v, gsv * vb1, gsv * vb2, gsg * g, gsg * gb1, gsg * gb2, grad_long * short_v)
-            acc = tuple(a + b for a, b in zip(acc, terms))
-            v, v1, v2, g, g1, g2, nv, ng = pv, pv1, pv2, pg, pg1, pg2, wv, wg
-        return (v, v1, v2), (g, g1, g2), nv, ng, acc
-
-    last_v = r_ref[31, 0:32, 128:256].astype(F32)
-    last_g = r_ref[31, 32:64, 128:256].astype(F32)
-    zero = jnp.zeros((32, 128), F32)
-    start = (
-        (last_v, *rolled(last_v)),
-        (last_g, *rolled(last_g)),
-        ahead(next_ref[0:32, :]),
-        ahead(next_ref[32:64, :]),
-        (zero,) * 7,
-    )
-    acc = lax.fori_loop(0, 8, block, start)[4]
-    total = zero
-    for k in range(7):
-        total = jnp.where(lane == k, jnp.sum(acc[k], axis=1, keepdims=True), total)
-    sums_ref[...] = total
+    for h in range(2):
+        one, two, three = (slice(h * 16 + k * 32, h * 16 + k * 32 + 16) for k in range(3))
+        cols = cols_ref[one, :]
+        tv = [column(cols, k) for k in range(3)]
+        tg = [column(cols, 3 + k) for k in range(3)]
+        skip = column(cols, 6)
+
+        def block(step, carry):
+            i = 7 - step
+            (v, v1, v2), (g, g1, g2), nv, ng, acc = carry
+            rows = pl.multiple_of(i * 32, 32) + h * 16
+            for t in reversed(range(8)):
+                piece, at = i * 4 + t // 2, slice((t % 2) * 128, (t % 2) * 128 + 128)
+                if t > 0:
+                    piece_b, at_b = i * 4 + (t - 1) // 2, slice(((t - 1) % 2) * 128, ((t - 1) % 2) * 128 + 128)
+                    pv = r_ref[piece_b, one, at_b].astype(F32)
+                    pg = r_ref[piece_b, two, at_b].astype(F32)
+                else:
+                    inside = i > 0
+                    piece_b = jnp.maximum(i * 4 - 1, 0)
+                    pv = jnp.where(inside, r_ref[piece_b, one, 128:256].astype(F32), rim_ref[one, :].astype(F32))
+                    pg = jnp.where(inside, r_ref[piece_b, two, 128:256].astype(F32), rim_ref[two, :].astype(F32))
+                pv1, pv2 = rolled(pv)
+                pg1, pg2 = rolled(pg)
+                vb1, vb2 = back_in_time(v1, pv1, 1, lane), back_in_time(v2, pv2, 2, lane)
+                gb1, gb2 = back_in_time(g1, pg1, 1, lane), back_in_time(g2, pg2, 2, lane)
+                short_v = (tv[0] * v + tv[1] * vb1 + tv[2] * vb2).astype(BF16).astype(F32)
+                short_g = tg[0] * g + tg[1] * gb1 + tg[2] * gb2
+                c = r_ref[piece, three, at].astype(F32)
+                grad_long = (c * short_g).astype(BF16).astype(F32)
+                long_v = d_ref[pl.ds(rows, 16), t * 128 : t * 128 + 128].astype(F32)
+                back_g = d_ref[pl.ds(rows + 256, 16), t * 128 : t * 128 + 128].astype(F32)
+                direct = long_v + skip * short_v
+                gsg = c * direct
+                gsv = skip * grad_long + back_g
+                wv, wg = ahead(gsv), ahead(gsg)
+                out_ref[piece, one, at] = (short_g * direct).astype(BF16)
+                out_ref[piece, two, at] = (
+                    tv[0] * gsv + tv[1] * jnp.where(lane > 126, nv[0], wv[0]) + tv[2] * jnp.where(lane > 125, nv[1], wv[1])
+                ).astype(BF16)
+                out_ref[piece, three, at] = (
+                    tg[0] * gsg + tg[1] * jnp.where(lane > 126, ng[0], wg[0]) + tg[2] * jnp.where(lane > 125, ng[1], wg[1])
+                ).astype(BF16)
+                terms = (gsv * v, gsv * vb1, gsv * vb2, gsg * g, gsg * gb1, gsg * gb2, grad_long * short_v)
+                acc = tuple(a + b for a, b in zip(acc, terms))
+                v, v1, v2, g, g1, g2, nv, ng = pv, pv1, pv2, pg, pg1, pg2, wv, wg
+            return (v, v1, v2), (g, g1, g2), nv, ng, acc
+
+        last_v = r_ref[31, one, 128:256].astype(F32)
+        last_g = r_ref[31, two, 128:256].astype(F32)
+        zero = jnp.zeros((16, 128), F32)
+        start = (
+            (last_v, *rolled(last_v)),
+            (last_g, *rolled(last_g)),
+            ahead(next_ref[one, :]),
+            ahead(next_ref[two, :]),
+            (zero,) * 7,
+        )
+        acc = lax.fori_loop(0, 8, block, start)[4]
+        total = zero
+        for k in range(7):
+            total = jnp.where(lane == k, jnp.sum(acc[k], axis=1, keepdims=True), total)
+        sums_ref[one, :] = total
 
 
 def call(kernel, outs, scratch, flops, moved, *args):
+    vmem = pl.BlockSpec(memory_space=pltpu.VMEM)
     return pl.pallas_call(
         kernel,
+        in_specs=[vmem] * len(args),
+        out_specs=[vmem] * len(outs),
+        compiler_params=pltpu.CompilerParams(vmem_limit_bytes=GRANT),
         out_shape=[jax.ShapeDtypeStruct(s, d) for s, d in outs],
         scratch_shapes=[pltpu.VMEM(s, d) for s, d in scratch],
         cost_estimate=pl.CostEstimate(flops=flops, bytes_accessed=moved, transcendentals=0),
@@ -274,6 +295,17 @@
     )
 
 
+def gather(*fields):
+    return pl.pallas_call(
+        gather_kernel,
+        in_specs=[pl.BlockSpec(memory_space=pltpu.HBM)] * 3,
+        out_specs=pl.BlockSpec(memory_space=pltpu.VMEM),
+        out_shape=jax.ShapeDtypeStruct((32, 96, 256), BF16),
+        scratch_shapes=[pltpu.SemaphoreType.DMA((3,))],
+        compiler_params=pltpu.CompilerParams(vmem_limit_bytes=GRANT),
+    )(*fields)
+
+
 def exchange(array, axis):
     return lax.all_to_all(array, axis, 0, 0, tiled=True)
 
@@ -281,7 +313,7 @@
 def per_device(values, gates, cotangent, taps_values, taps_gates, skip_gain, twiddle, mixing, spectrum):
     batch = lax.axis_size("batch")
     cas = jnp.asarray(cas_table())
-    raw = jnp.concatenate([x.reshape(32, 32, 256) for x in (values, gates, cotangent)], axis=1)
+    raw = gather(*(x.reshape(32, 32, 256) for x in (values, gates, cotangent)))
     r = exchange(raw, "seq")
     gains = jnp.concatenate([taps_values, taps_gates, skip_gain[None]], axis=0)
     cols = lax.dynamic_slice(gains, (0, lax.axis_index("seq") * 32), (7, 32))

time: 210 us -> 200 us (0.952)
  Pallas kernels: 26.5 us -> 17 us
  local copies, waits for them, and re-layouts: 5.19 us -> 8.1 us
  other arithmetic: 2.76 us -> 0.1 us
    pallas_call x4 -> x5, Pallas kernels: 26.5 us -> 17 us  [the longest x4 15.7 us: call(): pl.pallas_call(kernel, in_specs=[vmem] * len(args), out_specs=[vmem] * le...]
    unnamed x17 -> x25, local copies, waits for them, and re-layouts: 2.63 us -> 6.15 us
    concatenate x1 -> x0, other arithmetic: 2.66 us -> none  [per_device(): jnp.concatenate([x.reshape(32, 32, 256) for x in (values, gates, cotangen...]
  transfers between devices with their start and end apart: 8 -> 8, of which waited for: 7 -> 8; matrix products, arithmetic and copies ran while one was open for 1% -> 1% of each run, Pallas kernels for 0% -> 0%
where the time goes in v1:
time: 200 us
  blocking collectives  69.1 us (35%)
  waiting for transfers between devices  66.4 us (33%)
  starting transfers between devices  38.1 us (19%)
  Pallas kernels  17 us (8%)
  local copies, waits for them, and re-layouts  8.1 us (4%)
    all_to_all x2, blocking collectives, exchange(): return lax.all_to_all(array, axis, 0, 0, tiled=True)  69.1 us
    all_to_all x2, waiting for transfers between devices, exchange(): return lax.all_to_all(array, axis, 0, 0, tiled=True)  50.8 us
    all_to_all x2, starting transfers between devices, exchange(): return lax.all_to_all(array, axis, 0, 0, tiled=True)  19.2 us
    pallas_call x4, Pallas kernels, call(): pl.pallas_call(kernel, in_specs=[vmem] * len(args), out_specs=[vmem] * le...  15.7 us
    ppermute x4, waiting for transfers between devices, per_device(): lax.ppermute(sums, 'batch', [(i, i ^ step) for i in range(batch)])  11.6 us
    ppermute x4, starting transfers between devices, per_device(): lax.ppermute(sums, 'batch', [(i, i ^ step) for i in range(batch)])  10.5 us
    ppermute x1, starting transfers between devices, per_device(): lax.ppermute(r[31, :64, 128:], 'batch', [(i, i + 1) for i in range(batch...  6.46 us
    unnamed x25, local copies, waits for them, and re-layouts  6.15 us
  transfers between devices with their start and end apart: 8, of which 8 were waited for; matrix products, arithmetic and copies ran while one was open for 1% of the time, Pallas kernels for 0%

profile of v1, /device:TPU:1, one launch (start us, length us, event | category | flops | bytes accessed | tf_op | source)
XLA Modules:
  0.0 199.7 jit_solution(893672852192758219)
XLA Ops:
  3.8 1.3 shard_map.153
  5.1 13.8 %all-to-all-start = ((bf16[32,96,256]{2,1,0:T(8,128)(2,1)}), bf16[32,96,256]{2,1,0:T(8,128)(2,1)S(1)}, u32[]{:S(2)}, u32[]{:S(2)}) async-start(bf16[32,96,256]{2,1,0:T(8,128)(2,1)} %shard_map.153), calls=%async_computation | async-start | bytes 3145728 | tf_op jit(solution)/shard_map/all_to_all | solution.py:310
  19.0 36.9 %all-to-all-done.r_ref = bf16[32,96,256]{2,1,0:T(8,128)(2,1)S(1)} async-done(((bf16[32,96,256]{2,1,0:T(8,128)(2,1)}), bf16[32,96,256]{2,1,0:T(8,128)(2,1)S(1)}, u32[]{:S(2)}, u32[]{:S(2)}) %all-to-all-start) | async-done | bytes 1572896 | tf_op jit(solution)/shard_map/all_to_all | solution.py:310
  55.9 6.5 %collective-permute-start = (bf16[64,128]{1,0:T(8,128)(2,1)S(1)}, bf16[64,128]{1,0:T(8,128)(2,1)S(1)}, u32[]{:S(2)}, u32[]{:S(2)}) collective-permute-start(bf16[64,128]{1,0:T(8,128)(2,1)S(1)} %slice_bitcast_fusion), channel_id=1, source_target_pairs={{0,32},{32,64},{64,96},{96,128},{128,160},{160,192},{192,224},{224... | collective-permute-start | bytes 49160 | tf_op jit(solution)/shard_map/ppermute | solution.py:321
  63.2 1.6 copy-done
  64.8 4.2 %shard_map.154 = bf16[16,256,128]{2,1,0:T(8,128)(2,1)S(1)} custom-call(bf16[32,96,256]{2,1,0:T(8,128)(2,1)S(1)} %all-to-all-done.r_ref, bf16[64,128]{1,0:T(8,128)(2,1)S(1)} %collective-permute-done.rim_ref, f32[32,128]{1,0:T(8,128)S(1)} %pad.4.cols_ref, f32[8,1024]{1,0:T(8,128)S(1)} %copy-done.5, bf16[1024,1024]{1,0:T(8,128)(2,1)S(1)} %copy-done), custom_call_target="tpu_custom_call" | custom-call | flops 1073741824 | bytes 5242880 | tf_op jit(solution)/shard_map/pallas_call | solution.py:248
  69.0 37.8 %all_to_all.20.f_ref = bf16[16,256,128]{2,1,0:T(8,128)(2,1)S(1)} all-to-all(bf16[16,256,128]{2,1,0:T(8,128)(2,1)S(1)} %shard_map.154), channel_id=1, replica_groups=mesh['batch'=16,'seq'=32] {'batch'}, dimensions={0} | all-to-all | bytes 2097152 | tf_op jit(solution)/shard_map/all_to_all | solution.py:310
  106.8 2.9 %shard_map.155 = (f32[32,64,128]{2,1,0:T(8,128)}, bf16[16,256,128]{2,1,0:T(8,128)(2,1)S(1)}) custom-call(bf16[16,256,128]{2,1,0:T(8,128)(2,1)S(1)} %all_to_all.20.f_ref, bf16[32,64,128]{2,1,0:T(8,128)(2,1)S(1)} %bitcast.17, f32[128,128]{1,0:T(8,128)S(1)} %copy-done.7), custom_call_target="tpu_custom_call" | custom-call | flops 1073741824 | bytes 5242880 | tf_op jit(solution)/shard_map/pallas_call | solution.py:248
  109.7 31.3 %all_to_all.21.y_ref = bf16[16,256,128]{2,1,0:T(8,128)(2,1)S(1)} all-to-all(bf16[16,256,128]{2,1,0:T(8,128)(2,1)S(1)} %get-tuple-element.13), channel_id=1, replica_groups=mesh['batch'=16,'seq'=32] {'batch'}, dimensions={0} | all-to-all | bytes 2097152 | tf_op jit(solution)/shard_map/all_to_all | solution.py:310
  141.1 2.9 %shard_map.156 = (bf16[512,1024]{1,0:T(8,128)(2,1)S(1)}, f32[64,128]{1,0:T(8,128)S(1)}) custom-call(bf16[16,256,128]{2,1,0:T(8,128)(2,1)S(1)} %all_to_all.21.y_ref, bf16[32,96,256]{2,1,0:T(8,128)(2,1)S(1)} %all-to-all-done.r_ref, bf16[64,128]{1,0:T(8,128)(2,1)S(1)} %collective-permute-done.rim_ref, f32[32,128]{1,0:T(8,128)S(1)} %pad.4.cols_ref, ...), custom_call_target="tpu_custom_call" | custom-call | flops 1073741824 | bytes 5242880 | tf_op jit(solution)/shard_map/pallas_call | solution.py:248
  143.9 1.9 collective-permute-start.1
  145.9 3.3 %collective-permute-done.1.next_ref = f32[64,128]{1,0:T(8,128)S(1)} collective-permute-done((f32[64,128]{1,0:T(8,128)S(1)}, f32[64,128]{1,0:T(8,128)S(1)}, u32[]{:S(2)}, u32[]{:S(2)}) %collective-permute-start.1) | collective-permute-done | bytes 32800 | tf_op jit(solution)/shard_map/ppermute | solution.py:325
  149.2 5.7 %shard_map.157 = (bf16[32,96,256]{2,1,0:T(8,128)(2,1)}, f32[32,128]{1,0:T(8,128)S(1)}) custom-call(bf16[512,1024]{1,0:T(8,128)(2,1)S(1)} %get-tuple-element.14.d_ref, bf16[32,96,256]{2,1,0:T(8,128)(2,1)S(1)} %all-to-all-done.r_ref, bf16[64,128]{1,0:T(8,128)(2,1)S(1)} %collective-permute-done.rim_ref, f32[64,128]{1,0:T(8,128)S(1)} %collective-permute-done.1.next_ref, ...), custom_call_target="tpu_custom_call" | custom-call | flops 16777216 | bytes 5242880 | tf_op jit(solution)/shard_map/pallas_call | solution.py:248
  154.9 5.3 %all-to-all-start.3 = ((bf16[32,96,256]{2,1,0:T(8,128)(2,1)}), bf16[32,96,256]{2,1,0:T(8,128)(2,1)S(1)}, u32[]{:S(2)}, u32[]{:S(2)}) async-start(bf16[32,96,256]{2,1,0:T(8,128)(2,1)} %get-tuple-element.16), calls=%async_computation.3 | async-start | bytes 3145728 | tf_op jit(solution)/shard_map/all_to_all | solution.py:310
  160.3 1.9 collective-permute-start.2
  162.2 1.1 collective-permute-done.2
  163.3 1.9 collective-permute-start.3
  165.3 2.8 %collective-permute-done.3 = f32[32,128]{1,0:T(8,128)S(1)} collective-permute-done((f32[32,128]{1,0:T(8,128)S(1)}, f32[32,128]{1,0:T(8,128)S(1)}, u32[]{:S(2)}, u32[]{:S(2)}) %collective-permute-start.3) | collective-permute-done | bytes 16416 | tf_op jit(solution)/shard_map/ppermute | solution.py:330
  168.1 2.9 %collective-permute-start.4 = (f32[32,128]{1,0:T(8,128)S(1)}, f32[32,128]{1,0:T(8,128)S(1)}, u32[]{:S(2)}, u32[]{:S(2)}) collective-permute-start(f32[32,128]{1,0:T(8,128)S(1)} %add.19), channel_id=1, source_target_pairs={{0,128},{32,160},{64,192},{96,224},{128,0},{160,32},{192,64},{224,... | collective-permute-start | bytes 49160 | tf_op jit(solution)/shard_map/ppermute | solution.py:330
  171.0 2.8 %collective-permute-done.4 = f32[32,128]{1,0:T(8,128)S(1)} collective-permute-done((f32[32,128]{1,0:T(8,128)S(1)}, f32[32,128]{1,0:T(8,128)S(1)}, u32[]{:S(2)}, u32[]{:S(2)}) %collective-permute-start.4) | collective-permute-done | bytes 16416 | tf_op jit(solution)/shard_map/ppermute | solution.py:330
  173.8 3.8 %collective-permute-start.5 = (f32[32,128]{1,0:T(8,128)S(1)}, f32[32,128]{1,0:T(8,128)S(1)}, u32[]{:S(2)}, u32[]{:S(2)}) collective-permute-start(f32[32,128]{1,0:T(8,128)S(1)} %add.20), channel_id=1, source_target_pairs={{0,256},{32,288},{64,320},{96,352},{128,384},{160,416},{192,448},{... | collective-permute-start | bytes 49160 | tf_op jit(solution)/shard_map/ppermute | solution.py:330
  177.6 4.9 %collective-permute-done.5 = f32[32,128]{1,0:T(8,128)S(1)} collective-permute-done((f32[32,128]{1,0:T(8,128)S(1)}, f32[32,128]{1,0:T(8,128)S(1)}, u32[]{:S(2)}, u32[]{:S(2)}) %collective-permute-start.5) | collective-permute-done | bytes 16416 | tf_op jit(solution)/shard_map/ppermute | solution.py:330
  184.6 13.9 %all-to-all-done.3 = bf16[32,96,256]{2,1,0:T(8,128)(2,1)S(1)} async-done(((bf16[32,96,256]{2,1,0:T(8,128)(2,1)}), bf16[32,96,256]{2,1,0:T(8,128)(2,1)S(1)}, u32[]{:S(2)}, u32[]{:S(2)}) %all-to-all-start.3) | async-done | bytes 1572896 | tf_op jit(solution)/shard_map/all_to_all | solution.py:310
  198.5 1.2 fusion.3
  (34 shorter events, 6.1 us)
Async XLA Ops:
  0.6 1.0 copy-start.2
  1.7 1.0 copy-start.3
  2.7 1.0 copy-start.4
  5.1 57.3 %copy-start.8 = (f32[3,1024]{1,0:T(4,128)S(1)}, f32[3,1024]{1,0:T(4,128)}, u32[]{:S(2)}) copy-start(f32[3,1024]{1,0:T(4,128)} %param.13) | copy-start | bytes 36868
  5.1 57.3 %copy-start.9 = (f32[3,1024]{1,0:T(4,128)S(1)}, f32[3,1024]{1,0:T(4,128)}, u32[]{:S(2)}) copy-start(f32[3,1024]{1,0:T(4,128)} %param.14) | copy-start | bytes 36868
  5.1 57.3 %copy-start.10 = (f32[1024]{0:T(1024)S(1)}, f32[1024]{0:T(1024)}, u32[]{:S(2)}) copy-start(f32[1024]{0:T(1024)} %param.15) | copy-start | bytes 12292
  5.1 58.1 %copy-start.5 = (f32[8,1024]{1,0:T(8,128)S(1)}, f32[8,1024]{1,0:T(8,128)}, u32[]{:S(2)}) copy-start(f32[8,1024]{1,0:T(8,128)} %tw_ref.3) | copy-start | bytes 98308
  5.1 50.8 %all-to-all-start = ((bf16[32,96,256]{2,1,0:T(8,128)(2,1)}), bf16[32,96,256]{2,1,0:T(8,128)(2,1)S(1)}, u32[]{:S(2)}, u32[]{:S(2)}) async-start(bf16[32,96,256]{2,1,0:T(8,128)(2,1)} %shard_map.153), calls=%async_computation | async-start | bytes 3145728 | tf_op jit(solution)/shard_map/all_to_all | solution.py:310
  55.9 7.3 %collective-permute-start = (bf16[64,128]{1,0:T(8,128)(2,1)S(1)}, bf16[64,128]{1,0:T(8,128)(2,1)S(1)}, u32[]{:S(2)}, u32[]{:S(2)}) collective-permute-start(bf16[64,128]{1,0:T(8,128)(2,1)S(1)} %slice_bitcast_fusion), channel_id=1, source_target_pairs={{0,32},{32,64},{64,96},{96,128},{128,160},{160,192},{192,224},{224... | collective-permute-start | bytes 49160 | tf_op jit(solution)/shard_map/ppermute | solution.py:321
  63.2 1.6 copy-start
  69.0 37.8 %copy-start.6 = (bf16[32,128,64]{1,2,0:T(8,128)(2,1)S(1)}, bf16[32,128,64]{1,2,0:T(8,128)(2,1)}, u32[]{:S(2)}) copy-start(bf16[32,128,64]{1,2,0:T(8,128)(2,1)} %param.18) | copy-start | bytes 1572868
  69.0 37.8 %copy-start.7 = (f32[128,128]{1,0:T(8,128)S(1)}, f32[128,128]{1,0:T(8,128)}, u32[]{:S(2)}) copy-start(f32[128,128]{1,0:T(8,128)} %mix_ref.1) | copy-start | bytes 196612
  109.7 31.3 %copy-start.1 = (bf16[1024,1024]{1,0:T(8,128)(2,1)S(1)}, bf16[1024,1024]{1,0:T(8,128)(2,1)}, u32[]{:S(2)}) copy-start(bf16[1024,1024]{1,0:T(8,128)(2,1)} %constant.14.clone.cas_ref) | copy-start | bytes 6291460
  143.9 5.2 %collective-permute-start.1 = (f32[64,128]{1,0:T(8,128)S(1)}, f32[64,128]{1,0:T(8,128)S(1)}, u32[]{:S(2)}, u32[]{:S(2)}) collective-permute-start(f32[64,128]{1,0:T(8,128)S(1)} %get-tuple-element.15), channel_id=1, source_target_pairs={{32,0},{64,32},{96,64},{128,96},{160,128},{192,160},{224,192},{256... | collective-permute-start | bytes 98312 | tf_op jit(solution)/shard_map/ppermute | solution.py:325
  154.9 43.6 %all-to-all-start.3 = ((bf16[32,96,256]{2,1,0:T(8,128)(2,1)}), bf16[32,96,256]{2,1,0:T(8,128)(2,1)S(1)}, u32[]{:S(2)}, u32[]{:S(2)}) async-start(bf16[32,96,256]{2,1,0:T(8,128)(2,1)} %get-tuple-element.16), calls=%async_computation.3 | async-start | bytes 3145728 | tf_op jit(solution)/shard_map/all_to_all | solution.py:310
  160.3 3.1 %collective-permute-start.2 = (f32[32,128]{1,0:T(8,128)S(1)}, f32[32,128]{1,0:T(8,128)S(1)}, u32[]{:S(2)}, u32[]{:S(2)}) collective-permute-start(f32[32,128]{1,0:T(8,128)S(1)} %get-tuple-element.18), channel_id=1, source_target_pairs={{0,32},{32,0},{64,96},{96,64},{128,160},{160,128},{192,224},{224,1... | collective-permute-start | bytes 49160 | tf_op jit(solution)/shard_map/ppermute | solution.py:330
  163.3 4.8 %collective-permute-start.3 = (f32[32,128]{1,0:T(8,128)S(1)}, f32[32,128]{1,0:T(8,128)S(1)}, u32[]{:S(2)}, u32[]{:S(2)}) collective-permute-start(f32[32,128]{1,0:T(8,128)S(1)} %add.18), channel_id=1, source_target_pairs={{0,64},{32,96},{64,0},{96,32},{128,192},{160,224},{192,128},{224,1... | collective-permute-start | bytes 49160 | tf_op jit(solution)/shard_map/ppermute | solution.py:330
  168.1 5.7 %collective-permute-start.4 = (f32[32,128]{1,0:T(8,128)S(1)}, f32[32,128]{1,0:T(8,128)S(1)}, u32[]{:S(2)}, u32[]{:S(2)}) collective-permute-start(f32[32,128]{1,0:T(8,128)S(1)} %add.19), channel_id=1, source_target_pairs={{0,128},{32,160},{64,192},{96,224},{128,0},{160,32},{192,64},{224,... | collective-permute-start | bytes 49160 | tf_op jit(solution)/shard_map/ppermute | solution.py:330
  173.8 8.7 %collective-permute-start.5 = (f32[32,128]{1,0:T(8,128)S(1)}, f32[32,128]{1,0:T(8,128)S(1)}, u32[]{:S(2)}, u32[]{:S(2)}) collective-permute-start(f32[32,128]{1,0:T(8,128)S(1)} %add.20), channel_id=1, source_target_pairs={{0,256},{32,288},{64,320},{96,352},{128,384},{160,416},{192,448},{... | collective-permute-start | bytes 49160 | tf_op jit(solution)/shard_map/ppermute | solution.py:330

commit v2 on v1

--- a/solution.py
+++ b/solution.py
@@ -12,6 +12,7 @@
 BLOCK = 1024
 F32, BF16 = jnp.float32, jnp.bfloat16
 GRANT = 20 << 20
+PARTS = 4
 
 
 def cas_table():
@@ -38,15 +39,33 @@
     return jnp.broadcast_to(cols[:, at : at + 1], (cols.shape[0], 128))
 
 
-def gather_kernel(a_ref, b_ref, c_ref, out_ref, sems):
-    copies = [
-        pltpu.make_async_copy(ref, out_ref.at[:, k * 32 : k * 32 + 32, :], sems.at[k])
-        for k, ref in enumerate((a_ref, b_ref, c_ref))
-    ]
-    for copy in copies:
+def gather_kernel(a_ref, b_ref, c_ref, out_ref, held, in_sems, out_sems):
+    size = 32 // PARTS
+    arrive, leave = [], []
+    for p in range(PARTS):
+        own = slice(p * size, p * size + size)
+        arrive.append(
+            [
+                pltpu.make_async_copy(ref.at[own], held.at[own, k * 32 : k * 32 + 32, :], in_sems.at[p, k])
+                for k, ref in enumerate((a_ref, b_ref, c_ref))
+            ]
+        )
+        leave.append(pltpu.make_async_copy(held.at[own], out_ref.at[own], out_sems.at[p]))
+    for part in arrive:
+        for copy in part:
+            copy.start()
+    for part, copy in zip(arrive, leave):
+        for one in part:
+            one.wait()
         copy.start()
-    for copy in copies:
+    for copy in leave:
         copy.wait()
+
+
+def keep_kernel(table_ref, out_ref, sem):
+    copy = pltpu.make_async_copy(table_ref, out_ref, sem)
+    copy.start()
+    copy.wait()
 
 
 def spread_kernel(r_ref, rim_ref, cols_ref, tw_ref, cas_ref, out_ref, lhs):
@@ -127,20 +146,21 @@
         for f in range(2):
             wide[f][pl.ds(c, 128, stride=16), :] = sums[:, f * 128 : f * 128 + 128]
     for f in range(2):
+        wide[f][2048:2064, :] = jnp.zeros((16, 128), F32)
         for b in range(16):
-            out_ref[b, f * 128 : f * 128 + 128, :] = wide[f][b * 128 : b * 128 + 128, :].astype(BF16)
-
-
-def back_kernel(y_ref, r_ref, rim_ref, cols_ref, tw_ref, cas_ref, out_ref, head_ref, lhs):
+            out_ref[b, f * 144 : f * 144 + 144, :] = wide[f][b * 128 : b * 128 + 144, :].astype(BF16)
+
+
+def final_kernel(y_ref, r_ref, rim_ref, next_ref, cols_ref, tw_ref, cas_ref, out_ref, sums_ref, lhs, d_ref):
     low = lanes((16, 128)) < 64
 
     def unpack(y, _):
         at = pl.multiple_of(y * 128, 128)
         tw = tw_ref[:, pl.ds(at, 128)]
-        for m in range(16):
+        for m in range(18):
             e = y_ref[2 * y, m * 16 : m * 16 + 16, :].astype(F32)
             o = y_ref[2 * y + 1, m * 16 : m * 16 + 16, :].astype(F32)
-            row = tw[m % 8 : m % 8 + 1, :]
+            row = tw[m % 9 : m % 9 + 1, :]
             a = jnp.where(low, e, pltpu.roll(o, 64, 1)) * row
             b = jnp.where(low, pltpu.roll(e, 64, 1), o) * row
             lhs[m * 32 : m * 32 + 16, pl.ds(at, 128)] = a.astype(BF16)
@@ -152,27 +172,11 @@
     def strip(n, _):
         at = pl.multiple_of(n * 256, 256)
         sums = jnp.dot(lhs[...], cas_ref[:, pl.ds(at, 256)], preferred_element_type=F32)
-        out_ref[:, pl.ds(at, 256)] = sums.astype(BF16)
+        d_ref[:, pl.ds(at, 256)] = sums.astype(BF16)
         return 0
 
     lax.fori_loop(0, 4, strip, 0)
 
-    lane = lanes()
-    cols = cols_ref[...]
-    v, g, c = (r_ref[0, k * 32 : k * 32 + 32, 0:128].astype(F32) for k in range(3))
-    before_v, before_g = rim_ref[0:32, :].astype(F32), rim_ref[32:64, :].astype(F32)
-    short_v, short_g = v * column(cols, 0), g * column(cols, 3)
-    for k in (1, 2):
-        short_v += column(cols, k) * back_in_time(pltpu.roll(v, k, 1), pltpu.roll(before_v, k, 1), k, lane)
-        short_g += column(cols, 3 + k) * back_in_time(pltpu.roll(g, k, 1), pltpu.roll(before_g, k, 1), k, lane)
-    short_v = short_v.astype(BF16).astype(F32)
-    grad_long = (c * short_g).astype(BF16).astype(F32)
-    skip = column(cols, 6)
-    head_ref[0:32, :] = skip * grad_long + out_ref[256:288, 0:128].astype(F32)
-    head_ref[32:64, :] = c * (out_ref[0:32, 0:128].astype(F32) + skip * short_v)
-
-
-def final_kernel(d_ref, r_ref, rim_ref, next_ref, cols_ref, out_ref, sums_ref):
     lane = lanes((16, 128))
 
     def ahead(tile):
@@ -209,7 +213,7 @@
                 c = r_ref[piece, three, at].astype(F32)
                 grad_long = (c * short_g).astype(BF16).astype(F32)
                 long_v = d_ref[pl.ds(rows, 16), t * 128 : t * 128 + 128].astype(F32)
-                back_g = d_ref[pl.ds(rows + 256, 16), t * 128 : t * 128 + 128].astype(F32)
+                back_g = d_ref[pl.ds(rows + 288, 16), t * 128 : t * 128 + 128].astype(F32)
                 direct = long_v + skip * short_v
                 gsg = c * direct
                 gsv = skip * grad_long + back_g
@@ -228,12 +232,21 @@
 
         last_v = r_ref[31, one, 128:256].astype(F32)
         last_g = r_ref[31, two, 128:256].astype(F32)
+        next_v, next_g, next_c = (next_ref[rows, :].astype(F32) for rows in (one, two, three))
+        short_v, short_g = tv[0] * next_v, tg[0] * next_g
+        for k in (1, 2):
+            short_v += tv[k] * back_in_time(pltpu.roll(next_v, k, 1), pltpu.roll(last_v, k, 1), k, lane)
+            short_g += tg[k] * back_in_time(pltpu.roll(next_g, k, 1), pltpu.roll(last_g, k, 1), k, lane)
+        short_v = short_v.astype(BF16).astype(F32)
+        grad_long = (next_c * short_g).astype(BF16).astype(F32)
+        long_v = d_ref[h * 16 + 256 : h * 16 + 272, 0:128].astype(F32)
+        back_g = d_ref[h * 16 + 544 : h * 16 + 560, 0:128].astype(F32)
         zero = jnp.zeros((16, 128), F32)
         start = (
             (last_v, *rolled(last_v)),
             (last_g, *rolled(last_g)),
-            ahead(next_ref[one, :]),
-            ahead(next_ref[two, :]),
+            ahead(skip * grad_long + back_g),
+            ahead(next_c * (long_v + skip * short_v)),
             (zero,) * 7,
         )
         acc = lax.fori_loop(0, 8, block, start)[4]
@@ -263,8 +276,8 @@
 def mix(by_freq, spectrum, mixing):
     return call(
         mix_kernel,
-        [((32, 64, 128), F32), ((16, 256, 128), BF16)],
-        [((2048, 128), F32), ((2048, 128), F32)],
+        [((32, 64, 128), F32), ((16, 288, 128), BF16)],
+        [((2064, 128), F32), ((2064, 128), F32)],
         1 << 30,
         5 << 20,
         by_freq,
@@ -273,37 +286,64 @@
     )
 
 
-def back(returned, r, rim, cols, twiddle, cas):
+def final(returned, r, rim, following, cols, twiddle, cas):
     return call(
-        back_kernel,
-        [((512, 1024), BF16), ((64, 128), F32)],
-        [((512, 1024), BF16)],
+        final_kernel,
+        [((32, 96, 256), BF16), ((32, 128), F32)],
+        [((576, 1024), BF16), ((576, 1024), BF16)],
         1 << 30,
-        5 << 20,
+        8 << 20,
         returned,
         r,
         rim,
+        following,
         cols,
         twiddle,
         cas,
     )
 
 
-def final(d, r, rim, following, cols):
-    return call(
-        final_kernel, [((32, 96, 256), BF16), ((32, 128), F32)], [], 1 << 24, 5 << 20, d, r, rim, following, cols
-    )
-
-
 def gather(*fields):
     return pl.pallas_call(
         gather_kernel,
-        in_specs=[pl.BlockSpec(memory_space=pltpu.HBM)] * 3,
+        in_specs=[pl.BlockSpec(memory_space=pl.ANY)] * 3,
+        out_specs=pl.BlockSpec(memory_space=pl.ANY),
+        out_shape=jax.ShapeDtypeStruct((32, 96, 256), BF16),
+        scratch_shapes=[
+            pltpu.VMEM((32, 96, 256), BF16),
+            pltpu.SemaphoreType.DMA((PARTS, 3)),
+            pltpu.SemaphoreType.DMA((PARTS,)),
+        ],
+    )(*fields)
+
+
+def keep(table):
+    return pl.pallas_call(
+        keep_kernel,
+        in_specs=[pl.BlockSpec(memory_space=pl.ANY)],
         out_specs=pl.BlockSpec(memory_space=pltpu.VMEM),
-        out_shape=jax.ShapeDtypeStruct((32, 96, 256), BF16),
-        scratch_shapes=[pltpu.SemaphoreType.DMA((3,))],
+        out_shape=jax.ShapeDtypeStruct(table.shape, table.dtype),
+        scratch_shapes=[pltpu.SemaphoreType.DMA(())],
         compiler_params=pltpu.CompilerParams(vmem_limit_bytes=GRANT),
-    )(*fields)
+        cost_estimate=pl.CostEstimate(flops=0, bytes_accessed=4 << 20, transcendentals=0),
+    )(table)
+
+
+def last_columns(values, gates):
+    batch, seq = lax.axis_size("batch"), lax.axis_size("seq")
+    axes = ("batch", "seq")
+    rows = jnp.concatenate([values[:, -2:], gates[:, -2:]], axis=1).T
+    half = seq // 2
+    held = sum(
+        lax.ppermute(rows, axes, [(b * seq + seq - 1, (b + 1) * seq + at) for b in range(batch - 1)]) for at in (0, half)
+    )
+    step = half // 2
+    while step:
+        held = held + lax.ppermute(held, "seq", [(at, at + step) for at in range(0, seq, 2 * step)])
+        step //= 2
+    own = lax.dynamic_slice(held, (0, lax.axis_index("seq") * 32), (4, 32))
+    own = jnp.concatenate([own[:2].T, own[2:].T], axis=0)
+    return jnp.pad(own, ((0, 0), (126, 0)))
 
 
 def exchange(array, axis):
@@ -312,18 +352,20 @@
 
 def per_device(values, gates, cotangent, taps_values, taps_gates, skip_gain, twiddle, mixing, spectrum):
     batch = lax.axis_size("batch")
-    cas = jnp.asarray(cas_table())
     raw = gather(*(x.reshape(32, 32, 256) for x in (values, gates, cotangent)))
     r = exchange(raw, "seq")
+    cas = keep(jnp.asarray(cas_table()))
+    rim = last_columns(values, gates)
     gains = jnp.concatenate([taps_values, taps_gates, skip_gain[None]], axis=0)
     cols = lax.dynamic_slice(gains, (0, lax.axis_index("seq") * 32), (7, 32))
     cols = jnp.pad(cols.T, ((0, 0), (0, 121)))
-    rim = lax.ppermute(r[31, :64, 128:], "batch", [(i, i + 1) for i in range(batch - 1)])
     by_freq = exchange(spread(r, rim, cols, twiddle, cas), "batch")
+    behind = [(i + 1, i) for i in range(batch - 1)]
+    first, row = lax.optimization_barrier((r[0, :, :128], twiddle[:1]))
+    following = lax.ppermute(first, "batch", behind)
+    rows = jnp.concatenate([twiddle, lax.ppermute(row, "batch", behind)], axis=0)
     grad_spectrum, weighted = mix(by_freq, spectrum.transpose(0, 2, 1), mixing)
-    d, head = back(exchange(weighted, "batch"), r, rim, cols, twiddle, cas)
-    following = lax.ppermute(head, "batch", [(i + 1, i) for i in range(batch - 1)])
-    done, sums = final(d, r, rim, following, cols)
+    done, sums = final(exchange(weighted, "batch"), r, rim, following, cols, rows, cas)
     outs = exchange(done, "seq")
     step = 1
     while step < batch:

time: 200 us -> 206 us (1.030)
  blocking collectives: 69.1 us -> 36.2 us
  waiting for transfers between devices: 66.4 us -> 91.3 us
  starting transfers between devices: 38.1 us -> 47.6 us
  Pallas kernels: 17 us -> 20 us
    ppermute x2 -> x8, waiting for transfers between devices: 3.94 us -> 62.2 us  [the longest x2 36.7 us: last_columns(): lax.ppermute(rows, axes, [(b * seq + seq - 1, (b + 1) * seq + at) for b i...]
    all_to_all x2 -> x3, waiting for transfers between devices: 50.8 us -> 17.1 us  [exchange(): return lax.all_to_all(array, axis, 0, 0, tiled=True)]
    all_to_all x2 -> x1, blocking collectives: 69.1 us -> 36.2 us  [exchange(): return lax.all_to_all(array, axis, 0, 0, tiled=True)]
    all_to_all x2 -> x3, starting transfers between devices: 19.2 us -> 26.8 us  [exchange(): return lax.all_to_all(array, axis, 0, 0, tiled=True)]
    ppermute x2 -> x8, starting transfers between devices: 8.38 us -> 10.9 us  [the longest x4 5.14 us: last_columns(): lax.ppermute(held, 'seq', [(at, at + step) for at in range(0, seq, 2 * st...]
    pallas_call x4 -> x3, Pallas kernels: 15.7 us -> 17.5 us  [call(): pl.pallas_call(kernel, in_specs=[vmem] * len(args), out_specs=[vmem] * le...]
    unnamed x25 -> x27, local copies, waits for them, and re-layouts: 6.15 us -> 5.74 us
  transfers between devices with their start and end apart: 8 -> 15, of which waited for: 8 -> 12; matrix products, arithmetic and copies ran while one was open for 1% -> 2% of each run, Pallas kernels for 0% -> 0%
where the time goes in v2:
time: 206 us; the launch traced here: 205 us
  waiting for transfers between devices  91.3 us (44%)
  starting transfers between devices  47.6 us (23%)
  blocking collectives  36.2 us (18%)
  Pallas kernels  20 us (10%)
  local copies, waits for them, and re-layouts  8.9 us (4%)
    ppermute x2, waiting for transfers between devices, last_columns(): lax.ppermute(rows, axes, [(b * seq + seq - 1, (b + 1) * seq + at) for b i...  36.7 us
    all_to_all x1, blocking collectives, exchange(): return lax.all_to_all(array, axis, 0, 0, tiled=True)  36.2 us
    all_to_all x3, starting transfers between devices, exchange(): return lax.all_to_all(array, axis, 0, 0, tiled=True)  26.8 us
    ppermute x1, waiting for transfers between devices, per_device(): lax.ppermute(row, 'batch', behind)  23 us
    pallas_call x3, Pallas kernels, call(): pl.pallas_call(kernel, in_specs=[vmem] * len(args), out_specs=[vmem] * le...  17.5 us
    all_to_all x3, waiting for transfers between devices, exchange(): return lax.all_to_all(array, axis, 0, 0, tiled=True)  17.1 us
    ppermute x4, waiting for transfers between devices, per_device(): lax.ppermute(sums, 'batch', [(i, i ^ step) for i in range(batch)])  12 us
    ppermute x4, starting transfers between devices, per_device(): lax.ppermute(sums, 'batch', [(i, i ^ step) for i in range(batch)])  9.85 us
  transfers between devices with their start and end apart: 15, of which 12 were waited for; matrix products, arithmetic and copies ran while one was open for 2% of the time, Pallas kernels for 0%

profile of v2, /device:TPU:1, one launch (start us, length us, event | category | flops | bytes accessed | tf_op | source)
XLA Modules:
  0.0 205.3 jit_solution(17664415866733239871)
XLA Ops:
  0.6 2.4 %shard_map.153 = bf16[32,96,256]{2,1,0:T(8,128)(2,1)} custom-call(bf16[32,32,256]{2,1,0:T(8,128)(2,1)} %bitcast.21, bf16[32,32,256]{2,1,0:T(8,128)(2,1)} %bitcast.22, bf16[32,32,256]{2,1,0:T(8,128)(2,1)} %bitcast.23), custom_call_target="tpu_custom_call" | custom-call | tf_op jit(solution)/shard_map/pallas_call | solution.py:307
  3.0 14.0 %all-to-all-start = ((bf16[32,96,256]{2,1,0:T(8,128)(2,1)}), bf16[32,96,256]{2,1,0:T(8,128)(2,1)}, u32[]{:S(2)}, u32[]{:S(2)}) async-start(bf16[32,96,256]{2,1,0:T(8,128)(2,1)} %shard_map.153), calls=%async_computation | async-start | bytes 3145728 | tf_op jit(solution)/shard_map/all_to_all | solution.py:350
  18.3 1.3 collective-permute-start
  19.6 36.7 %collective-permute-done = bf16[4,1024]{1,0:T(4,128)(2,1)S(1)} collective-permute-done((bf16[4,1024]{1,0:T(4,128)(2,1)S(1)}, bf16[4,1024]{1,0:T(4,128)(2,1)S(1)}, u32[]{:S(2)}, u32[]{:S(2)}) %collective-permute-start) | collective-permute-done | bytes 8224 | tf_op jit(solution)/shard_map/ppermute | solution.py:338
  56.4 1.3 collective-permute-start.2
  64.1 1.6 copy-done
  66.4 5.6 %shard_map.155 = bf16[16,256,128]{2,1,0:T(8,128)(2,1)S(1)} custom-call(bf16[32,96,256]{2,1,0:T(8,128)(2,1)} %all-to-all-done.r_ref, bf16[64,128]{1,0:T(8,128)(2,1)S(1)} %pad.8.rim_ref, f32[32,128]{1,0:T(8,128)S(1)} %pad.9.cols_ref, f32[8,1024]{1,0:T(8,128)S(1)} %copy-done.3, bf16[1024,1024]{1,0:T(8,128)(2,1)S(1)} %shard_map.154.cas_ref), custom_call_target="tpu_custom_call" | custom-call | flops 1073741824 | bytes 5242880 | tf_op jit(solution)/shard_map/pallas_call | solution.py:261
  72.0 36.2 %all_to_all.20.f_ref = bf16[16,256,128]{2,1,0:T(8,128)(2,1)S(1)} all-to-all(bf16[16,256,128]{2,1,0:T(8,128)(2,1)S(1)} %shard_map.155), channel_id=1, replica_groups=mesh['batch'=16,'seq'=32] {'batch'}, dimensions={0} | all-to-all | bytes 2097152 | tf_op jit(solution)/shard_map/all_to_all | solution.py:350
  108.3 2.9 %shard_map.156 = (f32[32,64,128]{2,1,0:T(8,128)}, bf16[16,288,128]{2,1,0:T(8,128)(2,1)S(1)}) custom-call(bf16[16,256,128]{2,1,0:T(8,128)(2,1)S(1)} %all_to_all.20.f_ref, bf16[32,64,128]{2,1,0:T(8,128)(2,1)S(1)} %bitcast.20, f32[128,128]{1,0:T(8,128)S(1)} %copy-done.5), custom_call_target="tpu_custom_call" | custom-call | flops 1073741824 | bytes 5242880 | tf_op jit(solution)/shard_map/pallas_call | solution.py:261
  112.2 3.6 %all-to-all-start.2 = ((bf16[16,288,128]{2,1,0:T(8,128)(2,1)}), bf16[16,288,128]{2,1,0:T(8,128)(2,1)S(1)}, u32[]{:S(2)}, u32[]{:S(2)}) async-start(bf16[16,288,128]{2,1,0:T(8,128)(2,1)} %copy-done.2), calls=%async_computation.2 | async-start | bytes 2359296 | tf_op jit(solution)/shard_map/all_to_all | solution.py:350
  116.6 1.9 collective-permute-start.7
  118.5 1.9 collective-permute-start.6
  120.4 23.0 %collective-permute-done.7 = f32[1,1024]{1,0:T(1,128)S(1)} collective-permute-done((f32[1,1024]{1,0:T(1,128)S(1)}, f32[1,1024]{1,0:T(1,128)S(1)}, u32[]{:S(2)}, u32[]{:S(2)}) %collective-permute-start.7) | collective-permute-done | bytes 4128 | tf_op jit(solution)/shard_map/ppermute | solution.py:366
  143.7 2.1 %all-to-all-done.2.y_ref = bf16[16,288,128]{2,1,0:T(8,128)(2,1)S(1)} async-done(((bf16[16,288,128]{2,1,0:T(8,128)(2,1)}), bf16[16,288,128]{2,1,0:T(8,128)(2,1)S(1)}, u32[]{:S(2)}, u32[]{:S(2)}) %all-to-all-start.2) | async-done | bytes 1179680 | tf_op jit(solution)/shard_map/all_to_all | solution.py:350
  145.8 9.0 %shard_map.157 = (bf16[32,96,256]{2,1,0:T(8,128)(2,1)S(1)}, f32[32,128]{1,0:T(8,128)S(1)}) custom-call(bf16[16,288,128]{2,1,0:T(8,128)(2,1)S(1)} %all-to-all-done.2.y_ref, bf16[32,96,256]{2,1,0:T(8,128)(2,1)} %all-to-all-done.r_ref, bf16[64,128]{1,0:T(8,128)(2,1)S(1)} %pad.8.rim_ref, bf16[96,128]{1,0:T(8,128)(2,1)S(1)} %collective-permute-done.6.next_ref, ...), custom_call_target="tpu_custom_call" | custom-call | flops 1073741824 | bytes 8388608 | tf_op jit(solution)/shard_map/pallas_call | solution.py:261
  156.0 9.3 %all-to-all-start.3 = ((bf16[32,96,256]{2,1,0:T(8,128)(2,1)}), bf16[32,96,256]{2,1,0:T(8,128)(2,1)S(1)}, u32[]{:S(2)}, u32[]{:S(2)}) async-start(bf16[32,96,256]{2,1,0:T(8,128)(2,1)} %copy-done.1), calls=%async_computation.3 | async-start | bytes 3145728 | tf_op jit(solution)/shard_map/all_to_all | solution.py:350
  165.2 1.9 collective-permute-start.8
  168.3 1.9 collective-permute-start.9
  170.2 2.8 %collective-permute-done.9 = f32[32,128]{1,0:T(8,128)S(1)} collective-permute-done((f32[32,128]{1,0:T(8,128)S(1)}, f32[32,128]{1,0:T(8,128)S(1)}, u32[]{:S(2)}, u32[]{:S(2)}) %collective-permute-start.9) | collective-permute-done | bytes 16416 | tf_op jit(solution)/shard_map/ppermute | solution.py:372
  173.1 2.4 %collective-permute-start.10 = (f32[32,128]{1,0:T(8,128)S(1)}, f32[32,128]{1,0:T(8,128)S(1)}, u32[]{:S(2)}, u32[]{:S(2)}) collective-permute-start(f32[32,128]{1,0:T(8,128)S(1)} %add.42), channel_id=1, source_target_pairs={{0,128},{32,160},{64,192},{96,224},{128,0},{160,32},{192,64},{224,... | collective-permute-start | bytes 49160 | tf_op jit(solution)/shard_map/ppermute | solution.py:372
  175.5 3.3 %collective-permute-done.10 = f32[32,128]{1,0:T(8,128)S(1)} collective-permute-done((f32[32,128]{1,0:T(8,128)S(1)}, f32[32,128]{1,0:T(8,128)S(1)}, u32[]{:S(2)}, u32[]{:S(2)}) %collective-permute-start.10) | collective-permute-done | bytes 16416 | tf_op jit(solution)/shard_map/ppermute | solution.py:372
  178.8 3.6 %collective-permute-start.11 = (f32[32,128]{1,0:T(8,128)S(1)}, f32[32,128]{1,0:T(8,128)S(1)}, u32[]{:S(2)}, u32[]{:S(2)}) collective-permute-start(f32[32,128]{1,0:T(8,128)S(1)} %add.43), channel_id=1, source_target_pairs={{0,256},{32,288},{64,320},{96,352},{128,384},{160,416},{192,448},{... | collective-permute-start | bytes 49160 | tf_op jit(solution)/shard_map/ppermute | solution.py:372
  182.4 4.7 %collective-permute-done.11 = f32[32,128]{1,0:T(8,128)S(1)} collective-permute-done((f32[32,128]{1,0:T(8,128)S(1)}, f32[32,128]{1,0:T(8,128)S(1)}, u32[]{:S(2)}, u32[]{:S(2)}) %collective-permute-start.11) | collective-permute-done | bytes 16416 | tf_op jit(solution)/shard_map/ppermute | solution.py:372
  189.2 15.0 %all-to-all-done.3 = bf16[32,96,256]{2,1,0:T(8,128)(2,1)S(1)} async-done(((bf16[32,96,256]{2,1,0:T(8,128)(2,1)}), bf16[32,96,256]{2,1,0:T(8,128)(2,1)S(1)}, u32[]{:S(2)}, u32[]{:S(2)}) %all-to-all-start.3) | async-done | bytes 1572896 | tf_op jit(solution)/shard_map/all_to_all | solution.py:350
  (63 shorter events, 16.0 us)
Async XLA Ops:
  3.0 14.0 %copy-start.6 = (bf16[1024,256]{1,0:T(8,128)(2,1)S(1)}, bf16[1024,256]{1,0:T(8,128)(2,1)}, u32[]{:S(2)}) copy-start(bf16[1024,256]{1,0:T(8,128)(2,1)} %param.10) | copy-start | bytes 1572868
  3.0 14.2 %copy-start.7 = (bf16[1024,256]{1,0:T(8,128)(2,1)S(1)}, bf16[1024,256]{1,0:T(8,128)(2,1)}, u32[]{:S(2)}) copy-start(bf16[1024,256]{1,0:T(8,128)(2,1)} %param.11) | copy-start | bytes 1572868
  3.0 63.2 %all-to-all-start = ((bf16[32,96,256]{2,1,0:T(8,128)(2,1)}), bf16[32,96,256]{2,1,0:T(8,128)(2,1)}, u32[]{:S(2)}, u32[]{:S(2)}) async-start(bf16[32,96,256]{2,1,0:T(8,128)(2,1)} %shard_map.153), calls=%async_computation | async-start | bytes 3145728 | tf_op jit(solution)/shard_map/all_to_all | solution.py:350
  17.0 46.9 %copy-start.8 = (f32[3,1024]{1,0:T(4,128)S(1)}, f32[3,1024]{1,0:T(4,128)}, u32[]{:S(2)}) copy-start(f32[3,1024]{1,0:T(4,128)} %param.13) | copy-start | bytes 36868
  17.0 46.9 %copy-start.9 = (f32[3,1024]{1,0:T(4,128)S(1)}, f32[3,1024]{1,0:T(4,128)}, u32[]{:S(2)}) copy-start(f32[3,1024]{1,0:T(4,128)} %param.14) | copy-start | bytes 36868
  17.0 46.9 %copy-start.10 = (f32[1024]{0:T(1024)S(1)}, f32[1024]{0:T(1024)}, u32[]{:S(2)}) copy-start(f32[1024]{0:T(1024)} %param.15) | copy-start | bytes 12292
  17.7 2.0 collective-permute-start.1
  18.3 38.0 %collective-permute-start = (bf16[4,1024]{1,0:T(4,128)(2,1)S(1)}, bf16[4,1024]{1,0:T(4,128)(2,1)S(1)}, u32[]{:S(2)}, u32[]{:S(2)}) collective-permute-start(bf16[4,1024]{1,0:T(4,128)(2,1)S(1)} %maximum_bitcast_fusion), channel_id=1, source_target_pairs={{31,32},{63,64},{95,96},{127,128},{159,160},{191,192},{223,224},{2... | collective-permute-start | bytes 24584 | tf_op jit(solution)/shard_map/ppermute | solution.py:338
  56.4 2.1 %collective-permute-start.2 = (bf16[4,1024]{1,0:T(4,128)(2,1)S(1)}, bf16[4,1024]{1,0:T(4,128)(2,1)S(1)}, u32[]{:S(2)}, u32[]{:S(2)}) collective-permute-start(bf16[4,1024]{1,0:T(4,128)(2,1)S(1)} %add.35), channel_id=1, source_target_pairs={{0,8},{16,24},{32,40},{48,56},{64,72},{80,88},{96,104},{112,120},{... | collective-permute-start | bytes 24584 | tf_op jit(solution)/shard_map/ppermute | solution.py:342
  58.4 2.1 %collective-permute-start.3 = (bf16[4,1024]{1,0:T(4,128)(2,1)S(1)}, bf16[4,1024]{1,0:T(4,128)(2,1)S(1)}, u32[]{:S(2)}, u32[]{:S(2)}) collective-permute-start(bf16[4,1024]{1,0:T(4,128)(2,1)S(1)} %add.36), channel_id=1, source_target_pairs={{0,4},{8,12},{16,20},{24,28},{32,36},{40,44},{48,52},{56,60},{64,6... | collective-permute-start | bytes 24584 | tf_op jit(solution)/shard_map/ppermute | solution.py:342
  60.5 2.1 %collective-permute-start.4 = (bf16[4,1024]{1,0:T(4,128)(2,1)S(1)}, bf16[4,1024]{1,0:T(4,128)(2,1)S(1)}, u32[]{:S(2)}, u32[]{:S(2)}) collective-permute-start(bf16[4,1024]{1,0:T(4,128)(2,1)S(1)} %add.37), channel_id=1, source_target_pairs={{0,2},{4,6},{8,10},{12,14},{16,18},{20,22},{24,26},{28,30},{32,34}... | collective-permute-start | bytes 24584 | tf_op jit(solution)/shard_map/ppermute | solution.py:342
  62.6 3.3 %collective-permute-start.5 = (bf16[4,1024]{1,0:T(4,128)(2,1)S(1)}, bf16[4,1024]{1,0:T(4,128)(2,1)S(1)}, u32[]{:S(2)}, u32[]{:S(2)}) collective-permute-start(bf16[4,1024]{1,0:T(4,128)(2,1)S(1)} %add.38), channel_id=1, source_target_pairs={{0,1},{2,3},{4,5},{6,7},{8,9},{10,11},{12,13},{14,15},{16,17},{18,... | collective-permute-start | bytes 24584 | tf_op jit(solution)/shard_map/ppermute | solution.py:342
  64.1 1.6 copy-start
  72.0 36.2 %copy-start.4 = (bf16[32,128,64]{1,2,0:T(8,128)(2,1)S(1)}, bf16[32,128,64]{1,2,0:T(8,128)(2,1)}, u32[]{:S(2)}) copy-start(bf16[32,128,64]{1,2,0:T(8,128)(2,1)} %param.18) | copy-start | bytes 1572868
  72.0 36.2 %copy-start.5 = (f32[128,128]{1,0:T(8,128)S(1)}, f32[128,128]{1,0:T(8,128)}, u32[]{:S(2)}) copy-start(f32[128,128]{1,0:T(8,128)} %mix_ref.1) | copy-start | bytes 196612
  112.2 33.5 %all-to-all-start.2 = ((bf16[16,288,128]{2,1,0:T(8,128)(2,1)}), bf16[16,288,128]{2,1,0:T(8,128)(2,1)S(1)}, u32[]{:S(2)}, u32[]{:S(2)}) async-start(bf16[16,288,128]{2,1,0:T(8,128)(2,1)} %copy-done.2), calls=%async_computation.2 | async-start | bytes 2359296 | tf_op jit(solution)/shard_map/all_to_all | solution.py:350
  116.6 26.8 %collective-permute-start.7 = (f32[1,1024]{1,0:T(1,128)S(1)}, f32[1,1024]{1,0:T(1,128)S(1)}, u32[]{:S(2)}, u32[]{:S(2)}) collective-permute-start(f32[1,1024]{1,0:T(1,128)S(1)} %slice.44), channel_id=1, source_target_pairs={{32,0},{64,32},{96,64},{128,96},{160,128},{192,160},{224,192},{256... | collective-permute-start | bytes 12296 | tf_op jit(solution)/shard_map/ppermute | solution.py:366
  118.5 25.1 %collective-permute-start.6 = (bf16[96,128]{1,0:T(8,128)(2,1)S(1)}, bf16[96,128]{1,0:T(8,128)(2,1)S(1)}, u32[]{:S(2)}, u32[]{:S(2)}) collective-permute-start(bf16[96,128]{1,0:T(8,128)(2,1)S(1)} %slice_bitcast_fusion), channel_id=1, source_target_pairs={{32,0},{64,32},{96,64},{128,96},{160,128},{192,160},{224,192},{256... | collective-permute-start | bytes 73736 | tf_op jit(solution)/shard_map/ppermute | solution.py:365
  154.8 1.2 copy-start.1
  156.0 48.2 %all-to-all-start.3 = ((bf16[32,96,256]{2,1,0:T(8,128)(2,1)}), bf16[32,96,256]{2,1,0:T(8,128)(2,1)S(1)}, u32[]{:S(2)}, u32[]{:S(2)}) async-start(bf16[32,96,256]{2,1,0:T(8,128)(2,1)} %copy-done.1), calls=%async_computation.3 | async-start | bytes 3145728 | tf_op jit(solution)/shard_map/all_to_all | solution.py:350
  165.2 3.1 %collective-permute-start.8 = (f32[32,128]{1,0:T(8,128)S(1)}, f32[32,128]{1,0:T(8,128)S(1)}, u32[]{:S(2)}, u32[]{:S(2)}) collective-permute-start(f32[32,128]{1,0:T(8,128)S(1)} %get-tuple-element.18), channel_id=1, source_target_pairs={{0,32},{32,0},{64,96},{96,64},{128,160},{160,128},{192,224},{224,1... | collective-permute-start | bytes 49160 | tf_op jit(solution)/shard_map/ppermute | solution.py:372
  168.3 4.8 %collective-permute-start.9 = (f32[32,128]{1,0:T(8,128)S(1)}, f32[32,128]{1,0:T(8,128)S(1)}, u32[]{:S(2)}, u32[]{:S(2)}) collective-permute-start(f32[32,128]{1,0:T(8,128)S(1)} %add.41), channel_id=1, source_target_pairs={{0,64},{32,96},{64,0},{96,32},{128,192},{160,224},{192,128},{224,1... | collective-permute-start | bytes 49160 | tf_op jit(solution)/shard_map/ppermute | solution.py:372
  173.1 5.7 %collective-permute-start.10 = (f32[32,128]{1,0:T(8,128)S(1)}, f32[32,128]{1,0:T(8,128)S(1)}, u32[]{:S(2)}, u32[]{:S(2)}) collective-permute-start(f32[32,128]{1,0:T(8,128)S(1)} %add.42), channel_id=1, source_target_pairs={{0,128},{32,160},{64,192},{96,224},{128,0},{160,32},{192,64},{224,... | collective-permute-start | bytes 49160 | tf_op jit(solution)/shard_map/ppermute | solution.py:372
  178.8 8.4 %collective-permute-start.11 = (f32[32,128]{1,0:T(8,128)S(1)}, f32[32,128]{1,0:T(8,128)S(1)}, u32[]{:S(2)}, u32[]{:S(2)}) collective-permute-start(f32[32,128]{1,0:T(8,128)S(1)} %add.43), channel_id=1, source_target_pairs={{0,256},{32,288},{64,320},{96,352},{128,384},{160,416},{192,448},{... | collective-permute-start | bytes 49160 | tf_op jit(solution)/shard_map/ppermute | solution.py:372
  (2 other events, 1.8 us)

commit v3 on v1

--- a/solution.py
+++ b/solution.py
@@ -1,4 +1,3 @@
-import functools
 import math
 
 import jax
@@ -9,9 +8,11 @@
 from jax.experimental.pallas import tpu as pltpu
 from jax.sharding import PartitionSpec as P
 
+
 BLOCK = 1024
 F32, BF16 = jnp.float32, jnp.bfloat16
 GRANT = 20 << 20
+PARTS = 4
 
 
 def cas_table():
@@ -38,22 +39,45 @@
     return jnp.broadcast_to(cols[:, at : at + 1], (cols.shape[0], 128))
 
 
-def gather_kernel(a_ref, b_ref, c_ref, out_ref, sems):
-    copies = [
-        pltpu.make_async_copy(ref, out_ref.at[:, k * 32 : k * 32 + 32, :], sems.at[k])
-        for k, ref in enumerate((a_ref, b_ref, c_ref))
-    ]
-    for copy in copies:
+def gather_kernel(a_ref, b_ref, c_ref, out_ref, held, in_sems, out_sems):
+    size = 32 // PARTS
+    arrive, leave = [], []
+    for p in range(PARTS):
+        own = slice(p * size, p * size + size)
+        arrive.append(
+            [
+                pltpu.make_async_copy(ref.at[own], held.at[own, k * 32 : k * 32 + 32, :], in_sems.at[p, k])
+                for k, ref in enumerate((a_ref, b_ref, c_ref))
+            ]
+        )
+        leave.append(pltpu.make_async_copy(held.at[own], out_ref.at[own], out_sems.at[p]))
+    for part in arrive:
+        for copy in part:
+            copy.start()
+    for part, copy in zip(arrive, leave):
+        for one in part:
+            one.wait()
         copy.start()
-    for copy in copies:
+    for copy in leave:
         copy.wait()
 
 
-def spread_kernel(r_ref, rim_ref, cols_ref, tw_ref, cas_ref, out_ref, lhs):
+def keep_kernel(table_ref, out_ref, sem):
+    copy = pltpu.make_async_copy(table_ref, out_ref, sem)
+    copy.start()
+    copy.wait()
+
+
+def shorten(tile, one, two, taps):
+    return taps[0] * tile + taps[1] * one + taps[2] * two
+
+
+def local_kernel(r_ref, cols_ref, lhs_ref):
     lane = lanes((16, 128))
+    zero = jnp.zeros((16, 128), F32)
     for h in range(2):
-        own = slice(h * 16, h * 16 + 16)
-        cols = cols_ref[own, :]
+        one, two, three = (slice(h * 16 + k * 32, h * 16 + k * 32 + 16) for k in range(3))
+        cols = cols_ref[one, :]
         tv = [column(cols, k) for k in range(3)]
         tg = [column(cols, 3 + k) for k in range(3)]
 
@@ -62,20 +86,35 @@
             rows = pl.multiple_of(i * 32, 32) + h * 16
             for t in range(8):
                 piece, at = i * 4 + t // 2, slice((t % 2) * 128, (t % 2) * 128 + 128)
-                v = r_ref[piece, own, at].astype(F32)
-                g = r_ref[piece, h * 16 + 32 : h * 16 + 48, at].astype(F32)
-                c = r_ref[piece, h * 16 + 64 : h * 16 + 80, at].astype(F32)
+                v = r_ref[piece, one, at].astype(F32)
+                g = r_ref[piece, two, at].astype(F32)
+                c = r_ref[piece, three, at].astype(F32)
                 nv1, nv2 = rolled(v)
                 ng1, ng2 = rolled(g)
-                short_v = tv[0] * v + tv[1] * back_in_time(nv1, v1, 1, lane) + tv[2] * back_in_time(nv2, v2, 2, lane)
-                short_g = tg[0] * g + tg[1] * back_in_time(ng1, g1, 1, lane) + tg[2] * back_in_time(ng2, g2, 2, lane)
-                lhs[pl.ds(rows, 16), t * 128 : t * 128 + 128] = short_v.astype(BF16)
-                lhs[pl.ds(rows + 256, 16), t * 128 : t * 128 + 128] = (c * short_g).astype(BF16)
+                short_v = shorten(v, back_in_time(nv1, v1, 1, lane), back_in_time(nv2, v2, 2, lane), tv)
+                short_g = shorten(g, back_in_time(ng1, g1, 1, lane), back_in_time(ng2, g2, 2, lane), tg)
+                lhs_ref[pl.ds(rows, 16), t * 128 : t * 128 + 128] = short_v.astype(BF16)
+                lhs_ref[pl.ds(rows + 256, 16), t * 128 : t * 128 + 128] = (c * short_g).astype(BF16)
                 v1, v2, g1, g2 = nv1, nv2, ng1, ng2
             return v1, v2, g1, g2
 
-        start = rolled(rim_ref[own, :].astype(F32)) + rolled(rim_ref[h * 16 + 32 : h * 16 + 48, :].astype(F32))
-        lax.fori_loop(0, 8, block, start)
+        lax.fori_loop(0, 8, block, (zero,) * 4)
+
+
+def spread_kernel(part_ref, r_ref, rim_ref, cols_ref, tw_ref, cas_ref, out_ref, lhs):
+    lane = lanes((16, 128))
+    lhs[...] = part_ref[...]
+    for h in range(2):
+        one, two, three = (slice(h * 16 + k * 32, h * 16 + k * 32 + 16) for k in range(3))
+        cols = cols_ref[one, :]
+        short = []
+        for k, own in enumerate((one, two)):
+            tile = r_ref[0, own, 0:128].astype(F32)
+            before = rolled(rim_ref[own, :].astype(F32))
+            shifted = [back_in_time(a, b, n + 1, lane) for n, (a, b) in enumerate(zip(rolled(tile), before))]
+            short.append(shorten(tile, *shifted, [column(cols, 3 * k + n) for n in range(3)]))
+        lhs[one, 0:128] = short[0].astype(BF16)
+        lhs[256 + h * 16 : 272 + h * 16, 0:128] = (r_ref[0, three, 0:128].astype(F32) * short[1]).astype(BF16)
 
     low = lanes((16, 128)) < 64
 
@@ -172,7 +211,7 @@
     head_ref[32:64, :] = c * (out_ref[0:32, 0:128].astype(F32) + skip * short_v)
 
 
-def final_kernel(d_ref, r_ref, rim_ref, next_ref, cols_ref, out_ref, sums_ref):
+def finish(r_ref, d_ref, rim_ref, cols_ref, stage, sums_ref, first, count, following, on_block):
     lane = lanes((16, 128))
 
     def ahead(tile):
@@ -185,8 +224,15 @@
         tg = [column(cols, 3 + k) for k in range(3)]
         skip = column(cols, 6)
 
+        def gradients(v, vb, g, gb, c, long_v, back_g):
+            short_v = shorten(v, *vb, tv).astype(BF16).astype(F32)
+            short_g = shorten(g, *gb, tg)
+            grad_long = (c * short_g).astype(BF16).astype(F32)
+            direct = long_v + skip * short_v
+            return short_v, short_g, grad_long, direct, skip * grad_long + back_g, c * direct
+
         def block(step, carry):
-            i = 7 - step
+            i = first + count - 1 - step
             (v, v1, v2), (g, g1, g2), nv, ng, acc = carry
             rows = pl.multiple_of(i * 32, 32) + h * 16
             for t in reversed(range(8)):
@@ -202,62 +248,106 @@
                     pg = jnp.where(inside, r_ref[piece_b, two, 128:256].astype(F32), rim_ref[two, :].astype(F32))
                 pv1, pv2 = rolled(pv)
                 pg1, pg2 = rolled(pg)
-                vb1, vb2 = back_in_time(v1, pv1, 1, lane), back_in_time(v2, pv2, 2, lane)
-                gb1, gb2 = back_in_time(g1, pg1, 1, lane), back_in_time(g2, pg2, 2, lane)
-                short_v = (tv[0] * v + tv[1] * vb1 + tv[2] * vb2).astype(BF16).astype(F32)
-                short_g = tg[0] * g + tg[1] * gb1 + tg[2] * gb2
+                vb = back_in_time(v1, pv1, 1, lane), back_in_time(v2, pv2, 2, lane)
+                gb = back_in_time(g1, pg1, 1, lane), back_in_time(g2, pg2, 2, lane)
                 c = r_ref[piece, three, at].astype(F32)
-                grad_long = (c * short_g).astype(BF16).astype(F32)
                 long_v = d_ref[pl.ds(rows, 16), t * 128 : t * 128 + 128].astype(F32)
                 back_g = d_ref[pl.ds(rows + 256, 16), t * 128 : t * 128 + 128].astype(F32)
-                direct = long_v + skip * short_v
-                gsg = c * direct
-                gsv = skip * grad_long + back_g
+                short_v, short_g, grad_long, direct, gsv, gsg = gradients(v, vb, g, gb, c, long_v, back_g)
                 wv, wg = ahead(gsv), ahead(gsg)
-                out_ref[piece, one, at] = (short_g * direct).astype(BF16)
-                out_ref[piece, two, at] = (
-                    tv[0] * gsv + tv[1] * jnp.where(lane > 126, nv[0], wv[0]) + tv[2] * jnp.where(lane > 125, nv[1], wv[1])
+                put = piece - first * 4
+                stage[put, one, at] = (short_g * direct).astype(BF16)
+                stage[put, two, at] = shorten(
+                    gsv, jnp.where(lane > 126, nv[0], wv[0]), jnp.where(lane > 125, nv[1], wv[1]), tv
                 ).astype(BF16)
-                out_ref[piece, three, at] = (
-                    tg[0] * gsg + tg[1] * jnp.where(lane > 126, ng[0], wg[0]) + tg[2] * jnp.where(lane > 125, ng[1], wg[1])
+                stage[put, three, at] = shorten(
+                    gsg, jnp.where(lane > 126, ng[0], wg[0]), jnp.where(lane > 125, ng[1], wg[1]), tg
                 ).astype(BF16)
-                terms = (gsv * v, gsv * vb1, gsv * vb2, gsg * g, gsg * gb1, gsg * gb2, grad_long * short_v)
+                terms = (gsv * v, gsv * vb[0], gsv * vb[1], gsg * g, gsg * gb[0], gsg * gb[1], grad_long * short_v)
                 acc = tuple(a + b for a, b in zip(acc, terms))
                 v, v1, v2, g, g1, g2, nv, ng = pv, pv1, pv2, pg, pg1, pg2, wv, wg
+            if h == 1:
+                on_block(i - first)
             return (v, v1, v2), (g, g1, g2), nv, ng, acc
 
-        last_v = r_ref[31, one, 128:256].astype(F32)
-        last_g = r_ref[31, two, 128:256].astype(F32)
+        end = first * 4 + count * 4 - 1
+        last_v = r_ref[end, one, 128:256].astype(F32)
+        last_g = r_ref[end, two, 128:256].astype(F32)
+        last_v = last_v, *rolled(last_v)
+        last_g = last_g, *rolled(last_g)
+        if following is None:
+            rows = (first + count) * 32 + h * 16
+            next_v, next_g, c = (r_ref[end + 1, own, 0:128].astype(F32) for own in (one, two, three))
+            vb = [back_in_time(a, b, n + 1, lane) for n, (a, b) in enumerate(zip(rolled(next_v), last_v[1:]))]
+            gb = [back_in_time(a, b, n + 1, lane) for n, (a, b) in enumerate(zip(rolled(next_g), last_g[1:]))]
+            long_v = d_ref[rows : rows + 16, 0:128].astype(F32)
+            back_g = d_ref[rows + 256 : rows + 272, 0:128].astype(F32)
+            gsv, gsg = gradients(next_v, vb, next_g, gb, c, long_v, back_g)[4:]
+        else:
+            gsv, gsg = following[one, :], following[two, :]
         zero = jnp.zeros((16, 128), F32)
-        start = (
-            (last_v, *rolled(last_v)),
-            (last_g, *rolled(last_g)),
-            ahead(next_ref[one, :]),
-            ahead(next_ref[two, :]),
-            (zero,) * 7,
-        )
-        acc = lax.fori_loop(0, 8, block, start)[4]
+        start = last_v, last_g, ahead(gsv), ahead(gsg), (zero,) * 7
+        acc = lax.fori_loop(0, count, block, start)[4]
         total = zero
         for k in range(7):
             total = jnp.where(lane == k, jnp.sum(acc[k], axis=1, keepdims=True), total)
         sums_ref[one, :] = total
 
 
-def call(kernel, outs, scratch, flops, moved, *args):
-    vmem = pl.BlockSpec(memory_space=pltpu.VMEM)
+def most_kernel(d_ref, r_ref, rim_ref, cols_ref, out_ref, sums_ref, stage, sems):
+    def leave(i):
+        own = pl.ds(i * 4, 4)
+        return pltpu.make_async_copy(stage.at[own], out_ref.at[own], sems.at[i])
+
+    def on_block(i):
+        leave(i).start()
+
+    finish(r_ref, d_ref, rim_ref, cols_ref, stage, sums_ref, 0, 7, None, on_block)
+    for i in range(7):
+        leave(i).wait()
+
+
+def last_kernel(most_ref, d_ref, r_ref, rim_ref, next_ref, cols_ref, some_ref, out_ref, sums_ref, stage, sem):
+    finish(r_ref, d_ref, rim_ref, cols_ref, stage, sums_ref, 7, 1, next_ref, lambda i: None)
+    copy = pltpu.make_async_copy(stage, out_ref.at[28:32], sem)
+    copy.start()
+    sums_ref[...] = sums_ref[...] + some_ref[...]
+    copy.wait()
+
+
+VMEM = pl.BlockSpec(memory_space=pltpu.VMEM)
+ANY = pl.BlockSpec(memory_space=pl.ANY)
+
+
+def call(kernel, outs, scratch, flops, moved, *args, **more):
     return pl.pallas_call(
         kernel,
-        in_specs=[vmem] * len(args),
-        out_specs=[vmem] * len(outs),
+        **{"in_specs": [VMEM] * len(args), "out_specs": [VMEM] * len(outs), **more},
         compiler_params=pltpu.CompilerParams(vmem_limit_bytes=GRANT),
         out_shape=[jax.ShapeDtypeStruct(s, d) for s, d in outs],
-        scratch_shapes=[pltpu.VMEM(s, d) for s, d in scratch],
+        scratch_shapes=[s if d is None else pltpu.VMEM(s, d) for s, d in scratch],
         cost_estimate=pl.CostEstimate(flops=flops, bytes_accessed=moved, transcendentals=0),
     )(*args)
 
 
-def spread(r, rim, cols, twiddle, cas):
-    return call(spread_kernel, [((16, 256, 128), BF16)], [((512, 1024), BF16)], 1 << 30, 5 << 20, r, rim, cols, twiddle, cas)[0]
+def local(r, cols):
+    return call(local_kernel, [((512, 1024), BF16)], [], 1 << 24, 4 << 20, r, cols)[0]
+
+
+def spread(part, r, rim, cols, twiddle, cas):
+    return call(
+        spread_kernel,
+        [((16, 256, 128), BF16)],
+        [((512, 1024), BF16)],
+        1 << 30,
+        5 << 20,
+        part,
+        r,
+        rim,
+        cols,
+        twiddle,
+        cas,
+    )[0]
 
 
 def mix(by_freq, spectrum, mixing):
@@ -289,21 +379,65 @@
     )
 
 
-def final(d, r, rim, following, cols):
+def most(d, r, rim, cols):
     return call(
-        final_kernel, [((32, 96, 256), BF16), ((32, 128), F32)], [], 1 << 24, 5 << 20, d, r, rim, following, cols
+        most_kernel,
+        [((32, 96, 256), BF16), ((32, 128), F32)],
+        [((28, 96, 256), BF16), (pltpu.SemaphoreType.DMA((7,)), None)],
+        1 << 25,
+        8 << 20,
+        d,
+        r,
+        rim,
+        cols,
+        out_specs=[ANY, VMEM],
+    )
+
+
+def last(done, d, r, rim, following, cols, sums):
+    return call(
+        last_kernel,
+        [((32, 96, 256), BF16), ((32, 128), F32)],
+        [((4, 96, 256), BF16), (pltpu.SemaphoreType.DMA(()), None)],
+        1 << 22,
+        1 << 20,
+        done,
+        d,
+        r,
+        rim,
+        following,
+        cols,
+        sums,
+        in_specs=[ANY] + [VMEM] * 6,
+        out_specs=[ANY, VMEM],
+        input_output_aliases={0: 0},
     )
 
 
 def gather(*fields):
     return pl.pallas_call(
         gather_kernel,
-        in_specs=[pl.BlockSpec(memory_space=pltpu.HBM)] * 3,
+        in_specs=[pl.BlockSpec(memory_space=pl.ANY)] * 3,
+        out_specs=pl.BlockSpec(memory_space=pl.ANY),
+        out_shape=jax.ShapeDtypeStruct((32, 96, 256), BF16),
+        scratch_shapes=[
+            pltpu.VMEM((32, 96, 256), BF16),
+            pltpu.SemaphoreType.DMA((PARTS, 3)),
+            pltpu.SemaphoreType.DMA((PARTS,)),
+        ],
+    )(*fields)
+
+
+def keep(table):
+    return pl.pallas_call(
+        keep_kernel,
+        in_specs=[pl.BlockSpec(memory_space=pl.ANY)],
         out_specs=pl.BlockSpec(memory_space=pltpu.VMEM),
-        out_shape=jax.ShapeDtypeStruct((32, 96, 256), BF16),
-        scratch_shapes=[pltpu.SemaphoreType.DMA((3,))],
+        out_shape=jax.ShapeDtypeStruct(table.shape, table.dtype),
+        scratch_shapes=[pltpu.SemaphoreType.DMA(())],
         compiler_params=pltpu.CompilerParams(vmem_limit_bytes=GRANT),
-    )(*fields)
+        cost_estimate=pl.CostEstimate(flops=0, bytes_accessed=4 << 20, transcendentals=0),
+    )(table)
 
 
 def exchange(array, axis):
@@ -312,18 +446,19 @@
 
 def per_device(values, gates, cotangent, taps_values, taps_gates, skip_gain, twiddle, mixing, spectrum):
     batch = lax.axis_size("batch")
-    cas = jnp.asarray(cas_table())
     raw = gather(*(x.reshape(32, 32, 256) for x in (values, gates, cotangent)))
     r = exchange(raw, "seq")
+    cas = keep(jnp.asarray(cas_table()))
     gains = jnp.concatenate([taps_values, taps_gates, skip_gain[None]], axis=0)
     cols = lax.dynamic_slice(gains, (0, lax.axis_index("seq") * 32), (7, 32))
     cols = jnp.pad(cols.T, ((0, 0), (0, 121)))
     rim = lax.ppermute(r[31, :64, 128:], "batch", [(i, i + 1) for i in range(batch - 1)])
-    by_freq = exchange(spread(r, rim, cols, twiddle, cas), "batch")
+    by_freq = exchange(spread(local(r, cols), r, rim, cols, twiddle, cas), "batch")
     grad_spectrum, weighted = mix(by_freq, spectrum.transpose(0, 2, 1), mixing)
     d, head = back(exchange(weighted, "batch"), r, rim, cols, twiddle, cas)
     following = lax.ppermute(head, "batch", [(i + 1, i) for i in range(batch - 1)])
-    done, sums = final(d, r, rim, following, cols)
+    done, sums = most(d, r, rim, cols)
+    done, sums = last(done, d, r, rim, following, cols, sums)
     outs = exchange(done, "seq")
     step = 1
     while step < batch:

time: 200 us -> 193 us (0.965)
  waiting for transfers between devices: 66.4 us -> 60.5 us
  blocking collectives: 69.1 us -> 65.9 us
  local copies, waits for them, and re-layouts: 8.1 us -> 4.98 us
  Pallas kernels: 17 us -> 19.3 us
  starting transfers between devices: 38.1 us -> 40.3 us
    ppermute x1, waiting for transfers between devices: 3.31 us -> 0.01 us  [per_device(): lax.ppermute(head, 'batch', [(i + 1, i) for i in range(batch - 1)])]
    all_to_all x2, blocking collectives: 69.1 us -> 65.9 us  [exchange(): return lax.all_to_all(array, axis, 0, 0, tiled=True)]
    unnamed x25 -> x17, local copies, waits for them, and re-layouts: 6.15 us -> 3.03 us
    pallas_call x5 -> x8, Pallas kernels: 17 us -> 19.3 us  [the longest x6 16.8 us: call(): pl.pallas_call(kernel, **{'in_specs': [VMEM] * len(args), 'out_specs': [V...]
    ppermute x4, starting transfers between devices: 10.5 us -> 12.7 us  [per_device(): lax.ppermute(sums, 'batch', [(i, i ^ step) for i in range(batch)])]
  transfers between devices with their start and end apart: 8 -> 8, of which waited for: 8 -> 6; matrix products, arithmetic and copies ran while one was open for 1% -> 1% of each run, Pallas kernels for 0% -> 4%
where the time goes in v3:
time: 193 us; the launch traced here: 192 us
  blocking collectives  65.9 us (34%)
  waiting for transfers between devices  60.5 us (31%)
  starting transfers between devices  40.3 us (21%)
  Pallas kernels  19.3 us (10%)
  local copies, waits for them, and re-layouts  4.98 us (3%)
    all_to_all x2, blocking collectives, exchange(): return lax.all_to_all(array, axis, 0, 0, tiled=True)  65.9 us
    all_to_all x2, waiting for transfers between devices, exchange(): return lax.all_to_all(array, axis, 0, 0, tiled=True)  50.8 us
    all_to_all x2, starting transfers between devices, exchange(): return lax.all_to_all(array, axis, 0, 0, tiled=True)  19.2 us
    pallas_call x6, Pallas kernels, call(): pl.pallas_call(kernel, **{'in_specs': [VMEM] * len(args), 'out_specs': [V...  16.8 us
    ppermute x4, starting transfers between devices, per_device(): lax.ppermute(sums, 'batch', [(i, i ^ step) for i in range(batch)])  12.7 us
    ppermute x4, waiting for transfers between devices, per_device(): lax.ppermute(sums, 'batch', [(i, i ^ step) for i in range(batch)])  9.78 us
    ppermute x1, starting transfers between devices, per_device(): lax.ppermute(r[31, :64, 128:], 'batch', [(i, i + 1) for i in range(batch...  6.46 us
  transfers between devices with their start and end apart: 8, of which 6 were waited for; matrix products, arithmetic and copies ran while one was open for 1% of the time, Pallas kernels for 4%

profile of v3, /device:TPU:1, one launch (start us, length us, event | category | flops | bytes accessed | tf_op | source)
XLA Modules:
  0.0 192.0 jit_solution(11849449145598584752)
XLA Ops:
  0.6 2.4 %shard_map.153 = bf16[32,96,256]{2,1,0:T(8,128)(2,1)} custom-call(bf16[32,32,256]{2,1,0:T(8,128)(2,1)} %bitcast.15, bf16[32,32,256]{2,1,0:T(8,128)(2,1)} %bitcast.16, bf16[32,32,256]{2,1,0:T(8,128)(2,1)} %bitcast.17), custom_call_target="tpu_custom_call" | custom-call | tf_op jit(solution)/shard_map/pallas_call | solution.py:418
  3.1 13.8 %all-to-all-start = ((bf16[32,96,256]{2,1,0:T(8,128)(2,1)}), bf16[32,96,256]{2,1,0:T(8,128)(2,1)S(1)}, u32[]{:S(2)}, u32[]{:S(2)}) async-start(bf16[32,96,256]{2,1,0:T(8,128)(2,1)} %shard_map.153), calls=%async_computation | async-start | bytes 3145728 | tf_op jit(solution)/shard_map/all_to_all | solution.py:444
  16.9 36.9 %all-to-all-done.r_ref = bf16[32,96,256]{2,1,0:T(8,128)(2,1)S(1)} async-done(((bf16[32,96,256]{2,1,0:T(8,128)(2,1)}), bf16[32,96,256]{2,1,0:T(8,128)(2,1)S(1)}, u32[]{:S(2)}, u32[]{:S(2)}) %all-to-all-start) | async-done | bytes 1572896 | tf_op jit(solution)/shard_map/all_to_all | solution.py:444
  53.8 6.5 %collective-permute-start = (bf16[64,128]{1,0:T(8,128)(2,1)S(1)}, bf16[64,128]{1,0:T(8,128)(2,1)S(1)}, u32[]{:S(2)}, u32[]{:S(2)}) collective-permute-start(bf16[64,128]{1,0:T(8,128)(2,1)S(1)} %slice_bitcast_fusion), channel_id=1, source_target_pairs={{0,32},{32,64},{64,96},{96,128},{128,160},{160,192},{192,224},{224... | collective-permute-start | bytes 49160 | tf_op jit(solution)/shard_map/ppermute | solution.py:455
  60.5 1.6 copy-done
  62.3 2.1 %shard_map.154.part_ref = bf16[512,1024]{1,0:T(8,128)(2,1)S(1)} custom-call(bf16[32,96,256]{2,1,0:T(8,128)(2,1)S(1)} %all-to-all-done.r_ref, f32[32,128]{1,0:T(8,128)S(1)} %pad.4.cols_ref), custom_call_target="tpu_custom_call" | custom-call | flops 16777216 | bytes 4194304 | tf_op jit(solution)/shard_map/pallas_call | solution.py:323
  64.4 2.2 %shard_map.156 = bf16[16,256,128]{2,1,0:T(8,128)(2,1)S(1)} custom-call(bf16[512,1024]{1,0:T(8,128)(2,1)S(1)} %shard_map.154.part_ref, bf16[32,96,256]{2,1,0:T(8,128)(2,1)S(1)} %all-to-all-done.r_ref, bf16[64,128]{1,0:T(8,128)(2,1)S(1)} %collective-permute-done.rim_ref, f32[32,128]{1,0:T(8,128)S(1)} %pad.4.cols_ref, f32[8,1024]{1,0:T(8,128)S(1)} %copy-done.1, ...), custom_call_target="tpu_custom_call" | custom-call | flops 1073741824 | bytes 5242880 | tf_op jit(solution)/shard_map/pallas_call | solution.py:323
  66.6 34.7 %all_to_all.20.f_ref = bf16[16,256,128]{2,1,0:T(8,128)(2,1)S(1)} all-to-all(bf16[16,256,128]{2,1,0:T(8,128)(2,1)S(1)} %shard_map.156), channel_id=1, replica_groups=mesh['batch'=16,'seq'=32] {'batch'}, dimensions={0} | all-to-all | bytes 2097152 | tf_op jit(solution)/shard_map/all_to_all | solution.py:444
  101.3 2.9 %shard_map.157 = (f32[32,64,128]{2,1,0:T(8,128)}, bf16[16,256,128]{2,1,0:T(8,128)(2,1)S(1)}) custom-call(bf16[16,256,128]{2,1,0:T(8,128)(2,1)S(1)} %all_to_all.20.f_ref, bf16[32,64,128]{2,1,0:T(8,128)(2,1)S(1)} %bitcast.14, f32[128,128]{1,0:T(8,128)S(1)} %copy-done.3), custom_call_target="tpu_custom_call" | custom-call | flops 1073741824 | bytes 5242880 | tf_op jit(solution)/shard_map/pallas_call | solution.py:323
  104.3 31.2 %all_to_all.21.y_ref = bf16[16,256,128]{2,1,0:T(8,128)(2,1)S(1)} all-to-all(bf16[16,256,128]{2,1,0:T(8,128)(2,1)S(1)} %get-tuple-element.15), channel_id=1, replica_groups=mesh['batch'=16,'seq'=32] {'batch'}, dimensions={0} | all-to-all | bytes 2097152 | tf_op jit(solution)/shard_map/all_to_all | solution.py:444
  135.5 2.9 %shard_map.158 = (bf16[512,1024]{1,0:T(8,128)(2,1)S(1)}, f32[64,128]{1,0:T(8,128)S(1)}) custom-call(bf16[16,256,128]{2,1,0:T(8,128)(2,1)S(1)} %all_to_all.21.y_ref, bf16[32,96,256]{2,1,0:T(8,128)(2,1)S(1)} %all-to-all-done.r_ref, bf16[64,128]{1,0:T(8,128)(2,1)S(1)} %collective-permute-done.rim_ref, f32[32,128]{1,0:T(8,128)S(1)} %pad.4.cols_ref, ...), custom_call_target="tpu_custom_call" | custom-call | flops 1073741824 | bytes 5242880 | tf_op jit(solution)/shard_map/pallas_call | solution.py:323
  138.4 1.9 %collective-permute-start.1 = (f32[64,128]{1,0:T(8,128)S(1)}, f32[64,128]{1,0:T(8,128)S(1)}, u32[]{:S(2)}, u32[]{:S(2)}) collective-permute-start(f32[64,128]{1,0:T(8,128)S(1)} %get-tuple-element.18), channel_id=1, source_target_pairs={{32,0},{64,32},{96,64},{128,96},{160,128},{192,160},{224,192},{256... | collective-permute-start | bytes 98312 | tf_op jit(solution)/shard_map/ppermute | solution.py:459
  140.3 4.8 %shard_map.159 = (bf16[32,96,256]{2,1,0:T(8,128)(2,1)}, f32[32,128]{1,0:T(8,128)S(1)}) custom-call(bf16[512,1024]{1,0:T(8,128)(2,1)S(1)} %get-tuple-element.16.d_ref, bf16[32,96,256]{2,1,0:T(8,128)(2,1)S(1)} %all-to-all-done.r_ref, bf16[64,128]{1,0:T(8,128)(2,1)S(1)} %collective-permute-done.rim_ref, f32[32,128]{1,0:T(8,128)S(1)} %pad.4.cols_ref), custom_call_target="tpu_custom_call" | custom-call | flops 33554432 | bytes 8388608 | tf_op jit(solution)/shard_map/pallas_call | solution.py:323
  145.1 1.9 shard_map.160
  147.0 5.3 %all-to-all-start.3 = ((bf16[32,96,256]{2,1,0:T(8,128)(2,1)}), bf16[32,96,256]{2,1,0:T(8,128)(2,1)S(1)}, u32[]{:S(2)}, u32[]{:S(2)}) async-start(bf16[32,96,256]{2,1,0:T(8,128)(2,1)} %get-tuple-element.20), calls=%async_computation.3 | async-start | bytes 3145728 | tf_op jit(solution)/shard_map/all_to_all | solution.py:444
  152.3 1.9 %collective-permute-start.2 = (f32[32,128]{1,0:T(8,128)S(1)}, f32[32,128]{1,0:T(8,128)S(1)}, u32[]{:S(2)}, u32[]{:S(2)}) collective-permute-start(f32[32,128]{1,0:T(8,128)S(1)} %get-tuple-element.22), channel_id=1, source_target_pairs={{0,32},{32,0},{64,96},{96,64},{128,160},{160,128},{192,224},{224,1... | collective-permute-start | bytes 49160 | tf_op jit(solution)/shard_map/ppermute | solution.py:465
  155.4 3.7 %collective-permute-start.3 = (f32[32,128]{1,0:T(8,128)S(1)}, f32[32,128]{1,0:T(8,128)S(1)}, u32[]{:S(2)}, u32[]{:S(2)}) collective-permute-start(f32[32,128]{1,0:T(8,128)S(1)} %add.18), channel_id=1, source_target_pairs={{0,64},{32,96},{64,0},{96,32},{128,192},{160,224},{192,128},{224,1... | collective-permute-start | bytes 49160 | tf_op jit(solution)/shard_map/ppermute | solution.py:465
  159.1 1.4 collective-permute-done.3
  160.5 1.9 collective-permute-start.4
  162.4 3.7 %collective-permute-done.4 = f32[32,128]{1,0:T(8,128)S(1)} collective-permute-done((f32[32,128]{1,0:T(8,128)S(1)}, f32[32,128]{1,0:T(8,128)S(1)}, u32[]{:S(2)}, u32[]{:S(2)}) %collective-permute-start.4) | collective-permute-done | bytes 16416 | tf_op jit(solution)/shard_map/ppermute | solution.py:465
  166.2 5.2 %collective-permute-start.5 = (f32[32,128]{1,0:T(8,128)S(1)}, f32[32,128]{1,0:T(8,128)S(1)}, u32[]{:S(2)}, u32[]{:S(2)}) collective-permute-start(f32[32,128]{1,0:T(8,128)S(1)} %add.20), channel_id=1, source_target_pairs={{0,256},{32,288},{64,320},{96,352},{128,384},{160,416},{192,448},{... | collective-permute-start | bytes 49160 | tf_op jit(solution)/shard_map/ppermute | solution.py:465
  171.4 3.5 %collective-permute-done.5 = f32[32,128]{1,0:T(8,128)S(1)} collective-permute-done((f32[32,128]{1,0:T(8,128)S(1)}, f32[32,128]{1,0:T(8,128)S(1)}, u32[]{:S(2)}, u32[]{:S(2)}) %collective-permute-start.5) | collective-permute-done | bytes 16416 | tf_op jit(solution)/shard_map/ppermute | solution.py:465
  177.0 13.9 %all-to-all-done.3 = bf16[32,96,256]{2,1,0:T(8,128)(2,1)S(1)} async-done(((bf16[32,96,256]{2,1,0:T(8,128)(2,1)}), bf16[32,96,256]{2,1,0:T(8,128)(2,1)S(1)}, u32[]{:S(2)}, u32[]{:S(2)}) %all-to-all-start.3) | async-done | bytes 1572896 | tf_op jit(solution)/shard_map/all_to_all | solution.py:444
  190.8 1.2 fusion.3
  (29 shorter events, 3.6 us)
Async XLA Ops:
  3.0 57.3 %copy-start.4 = (f32[3,1024]{1,0:T(4,128)S(1)}, f32[3,1024]{1,0:T(4,128)}, u32[]{:S(2)}) copy-start(f32[3,1024]{1,0:T(4,128)} %param.13) | copy-start | bytes 36868
  3.0 57.3 %copy-start.5 = (f32[3,1024]{1,0:T(4,128)S(1)}, f32[3,1024]{1,0:T(4,128)}, u32[]{:S(2)}) copy-start(f32[3,1024]{1,0:T(4,128)} %param.14) | copy-start | bytes 36868
  3.0 57.3 %copy-start.6 = (f32[1024]{0:T(1024)S(1)}, f32[1024]{0:T(1024)}, u32[]{:S(2)}) copy-start(f32[1024]{0:T(1024)} %param.15) | copy-start | bytes 12292
  3.1 50.8 %all-to-all-start = ((bf16[32,96,256]{2,1,0:T(8,128)(2,1)}), bf16[32,96,256]{2,1,0:T(8,128)(2,1)S(1)}, u32[]{:S(2)}, u32[]{:S(2)}) async-start(bf16[32,96,256]{2,1,0:T(8,128)(2,1)} %shard_map.153), calls=%async_computation | async-start | bytes 3145728 | tf_op jit(solution)/shard_map/all_to_all | solution.py:444
  53.8 10.5 %collective-permute-start = (bf16[64,128]{1,0:T(8,128)(2,1)S(1)}, bf16[64,128]{1,0:T(8,128)(2,1)S(1)}, u32[]{:S(2)}, u32[]{:S(2)}) collective-permute-start(bf16[64,128]{1,0:T(8,128)(2,1)S(1)} %slice_bitcast_fusion), channel_id=1, source_target_pairs={{0,32},{32,64},{64,96},{96,128},{128,160},{160,192},{192,224},{224... | collective-permute-start | bytes 49160 | tf_op jit(solution)/shard_map/ppermute | solution.py:455
  60.5 1.6 copy-start
  62.2 2.1 %copy-start.1 = (f32[8,1024]{1,0:T(8,128)S(1)}, f32[8,1024]{1,0:T(8,128)}, u32[]{:S(2)}) copy-start(f32[8,1024]{1,0:T(8,128)} %tw_ref.3) | copy-start | bytes 98308
  66.6 34.7 %copy-start.2 = (bf16[32,128,64]{1,2,0:T(8,128)(2,1)S(1)}, bf16[32,128,64]{1,2,0:T(8,128)(2,1)}, u32[]{:S(2)}) copy-start(bf16[32,128,64]{1,2,0:T(8,128)(2,1)} %param.18) | copy-start | bytes 1572868
  66.6 34.7 %copy-start.3 = (f32[128,128]{1,0:T(8,128)S(1)}, f32[128,128]{1,0:T(8,128)}, u32[]{:S(2)}) copy-start(f32[128,128]{1,0:T(8,128)} %mix_ref.1) | copy-start | bytes 196612
  138.4 6.8 %collective-permute-start.1 = (f32[64,128]{1,0:T(8,128)S(1)}, f32[64,128]{1,0:T(8,128)S(1)}, u32[]{:S(2)}, u32[]{:S(2)}) collective-permute-start(f32[64,128]{1,0:T(8,128)S(1)} %get-tuple-element.18), channel_id=1, source_target_pairs={{32,0},{64,32},{96,64},{128,96},{160,128},{192,160},{224,192},{256... | collective-permute-start | bytes 98312 | tf_op jit(solution)/shard_map/ppermute | solution.py:459
  147.0 43.8 %all-to-all-start.3 = ((bf16[32,96,256]{2,1,0:T(8,128)(2,1)}), bf16[32,96,256]{2,1,0:T(8,128)(2,1)S(1)}, u32[]{:S(2)}, u32[]{:S(2)}) async-start(bf16[32,96,256]{2,1,0:T(8,128)(2,1)} %get-tuple-element.20), calls=%async_computation.3 | async-start | bytes 3145728 | tf_op jit(solution)/shard_map/all_to_all | solution.py:444
  152.3 3.1 %collective-permute-start.2 = (f32[32,128]{1,0:T(8,128)S(1)}, f32[32,128]{1,0:T(8,128)S(1)}, u32[]{:S(2)}, u32[]{:S(2)}) collective-permute-start(f32[32,128]{1,0:T(8,128)S(1)} %get-tuple-element.22), channel_id=1, source_target_pairs={{0,32},{32,0},{64,96},{96,64},{128,160},{160,128},{192,224},{224,1... | collective-permute-start | bytes 49160 | tf_op jit(solution)/shard_map/ppermute | solution.py:465
  155.4 5.1 %collective-permute-start.3 = (f32[32,128]{1,0:T(8,128)S(1)}, f32[32,128]{1,0:T(8,128)S(1)}, u32[]{:S(2)}, u32[]{:S(2)}) collective-permute-start(f32[32,128]{1,0:T(8,128)S(1)} %add.18), channel_id=1, source_target_pairs={{0,64},{32,96},{64,0},{96,32},{128,192},{160,224},{192,128},{224,1... | collective-permute-start | bytes 49160 | tf_op jit(solution)/shard_map/ppermute | solution.py:465
  160.5 5.7 %collective-permute-start.4 = (f32[32,128]{1,0:T(8,128)S(1)}, f32[32,128]{1,0:T(8,128)S(1)}, u32[]{:S(2)}, u32[]{:S(2)}) collective-permute-start(f32[32,128]{1,0:T(8,128)S(1)} %add.19), channel_id=1, source_target_pairs={{0,128},{32,160},{64,192},{96,224},{128,0},{160,32},{192,64},{224,... | collective-permute-start | bytes 49160 | tf_op jit(solution)/shard_map/ppermute | solution.py:465
  166.2 8.7 %collective-permute-start.5 = (f32[32,128]{1,0:T(8,128)S(1)}, f32[32,128]{1,0:T(8,128)S(1)}, u32[]{:S(2)}, u32[]{:S(2)}) collective-permute-start(f32[32,128]{1,0:T(8,128)S(1)} %add.20), channel_id=1, source_target_pairs={{0,256},{32,288},{64,320},{96,352},{128,384},{160,416},{192,448},{... | collective-permute-start | bytes 49160 | tf_op jit(solution)/shard_map/ppermute | solution.py:465

commit v4 on v3

--- a/solution.py
+++ b/solution.py
@@ -211,7 +211,7 @@
     head_ref[32:64, :] = c * (out_ref[0:32, 0:128].astype(F32) + skip * short_v)
 
 
-def finish(r_ref, d_ref, rim_ref, cols_ref, stage, sums_ref, first, count, following, on_block):
+def finish(r_ref, d_ref, rim_ref, cols_ref, stage, heads, sums_ref, first, count, following, on_block):
     lane = lanes((16, 128))
 
     def ahead(tile):
@@ -233,7 +233,7 @@
 
         def block(step, carry):
             i = first + count - 1 - step
-            (v, v1, v2), (g, g1, g2), nv, ng, acc = carry
+            (v, v1, v2), (g, g1, g2), nv, acc = carry
             rows = pl.multiple_of(i * 32, 32) + h * 16
             for t in reversed(range(8)):
                 piece, at = i * 4 + t // 2, slice((t % 2) * 128, (t % 2) * 128 + 128)
@@ -253,22 +253,21 @@
                 c = r_ref[piece, three, at].astype(F32)
                 long_v = d_ref[pl.ds(rows, 16), t * 128 : t * 128 + 128].astype(F32)
                 back_g = d_ref[pl.ds(rows + 256, 16), t * 128 : t * 128 + 128].astype(F32)
-                short_v, short_g, grad_long, direct, gsv, gsg = gradients(v, vb, g, gb, c, long_v, back_g)
-                wv, wg = ahead(gsv), ahead(gsg)
+                short_v, _, grad_long, direct, gsv, gsg = gradients(v, vb, g, gb, c, long_v, back_g)
+                wv = ahead(gsv)
                 put = piece - first * 4
-                stage[put, one, at] = (short_g * direct).astype(BF16)
+                stage[put, one, at] = direct.astype(BF16)
                 stage[put, two, at] = shorten(
                     gsv, jnp.where(lane > 126, nv[0], wv[0]), jnp.where(lane > 125, nv[1], wv[1]), tv
                 ).astype(BF16)
-                stage[put, three, at] = shorten(
-                    gsg, jnp.where(lane > 126, ng[0], wg[0]), jnp.where(lane > 125, ng[1], wg[1]), tg
-                ).astype(BF16)
+                if t % 2 == 0:
+                    heads[pl.ds(pl.multiple_of(put * 32, 32) + h * 16, 16), :] = gsg.astype(BF16)
                 terms = (gsv * v, gsv * vb[0], gsv * vb[1], gsg * g, gsg * gb[0], gsg * gb[1], grad_long * short_v)
                 acc = tuple(a + b for a, b in zip(acc, terms))
-                v, v1, v2, g, g1, g2, nv, ng = pv, pv1, pv2, pg, pg1, pg2, wv, wg
+                v, v1, v2, g, g1, g2, nv = pv, pv1, pv2, pg, pg1, pg2, wv
             if h == 1:
                 on_block(i - first)
-            return (v, v1, v2), (g, g1, g2), nv, ng, acc
+            return (v, v1, v2), (g, g1, g2), nv, acc
 
         end = first * 4 + count * 4 - 1
         last_v = r_ref[end, one, 128:256].astype(F32)
@@ -282,37 +281,119 @@
             gb = [back_in_time(a, b, n + 1, lane) for n, (a, b) in enumerate(zip(rolled(next_g), last_g[1:]))]
             long_v = d_ref[rows : rows + 16, 0:128].astype(F32)
             back_g = d_ref[rows + 256 : rows + 272, 0:128].astype(F32)
-            gsv, gsg = gradients(next_v, vb, next_g, gb, c, long_v, back_g)[4:]
+            gsv = gradients(next_v, vb, next_g, gb, c, long_v, back_g)[4]
         else:
-            gsv, gsg = following[one, :], following[two, :]
+            gsv = following[one, :]
         zero = jnp.zeros((16, 128), F32)
-        start = last_v, last_g, ahead(gsv), ahead(gsg), (zero,) * 7
-        acc = lax.fori_loop(0, count, block, start)[4]
+        start = last_v, last_g, ahead(gsv), (zero,) * 7
+        acc = lax.fori_loop(0, count, block, start)[3]
         total = zero
         for k in range(7):
             total = jnp.where(lane == k, jnp.sum(acc[k], axis=1, keepdims=True), total)
         sums_ref[one, :] = total
 
 
-def most_kernel(d_ref, r_ref, rim_ref, cols_ref, out_ref, sums_ref, stage, sems):
+def most_kernel(d_ref, r_ref, rim_ref, cols_ref, out_ref, sums_ref, heads_ref, stage, sems):
     def leave(i):
         own = pl.ds(i * 4, 4)
-        return pltpu.make_async_copy(stage.at[own], out_ref.at[own], sems.at[i])
+        return pltpu.make_async_copy(stage.at[own], out_ref.at[own, 0:64, :], sems.at[i])
 
     def on_block(i):
         leave(i).start()
 
-    finish(r_ref, d_ref, rim_ref, cols_ref, stage, sums_ref, 0, 7, None, on_block)
+    finish(r_ref, d_ref, rim_ref, cols_ref, stage, heads_ref, sums_ref, 0, 7, None, on_block)
     for i in range(7):
         leave(i).wait()
 
 
-def last_kernel(most_ref, d_ref, r_ref, rim_ref, next_ref, cols_ref, some_ref, out_ref, sums_ref, stage, sem):
-    finish(r_ref, d_ref, rim_ref, cols_ref, stage, sums_ref, 7, 1, next_ref, lambda i: None)
-    copy = pltpu.make_async_copy(stage, out_ref.at[28:32], sem)
-    copy.start()
+def last_kernel(
+    most_ref, d_ref, r_ref, rim_ref, next_ref, cols_ref, some_ref, heads_ref, out_ref, sums_ref, stage, edges, held, sems
+):
+    finish(r_ref, d_ref, rim_ref, cols_ref, stage, held, sums_ref, 7, 1, next_ref, lambda i: None)
+    copies = [
+        pltpu.make_async_copy(stage, out_ref.at[28:32, 0:64, :], sems.at[0]),
+        pltpu.make_async_copy(edges, out_ref.at[:, 64:72, :], sems.at[1]),
+    ]
+    copies[0].start()
     sums_ref[...] = sums_ref[...] + some_ref[...]
-    copy.wait()
+    held[128:160, :] = next_ref[32:64, :].astype(BF16)
+    line = lax.broadcasted_iota(jnp.int32, (8, 128), 0)
+    lane = lanes((8, 128))
+    after = ((line < 2) & (lane == line)).astype(F32).astype(BF16)
+    before = ((line > 1) & (line < 4) & (lane == line + 124)).astype(F32).astype(BF16)
+    dims = (((1,), (1,)), ((), ()))
+    edges[:, :, 128:256] = jnp.zeros((32, 8, 128), BF16)
+    for j in range(8):
+        if j < 6:
+            ahead = heads_ref[j * 128 + 32 : j * 128 + 160, :]
+        elif j == 6:
+            ahead = jnp.concatenate([heads_ref[800:896, :], held[0:32, :]], axis=0)
+        else:
+            ahead = held[32:160, :]
+        pieces = [r_ref[p, 32:64, 128:256] if p >= 0 else rim_ref[32:64, :] for p in range(4 * j - 1, 4 * j + 3)]
+        rows = lax.dot_general(after, ahead, dims, preferred_element_type=F32)
+        rows += lax.dot_general(before, jnp.concatenate(pieces, axis=0), dims, preferred_element_type=F32)
+        for p in range(4 * j, 4 * j + 4):
+            edges[p, :, 0:128] = rows.astype(BF16)
+    copies[1].start()
+    for copy in copies:
+        copy.wait()
+
+
+def home_kernel(
+    u_ref, g_ref, c_ref, cols_ref, sel_ref, mixed_ref, gv_ref, gg_ref, stage_m, stage_g, turned, sems
+):
+    direct = pltpu.make_async_copy(u_ref.at[:, 32:64, :], gv_ref, sems.at[0, 2])
+    direct.start()
+    lane = lanes((16, 128))
+    for j in range(2):
+        edge = u_ref[j * 16 : j * 16 + 16, 64:72, 0:128].astype(F32).reshape(128, 128).astype(BF16)
+        turned[j] = lax.dot_general(sel_ref[...], edge, (((1,), (1,)), ((), ())), preferred_element_type=F32)
+
+    def leave(j):
+        own = pl.ds(pl.multiple_of(j * 512, 512), 512)
+        return (
+            pltpu.make_async_copy(stage_m.at[own], mixed_ref.at[own], sems.at[j, 0]),
+            pltpu.make_async_copy(stage_g.at[own], gg_ref.at[own], sems.at[j, 1]),
+        )
+
+    def half(j, _):
+        for k in range(16):
+            for h in range(2):
+                q = j * 16 + k
+                rows = pl.ds(pl.multiple_of(q * 32, 32) + h * 16, 16)
+                own = slice(h * 16, h * 16 + 16)
+                after0, after1, before2, before1 = (
+                    jnp.broadcast_to(turned[j, own, k * 8 + n : k * 8 + n + 1], (16, 128)) for n in range(4)
+                )
+                cols = cols_ref[rows, :]
+                tg = [column(cols, n) for n in range(3)]
+                g, c, u = (
+                    [ref[:, at : at + 128].astype(F32) for at in (0, 128)]
+                    for ref in (g_ref.at[rows], c_ref.at[rows], u_ref.at[q, own])
+                )
+                ones, twos = zip(*(rolled(x) for x in g))
+                one = jnp.where(lane < 1, before1, ones[0]), back_in_time(ones[1], ones[0], 1, lane)
+                two = jnp.where(lane < 1, before2, back_in_time(twos[0], before1, 2, lane)), back_in_time(twos[1], twos[0], 2, lane)
+                s = [a * b for a, b in zip(c, u)]
+                left = [(pltpu.roll(x, 127, 1), pltpu.roll(x, 126, 1)) for x in s]
+                next1 = jnp.where(lane > 126, left[1][0], left[0][0]), jnp.where(lane > 126, after0, left[1][0])
+                next2 = (
+                    jnp.where(lane > 125, left[1][1], left[0][1]),
+                    jnp.where(lane > 126, after1, jnp.where(lane > 125, after0, left[1][1])),
+                )
+                for n, at in enumerate((0, 128)):
+                    stage_m[rows, at : at + 128] = (shorten(g[n], one[n], two[n], tg) * u[n]).astype(BF16)
+                    stage_g[rows, at : at + 128] = shorten(s[n], next1[n], next2[n], tg).astype(BF16)
+        for copy in leave(j):
+            copy.start()
+        return 0
+
+    lax.fori_loop(0, 2, half, 0)
+    direct.wait()
+    for j in range(2):
+        for copy in leave(j):
+            copy.wait()
 
 
 VMEM = pl.BlockSpec(memory_space=pltpu.VMEM)
@@ -382,23 +463,28 @@
 def most(d, r, rim, cols):
     return call(
         most_kernel,
-        [((32, 96, 256), BF16), ((32, 128), F32)],
-        [((28, 96, 256), BF16), (pltpu.SemaphoreType.DMA((7,)), None)],
+        [((32, 72, 256), BF16), ((32, 128), F32), ((896, 128), BF16)],
+        [((28, 64, 256), BF16), (pltpu.SemaphoreType.DMA((7,)), None)],
         1 << 25,
         8 << 20,
         d,
         r,
         rim,
         cols,
-        out_specs=[ANY, VMEM],
+        out_specs=[ANY, VMEM, VMEM],
     )
 
 
-def last(done, d, r, rim, following, cols, sums):
+def last(done, d, r, rim, following, cols, sums, heads):
     return call(
         last_kernel,
-        [((32, 96, 256), BF16), ((32, 128), F32)],
-        [((4, 96, 256), BF16), (pltpu.SemaphoreType.DMA(()), None)],
+        [((32, 72, 256), BF16), ((32, 128), F32)],
+        [
+            ((4, 64, 256), BF16),
+            ((32, 8, 256), BF16),
+            ((160, 128), BF16),
+            (pltpu.SemaphoreType.DMA((2,)), None),
+        ],
         1 << 22,
         1 << 20,
         done,
@@ -408,9 +494,31 @@
         following,
         cols,
         sums,
-        in_specs=[ANY] + [VMEM] * 6,
+        heads,
+        in_specs=[ANY] + [VMEM] * 7,
         out_specs=[ANY, VMEM],
         input_output_aliases={0: 0},
+    )
+
+
+def home(u, gates, cotangent, cols, sel):
+    return call(
+        home_kernel,
+        [((1024, 256), BF16), ((32, 32, 256), BF16), ((1024, 256), BF16)],
+        [
+            ((1024, 256), BF16),
+            ((1024, 256), BF16),
+            ((2, 32, 128), F32),
+            (pltpu.SemaphoreType.DMA((2, 3)), None),
+        ],
+        1 << 24,
+        6 << 20,
+        u,
+        gates,
+        cotangent,
+        cols,
+        sel,
+        out_specs=[ANY] * 3,
     )
 
 
@@ -457,15 +565,19 @@
     grad_spectrum, weighted = mix(by_freq, spectrum.transpose(0, 2, 1), mixing)
     d, head = back(exchange(weighted, "batch"), r, rim, cols, twiddle, cas)
     following = lax.ppermute(head, "batch", [(i + 1, i) for i in range(batch - 1)])
-    done, sums = most(d, r, rim, cols)
-    done, sums = last(done, d, r, rim, following, cols, sums)
+    done, sums, heads = most(d, r, rim, cols)
+    done, sums = last(done, d, r, rim, following, cols, sums, heads)
     outs = exchange(done, "seq")
+    gate_cols = jnp.pad(taps_gates.T, ((0, 0), (0, 125)))
+    own = lax.rem(lax.axis_index("seq"), 4) * 32 + lax.broadcasted_iota(jnp.int32, (32, 128), 0)
+    sel = (own == lanes()).astype(BF16)
+    mixed, grad_values, grad_gates = home(outs, gates, cotangent, gate_cols, sel)
     step = 1
     while step < batch:
         sums = sums + lax.ppermute(sums, "batch", [(i, i ^ step) for i in range(batch)])
         step *= 2
     sums = sums[:, :7].T
-    mixed, grad_values, grad_gates = (outs[:, k * 32 : k * 32 + 32].reshape(values.shape) for k in range(3))
+    grad_values = grad_values.reshape(values.shape)
     return mixed, grad_values, grad_gates, grad_spectrum.transpose(0, 2, 1), sums[0:3], sums[3:6], sums[6]
 
 

time: 193 us -> 186 us (0.964)
  waiting for transfers between devices: 60.5 us -> 52.2 us
  Pallas kernels: 19.3 us -> 21.8 us
    all_to_all x2, waiting for transfers between devices: 50.8 us -> 43 us  [exchange(): return lax.all_to_all(array, axis, 0, 0, tiled=True)]
    pallas_call x6 -> x7, Pallas kernels: 16.8 us -> 19.2 us  [call(): pl.pallas_call(kernel, **{'in_specs': [VMEM] * len(args), 'out_specs': [V...]
  transfers between devices with their start and end apart: 8 -> 8, of which waited for: 6 -> 6; matrix products, arithmetic and copies ran while one was open for 1% -> 1% of each run, Pallas kernels for 4% -> 3%
where the time goes in v4:
time: 186 us; the launch traced here: 185 us
  blocking collectives  65.9 us (35%)
  waiting for transfers between devices  52.2 us (28%)
  starting transfers between devices  40.4 us (22%)
  Pallas kernels  21.8 us (12%)
  local copies, waits for them, and re-layouts  4.07 us (2%)
    all_to_all x2, blocking collectives, exchange(): return lax.all_to_all(array, axis, 0, 0, tiled=True)  65.9 us
    all_to_all x2, waiting for transfers between devices, exchange(): return lax.all_to_all(array, axis, 0, 0, tiled=True)  43 us
    all_to_all x2, starting transfers between devices, exchange(): return lax.all_to_all(array, axis, 0, 0, tiled=True)  19.3 us
    pallas_call x7, Pallas kernels, call(): pl.pallas_call(kernel, **{'in_specs': [VMEM] * len(args), 'out_specs': [V...  19.2 us
    ppermute x4, starting transfers between devices, per_device(): lax.ppermute(sums, 'batch', [(i, i ^ step) for i in range(batch)])  12.7 us
    ppermute x4, waiting for transfers between devices, per_device(): lax.ppermute(sums, 'batch', [(i, i ^ step) for i in range(batch)])  9.2 us
    ppermute x1, starting transfers between devices, per_device(): lax.ppermute(r[31, :64, 128:], 'batch', [(i, i + 1) for i in range(batch...  6.46 us
  transfers between devices with their start and end apart: 8, of which 6 were waited for; matrix products, arithmetic and copies ran while one was open for 1% of the time, Pallas kernels for 3%

profile of v4, /device:TPU:1, one launch (start us, length us, event | category | flops | bytes accessed | tf_op | source)
XLA Modules:
  0.0 185.5 jit_solution(6925334262082142690)
XLA Ops:
  0.6 2.4 %shard_map.153 = bf16[32,96,256]{2,1,0:T(8,128)(2,1)} custom-call(bf16[32,32,256]{2,1,0:T(8,128)(2,1)} %bitcast.17, bf16[32,32,256]{2,1,0:T(8,128)(2,1)} %bitcast.13, bf16[32,32,256]{2,1,0:T(8,128)(2,1)} %bitcast.14), custom_call_target="tpu_custom_call" | custom-call | tf_op jit(solution)/shard_map/pallas_call | solution.py:526
  3.0 13.8 %all-to-all-start = ((bf16[32,96,256]{2,1,0:T(8,128)(2,1)}), bf16[32,96,256]{2,1,0:T(8,128)(2,1)S(1)}, u32[]{:S(2)}, u32[]{:S(2)}) async-start(bf16[32,96,256]{2,1,0:T(8,128)(2,1)} %shard_map.153), calls=%async_computation | async-start | bytes 3145728 | tf_op jit(solution)/shard_map/all_to_all | solution.py:552
  16.9 36.9 %all-to-all-done.r_ref = bf16[32,96,256]{2,1,0:T(8,128)(2,1)S(1)} async-done(((bf16[32,96,256]{2,1,0:T(8,128)(2,1)}), bf16[32,96,256]{2,1,0:T(8,128)(2,1)S(1)}, u32[]{:S(2)}, u32[]{:S(2)}) %all-to-all-start) | async-done | bytes 1572896 | tf_op jit(solution)/shard_map/all_to_all | solution.py:552
  53.8 6.5 %collective-permute-start = (bf16[64,128]{1,0:T(8,128)(2,1)S(1)}, bf16[64,128]{1,0:T(8,128)(2,1)S(1)}, u32[]{:S(2)}, u32[]{:S(2)}) collective-permute-start(bf16[64,128]{1,0:T(8,128)(2,1)S(1)} %slice_bitcast_fusion), channel_id=1, source_target_pairs={{0,32},{32,64},{64,96},{96,128},{128,160},{160,192},{192,224},{224... | collective-permute-start | bytes 49160 | tf_op jit(solution)/shard_map/ppermute | solution.py:563
  60.5 1.6 copy-done
  62.3 2.1 %shard_map.154.part_ref = bf16[512,1024]{1,0:T(8,128)(2,1)S(1)} custom-call(bf16[32,96,256]{2,1,0:T(8,128)(2,1)S(1)} %all-to-all-done.r_ref, f32[32,128]{1,0:T(8,128)S(1)} %pad.8.cols_ref), custom_call_target="tpu_custom_call" | custom-call | flops 16777216 | bytes 4194304 | tf_op jit(solution)/shard_map/pallas_call | solution.py:404
  64.4 2.2 %shard_map.156 = bf16[16,256,128]{2,1,0:T(8,128)(2,1)S(1)} custom-call(bf16[512,1024]{1,0:T(8,128)(2,1)S(1)} %shard_map.154.part_ref, bf16[32,96,256]{2,1,0:T(8,128)(2,1)S(1)} %all-to-all-done.r_ref, bf16[64,128]{1,0:T(8,128)(2,1)S(1)} %collective-permute-done.rim_ref, f32[32,128]{1,0:T(8,128)S(1)} %pad.8.cols_ref, f32[8,1024]{1,0:T(8,128)S(1)} %copy-done.3, ...), custom_call_target="tpu_custom_call" | custom-call | flops 1073741824 | bytes 5242880 | tf_op jit(solution)/shard_map/pallas_call | solution.py:404
  66.6 34.7 %all_to_all.20.f_ref = bf16[16,256,128]{2,1,0:T(8,128)(2,1)S(1)} all-to-all(bf16[16,256,128]{2,1,0:T(8,128)(2,1)S(1)} %shard_map.156), channel_id=1, replica_groups=mesh['batch'=16,'seq'=32] {'batch'}, dimensions={0} | all-to-all | bytes 2097152 | tf_op jit(solution)/shard_map/all_to_all | solution.py:552
  101.3 2.9 %shard_map.157 = (f32[32,64,128]{2,1,0:T(8,128)}, bf16[16,256,128]{2,1,0:T(8,128)(2,1)S(1)}) custom-call(bf16[16,256,128]{2,1,0:T(8,128)(2,1)S(1)} %all_to_all.20.f_ref, bf16[32,64,128]{2,1,0:T(8,128)(2,1)S(1)} %bitcast.15, f32[128,128]{1,0:T(8,128)S(1)} %copy-done.5), custom_call_target="tpu_custom_call" | custom-call | flops 1073741824 | bytes 5242880 | tf_op jit(solution)/shard_map/pallas_call | solution.py:404
  104.3 31.2 %all_to_all.21.y_ref = bf16[16,256,128]{2,1,0:T(8,128)(2,1)S(1)} all-to-all(bf16[16,256,128]{2,1,0:T(8,128)(2,1)S(1)} %get-tuple-element.19), channel_id=1, replica_groups=mesh['batch'=16,'seq'=32] {'batch'}, dimensions={0} | all-to-all | bytes 2097152 | tf_op jit(solution)/shard_map/all_to_all | solution.py:552
  135.5 2.8 %shard_map.158 = (bf16[512,1024]{1,0:T(8,128)(2,1)S(1)}, f32[64,128]{1,0:T(8,128)S(1)}) custom-call(bf16[16,256,128]{2,1,0:T(8,128)(2,1)S(1)} %all_to_all.21.y_ref, bf16[32,96,256]{2,1,0:T(8,128)(2,1)S(1)} %all-to-all-done.r_ref, bf16[64,128]{1,0:T(8,128)(2,1)S(1)} %collective-permute-done.rim_ref, f32[32,128]{1,0:T(8,128)S(1)} %pad.8.cols_ref, ...), custom_call_target="tpu_custom_call" | custom-call | flops 1073741824 | bytes 5242880 | tf_op jit(solution)/shard_map/pallas_call | solution.py:404
  138.3 1.9 %collective-permute-start.1 = (f32[64,128]{1,0:T(8,128)S(1)}, f32[64,128]{1,0:T(8,128)S(1)}, u32[]{:S(2)}, u32[]{:S(2)}) collective-permute-start(f32[64,128]{1,0:T(8,128)S(1)} %get-tuple-element.22), channel_id=1, source_target_pairs={{32,0},{64,32},{96,64},{128,96},{160,128},{192,160},{224,192},{256... | collective-permute-start | bytes 98312 | tf_op jit(solution)/shard_map/ppermute | solution.py:567
  140.3 4.0 %shard_map.159 = (bf16[32,72,256]{2,1,0:T(8,128)(2,1)}, f32[32,128]{1,0:T(8,128)S(1)}, bf16[896,128]{1,0:T(8,128)(2,1)S(1)}) custom-call(bf16[512,1024]{1,0:T(8,128)(2,1)S(1)} %get-tuple-element.20.d_ref, bf16[32,96,256]{2,1,0:T(8,128)(2,1)S(1)} %all-to-all-done.r_ref, bf16[64,128]{1,0:T(8,128)(2,1)S(1)} %collective-permute-done.rim_ref, ...), custom_call_target="tpu_custom_call" | custom-call | flops 33554432 | bytes 8388608 | tf_op jit(solution)/shard_map/pallas_call | solution.py:404
  144.3 1.4 shard_map.160
  145.8 5.5 %all-to-all-start.3 = ((bf16[32,72,256]{2,1,0:T(8,128)(2,1)}), bf16[32,72,256]{2,1,0:T(8,128)(2,1)S(1)}, u32[]{:S(2)}, u32[]{:S(2)}) async-start(bf16[32,72,256]{2,1,0:T(8,128)(2,1)} %get-tuple-element.25), calls=%async_computation.3 | async-start | bytes 2359296 | tf_op jit(solution)/shard_map/all_to_all | solution.py:552
  151.2 1.9 %collective-permute-start.2 = (f32[32,128]{1,0:T(8,128)S(1)}, f32[32,128]{1,0:T(8,128)S(1)}, u32[]{:S(2)}, u32[]{:S(2)}) collective-permute-start(f32[32,128]{1,0:T(8,128)S(1)} %get-tuple-element.30), channel_id=1, source_target_pairs={{0,32},{32,0},{64,96},{96,64},{128,160},{160,128},{192,224},{224,1... | collective-permute-start | bytes 49160 | tf_op jit(solution)/shard_map/ppermute | solution.py:577
  154.3 3.7 %collective-permute-start.3 = (f32[32,128]{1,0:T(8,128)S(1)}, f32[32,128]{1,0:T(8,128)S(1)}, u32[]{:S(2)}, u32[]{:S(2)}) collective-permute-start(f32[32,128]{1,0:T(8,128)S(1)} %add.29), channel_id=1, source_target_pairs={{0,64},{32,96},{64,0},{96,32},{128,192},{160,224},{192,128},{224,1... | collective-permute-start | bytes 49160 | tf_op jit(solution)/shard_map/ppermute | solution.py:577
  158.0 1.4 collective-permute-done.3
  159.4 1.9 %collective-permute-start.4 = (f32[32,128]{1,0:T(8,128)S(1)}, f32[32,128]{1,0:T(8,128)S(1)}, u32[]{:S(2)}, u32[]{:S(2)}) collective-permute-start(f32[32,128]{1,0:T(8,128)S(1)} %add.30), channel_id=1, source_target_pairs={{0,128},{32,160},{64,192},{96,224},{128,0},{160,32},{192,64},{224,... | collective-permute-start | bytes 49160 | tf_op jit(solution)/shard_map/ppermute | solution.py:577
  161.3 3.7 %collective-permute-done.4 = f32[32,128]{1,0:T(8,128)S(1)} collective-permute-done((f32[32,128]{1,0:T(8,128)S(1)}, f32[32,128]{1,0:T(8,128)S(1)}, u32[]{:S(2)}, u32[]{:S(2)}) %collective-permute-start.4) | collective-permute-done | bytes 16416 | tf_op jit(solution)/shard_map/ppermute | solution.py:577
  165.1 5.2 %collective-permute-start.5 = (f32[32,128]{1,0:T(8,128)S(1)}, f32[32,128]{1,0:T(8,128)S(1)}, u32[]{:S(2)}, u32[]{:S(2)}) collective-permute-start(f32[32,128]{1,0:T(8,128)S(1)} %add.31), channel_id=1, source_target_pairs={{0,256},{32,288},{64,320},{96,352},{128,384},{160,416},{192,448},{... | collective-permute-start | bytes 49160 | tf_op jit(solution)/shard_map/ppermute | solution.py:577
  170.7 2.9 %collective-permute-done.5 = f32[32,128]{1,0:T(8,128)S(1)} collective-permute-done((f32[32,128]{1,0:T(8,128)S(1)}, f32[32,128]{1,0:T(8,128)S(1)}, u32[]{:S(2)}, u32[]{:S(2)}) %collective-permute-start.5) | collective-permute-done | bytes 16416 | tf_op jit(solution)/shard_map/ppermute | solution.py:577
  175.6 6.1 %all-to-all-done.3.u_ref = bf16[32,72,256]{2,1,0:T(8,128)(2,1)S(1)} async-done(((bf16[32,72,256]{2,1,0:T(8,128)(2,1)}), bf16[32,72,256]{2,1,0:T(8,128)(2,1)S(1)}, u32[]{:S(2)}, u32[]{:S(2)}) %all-to-all-start.3) | async-done | bytes 1179680 | tf_op jit(solution)/shard_map/all_to_all | solution.py:552
  181.8 3.7 %shard_map.161 = (bf16[1024,256]{1,0:T(8,128)(2,1)}, bf16[32,32,256]{2,1,0:T(8,128)(2,1)}, bf16[1024,256]{1,0:T(8,128)(2,1)}) custom-call(bf16[32,72,256]{2,1,0:T(8,128)(2,1)S(1)} %all-to-all-done.3.u_ref, bf16[1024,256]{1,0:T(8,128)(2,1)S(1)} %copy-done.1, bf16[1024,256]{1,0:T(8,128)(2,1)S(1)} %copy-done.2, f32[1024,128]{1,0:T(8,128)S(1)} %pad.9.cols_ref, ...), custom_call_target="tpu_custom_call" | custom-call | flops 16777216 | bytes 6291456 | tf_op jit(solution)/shard_map/pallas_call | solution.py:404
  (37 shorter events, 4.0 us)
Async XLA Ops:
  3.0 57.3 %copy-start.6 = (f32[3,1024]{1,0:T(4,128)S(1)}, f32[3,1024]{1,0:T(4,128)}, u32[]{:S(2)}) copy-start(f32[3,1024]{1,0:T(4,128)} %param.14) | copy-start | bytes 36868
  3.0 57.3 %copy-start.7 = (f32[3,1024]{1,0:T(4,128)S(1)}, f32[3,1024]{1,0:T(4,128)}, u32[]{:S(2)}) copy-start(f32[3,1024]{1,0:T(4,128)} %param.13) | copy-start | bytes 36868
  3.0 57.3 %copy-start.8 = (f32[1024]{0:T(1024)S(1)}, f32[1024]{0:T(1024)}, u32[]{:S(2)}) copy-start(f32[1024]{0:T(1024)} %param.15) | copy-start | bytes 12292
  3.0 50.8 %all-to-all-start = ((bf16[32,96,256]{2,1,0:T(8,128)(2,1)}), bf16[32,96,256]{2,1,0:T(8,128)(2,1)S(1)}, u32[]{:S(2)}, u32[]{:S(2)}) async-start(bf16[32,96,256]{2,1,0:T(8,128)(2,1)} %shard_map.153), calls=%async_computation | async-start | bytes 3145728 | tf_op jit(solution)/shard_map/all_to_all | solution.py:552
  53.8 10.5 %collective-permute-start = (bf16[64,128]{1,0:T(8,128)(2,1)S(1)}, bf16[64,128]{1,0:T(8,128)(2,1)S(1)}, u32[]{:S(2)}, u32[]{:S(2)}) collective-permute-start(bf16[64,128]{1,0:T(8,128)(2,1)S(1)} %slice_bitcast_fusion), channel_id=1, source_target_pairs={{0,32},{32,64},{64,96},{96,128},{128,160},{160,192},{192,224},{224... | collective-permute-start | bytes 49160 | tf_op jit(solution)/shard_map/ppermute | solution.py:563
  60.5 1.6 copy-start
  62.2 2.1 %copy-start.3 = (f32[8,1024]{1,0:T(8,128)S(1)}, f32[8,1024]{1,0:T(8,128)}, u32[]{:S(2)}) copy-start(f32[8,1024]{1,0:T(8,128)} %tw_ref.3) | copy-start | bytes 98308
  66.6 34.7 %copy-start.4 = (bf16[32,128,64]{1,2,0:T(8,128)(2,1)S(1)}, bf16[32,128,64]{1,2,0:T(8,128)(2,1)}, u32[]{:S(2)}) copy-start(bf16[32,128,64]{1,2,0:T(8,128)(2,1)} %param.18) | copy-start | bytes 1572868
  66.6 34.7 %copy-start.5 = (f32[128,128]{1,0:T(8,128)S(1)}, f32[128,128]{1,0:T(8,128)}, u32[]{:S(2)}) copy-start(f32[128,128]{1,0:T(8,128)} %mix_ref.1) | copy-start | bytes 196612
  138.3 6.0 %collective-permute-start.1 = (f32[64,128]{1,0:T(8,128)S(1)}, f32[64,128]{1,0:T(8,128)S(1)}, u32[]{:S(2)}, u32[]{:S(2)}) collective-permute-start(f32[64,128]{1,0:T(8,128)S(1)} %get-tuple-element.22), channel_id=1, source_target_pairs={{32,0},{64,32},{96,64},{128,96},{160,128},{192,160},{224,192},{256... | collective-permute-start | bytes 98312 | tf_op jit(solution)/shard_map/ppermute | solution.py:567
  145.7 36.0 %copy-start.1 = (bf16[1024,256]{1,0:T(8,128)(2,1)S(1)}, bf16[1024,256]{1,0:T(8,128)(2,1)}, u32[]{:S(2)}) copy-start(bf16[1024,256]{1,0:T(8,128)(2,1)} %g_ref.1) | copy-start | bytes 1572868
  145.7 36.0 %copy-start.2 = (bf16[1024,256]{1,0:T(8,128)(2,1)S(1)}, bf16[1024,256]{1,0:T(8,128)(2,1)}, u32[]{:S(2)}) copy-start(bf16[1024,256]{1,0:T(8,128)(2,1)} %c_ref.1) | copy-start | bytes 1572868
  145.8 36.0 %all-to-all-start.3 = ((bf16[32,72,256]{2,1,0:T(8,128)(2,1)}), bf16[32,72,256]{2,1,0:T(8,128)(2,1)S(1)}, u32[]{:S(2)}, u32[]{:S(2)}) async-start(bf16[32,72,256]{2,1,0:T(8,128)(2,1)} %get-tuple-element.25), calls=%async_computation.3 | async-start | bytes 2359296 | tf_op jit(solution)/shard_map/all_to_all | solution.py:552
  151.2 3.1 %collective-permute-start.2 = (f32[32,128]{1,0:T(8,128)S(1)}, f32[32,128]{1,0:T(8,128)S(1)}, u32[]{:S(2)}, u32[]{:S(2)}) collective-permute-start(f32[32,128]{1,0:T(8,128)S(1)} %get-tuple-element.30), channel_id=1, source_target_pairs={{0,32},{32,0},{64,96},{96,64},{128,160},{160,128},{192,224},{224,1... | collective-permute-start | bytes 49160 | tf_op jit(solution)/shard_map/ppermute | solution.py:577
  154.3 5.1 %collective-permute-start.3 = (f32[32,128]{1,0:T(8,128)S(1)}, f32[32,128]{1,0:T(8,128)S(1)}, u32[]{:S(2)}, u32[]{:S(2)}) collective-permute-start(f32[32,128]{1,0:T(8,128)S(1)} %add.29), channel_id=1, source_target_pairs={{0,64},{32,96},{64,0},{96,32},{128,192},{160,224},{192,128},{224,1... | collective-permute-start | bytes 49160 | tf_op jit(solution)/shard_map/ppermute | solution.py:577
  159.4 5.7 %collective-permute-start.4 = (f32[32,128]{1,0:T(8,128)S(1)}, f32[32,128]{1,0:T(8,128)S(1)}, u32[]{:S(2)}, u32[]{:S(2)}) collective-permute-start(f32[32,128]{1,0:T(8,128)S(1)} %add.30), channel_id=1, source_target_pairs={{0,128},{32,160},{64,192},{96,224},{128,0},{160,32},{192,64},{224,... | collective-permute-start | bytes 49160 | tf_op jit(solution)/shard_map/ppermute | solution.py:577
  165.1 8.5 %collective-permute-start.5 = (f32[32,128]{1,0:T(8,128)S(1)}, f32[32,128]{1,0:T(8,128)S(1)}, u32[]{:S(2)}, u32[]{:S(2)}) collective-permute-start(f32[32,128]{1,0:T(8,128)S(1)} %add.31), channel_id=1, source_target_pairs={{0,256},{32,288},{64,320},{96,352},{128,384},{160,416},{192,448},{... | collective-permute-start | bytes 49160 | tf_op jit(solution)/shard_map/ppermute | solution.py:577

commit v5 on v4

--- a/solution.py
+++ b/solution.py
@@ -12,7 +12,7 @@
 BLOCK = 1024
 F32, BF16 = jnp.float32, jnp.bfloat16
 GRANT = 20 << 20
-PARTS = 4
+PARTS, AHEAD = 4, 2
 
 
 def cas_table():
@@ -51,13 +51,15 @@
             ]
         )
         leave.append(pltpu.make_async_copy(held.at[own], out_ref.at[own], out_sems.at[p]))
-    for part in arrive:
+    for part in arrive[:AHEAD]:
         for copy in part:
             copy.start()
-    for part, copy in zip(arrive, leave):
-        for one in part:
+    for p in range(PARTS):
+        for one in arrive[p]:
             one.wait()
-        copy.start()
+        leave[p].start()
+        for one in arrive[p + AHEAD] if p + AHEAD < PARTS else ():
+            one.start()
     for copy in leave:
         copy.wait()
 
@@ -136,7 +138,7 @@
     lax.fori_loop(0, 4, strip, 0)
 
 
-def mix_kernel(f_ref, spec_ref, mix_ref, gs_ref, out_ref, wide_v, wide_g):
+def mix_kernel(f_ref, spec_ref, mix_ref, gs_ref, out_ref, wide_v, wide_g, stage, sems):
     wide = (wide_v, wide_g)
     for f in range(2):
         for b in range(16):
@@ -148,6 +150,7 @@
     ahead = jnp.concatenate([high, low], axis=1)
     again = jnp.concatenate([jnp.concatenate([high, high], axis=1), jnp.concatenate([low, low], axis=1)], axis=0)
 
+    leaving = []
     for c in range(16):
         slabs = [wide[f][pl.ds(c, 128, stride=16), :].T.astype(BF16) for f in range(2)]
         both = jnp.dot(jnp.concatenate(slabs, axis=0), ahead, preferred_element_type=F32)
@@ -155,8 +158,10 @@
         sv, sg = both[:128], both[128:]
         filters = jnp.concatenate([spec_ref[c], spec_ref[16 + c]], axis=0).astype(F32)
         grad = sv * sg
-        gs_ref[c] = grad[:64]
-        gs_ref[16 + c] = grad[64:]
+        for n, channel in enumerate((c, 16 + c)):
+            stage[channel] = grad[n * 64 : n * 64 + 64]
+            leaving.append(pltpu.make_async_copy(stage.at[channel], gs_ref.at[channel], sems.at[channel]))
+            leaving[-1].start()
         product = jnp.concatenate([sv * filters, sg * filters], axis=0)
         top = product.astype(BF16)
         rest = (product - top.astype(F32)).astype(BF16)
@@ -168,6 +173,8 @@
     for f in range(2):
         for b in range(16):
             out_ref[b, f * 128 : f * 128 + 128, :] = wide[f][b * 128 : b * 128 + 128, :].astype(BF16)
+    for copy in leaving:
+        copy.wait()
 
 
 def back_kernel(y_ref, r_ref, rim_ref, cols_ref, tw_ref, cas_ref, out_ref, head_ref, lhs):
@@ -346,21 +353,21 @@
     direct = pltpu.make_async_copy(u_ref.at[:, 32:64, :], gv_ref, sems.at[0, 2])
     direct.start()
     lane = lanes((16, 128))
-    for j in range(2):
-        edge = u_ref[j * 16 : j * 16 + 16, 64:72, 0:128].astype(F32).reshape(128, 128).astype(BF16)
+    for j in range(4):
+        edge = u_ref[j * 8 : j * 8 + 8, 64:72, 0:128].astype(F32).reshape(64, 128).astype(BF16)
         turned[j] = lax.dot_general(sel_ref[...], edge, (((1,), (1,)), ((), ())), preferred_element_type=F32)
 
     def leave(j):
-        own = pl.ds(pl.multiple_of(j * 512, 512), 512)
+        own = pl.ds(pl.multiple_of(j * 256, 256), 256)
         return (
             pltpu.make_async_copy(stage_m.at[own], mixed_ref.at[own], sems.at[j, 0]),
             pltpu.make_async_copy(stage_g.at[own], gg_ref.at[own], sems.at[j, 1]),
         )
 
-    def half(j, _):
-        for k in range(16):
+    def part(j, _):
+        for k in range(8):
             for h in range(2):
-                q = j * 16 + k
+                q = j * 8 + k
                 rows = pl.ds(pl.multiple_of(q * 32, 32) + h * 16, 16)
                 own = slice(h * 16, h * 16 + 16)
                 after0, after1, before2, before1 = (
@@ -389,9 +396,9 @@
             copy.start()
         return 0
 
-    lax.fori_loop(0, 2, half, 0)
+    lax.fori_loop(0, 4, part, 0)
     direct.wait()
-    for j in range(2):
+    for j in range(4):
         for copy in leave(j):
             copy.wait()
 
@@ -435,12 +442,18 @@
     return call(
         mix_kernel,
         [((32, 64, 128), F32), ((16, 256, 128), BF16)],
-        [((2048, 128), F32), ((2048, 128), F32)],
+        [
+            ((2048, 128), F32),
+            ((2048, 128), F32),
+            ((32, 64, 128), F32),
+            (pltpu.SemaphoreType.DMA((32,)), None),
+        ],
         1 << 30,
         5 << 20,
         by_freq,
         spectrum,
         mixing,
+        out_specs=[ANY, VMEM],
     )
 
 
@@ -508,8 +521,8 @@
         [
             ((1024, 256), BF16),
             ((1024, 256), BF16),
-            ((2, 32, 128), F32),
-            (pltpu.SemaphoreType.DMA((2, 3)), None),
+            ((4, 32, 64), F32),
+            (pltpu.SemaphoreType.DMA((4, 3)), None),
         ],
         1 << 24,
         6 << 20,

time: 186 us -> 187 us (level)
  no operation moved by 1% of the time
where the time goes in v5:
time: 187 us; the launch traced here: 186 us
  blocking collectives  65.9 us (35%)
  waiting for transfers between devices  52.2 us (28%)
  starting transfers between devices  40.4 us (22%)
  Pallas kernels  22.8 us (12%)
  local copies, waits for them, and re-layouts  4.07 us (2%)
    all_to_all x2, blocking collectives, exchange(): return lax.all_to_all(array, axis, 0, 0, tiled=True)  65.9 us
    all_to_all x2, waiting for transfers between devices, exchange(): return lax.all_to_all(array, axis, 0, 0, tiled=True)  43 us
    all_to_all x2, starting transfers between devices, exchange(): return lax.all_to_all(array, axis, 0, 0, tiled=True)  19.3 us
    pallas_call x7, Pallas kernels, call(): pl.pallas_call(kernel, **{'in_specs': [VMEM] * len(args), 'out_specs': [V...  19.2 us
    ppermute x4, starting transfers between devices, per_device(): lax.ppermute(sums, 'batch', [(i, i ^ step) for i in range(batch)])  12.7 us
    ppermute x4, waiting for transfers between devices, per_device(): lax.ppermute(sums, 'batch', [(i, i ^ step) for i in range(batch)])  9.2 us
    ppermute x1, starting transfers between devices, per_device(): lax.ppermute(r[31, :64, 128:], 'batch', [(i, i + 1) for i in range(batch...  6.46 us
  transfers between devices with their start and end apart: 8, of which 6 were waited for; matrix products, arithmetic and copies ran while one was open for 1% of the time, Pallas kernels for 3%

profile of v5, /device:TPU:1, one launch (start us, length us, event | category | flops | bytes accessed | tf_op | source)
XLA Modules:
  0.0 186.5 jit_solution(17474846634045916668)
XLA Ops:
  0.6 3.4 %shard_map.153 = bf16[32,96,256]{2,1,0:T(8,128)(2,1)} custom-call(bf16[32,32,256]{2,1,0:T(8,128)(2,1)} %bitcast.17, bf16[32,32,256]{2,1,0:T(8,128)(2,1)} %bitcast.13, bf16[32,32,256]{2,1,0:T(8,128)(2,1)} %bitcast.14), custom_call_target="tpu_custom_call" | custom-call | tf_op jit(solution)/shard_map/pallas_call | solution.py:539
  4.1 13.8 %all-to-all-start = ((bf16[32,96,256]{2,1,0:T(8,128)(2,1)}), bf16[32,96,256]{2,1,0:T(8,128)(2,1)S(1)}, u32[]{:S(2)}, u32[]{:S(2)}) async-start(bf16[32,96,256]{2,1,0:T(8,128)(2,1)} %shard_map.153), calls=%async_computation | async-start | bytes 3145728 | tf_op jit(solution)/shard_map/all_to_all | solution.py:565
  17.9 36.9 %all-to-all-done.r_ref = bf16[32,96,256]{2,1,0:T(8,128)(2,1)S(1)} async-done(((bf16[32,96,256]{2,1,0:T(8,128)(2,1)}), bf16[32,96,256]{2,1,0:T(8,128)(2,1)S(1)}, u32[]{:S(2)}, u32[]{:S(2)}) %all-to-all-start) | async-done | bytes 1572896 | tf_op jit(solution)/shard_map/all_to_all | solution.py:565
  54.8 6.5 %collective-permute-start = (bf16[64,128]{1,0:T(8,128)(2,1)S(1)}, bf16[64,128]{1,0:T(8,128)(2,1)S(1)}, u32[]{:S(2)}, u32[]{:S(2)}) collective-permute-start(bf16[64,128]{1,0:T(8,128)(2,1)S(1)} %slice_bitcast_fusion), channel_id=1, source_target_pairs={{0,32},{32,64},{64,96},{96,128},{128,160},{160,192},{192,224},{224... | collective-permute-start | bytes 49160 | tf_op jit(solution)/shard_map/ppermute | solution.py:576
  61.5 1.6 copy-done
  63.3 2.1 %shard_map.154.part_ref = bf16[512,1024]{1,0:T(8,128)(2,1)S(1)} custom-call(bf16[32,96,256]{2,1,0:T(8,128)(2,1)S(1)} %all-to-all-done.r_ref, f32[32,128]{1,0:T(8,128)S(1)} %pad.8.cols_ref), custom_call_target="tpu_custom_call" | custom-call | flops 16777216 | bytes 4194304 | tf_op jit(solution)/shard_map/pallas_call | solution.py:411
  65.4 2.2 %shard_map.156 = bf16[16,256,128]{2,1,0:T(8,128)(2,1)S(1)} custom-call(bf16[512,1024]{1,0:T(8,128)(2,1)S(1)} %shard_map.154.part_ref, bf16[32,96,256]{2,1,0:T(8,128)(2,1)S(1)} %all-to-all-done.r_ref, bf16[64,128]{1,0:T(8,128)(2,1)S(1)} %collective-permute-done.rim_ref, f32[32,128]{1,0:T(8,128)S(1)} %pad.8.cols_ref, f32[8,1024]{1,0:T(8,128)S(1)} %copy-done.3, ...), custom_call_target="tpu_custom_call" | custom-call | flops 1073741824 | bytes 5242880 | tf_op jit(solution)/shard_map/pallas_call | solution.py:411
  67.7 34.7 %all_to_all.20.f_ref = bf16[16,256,128]{2,1,0:T(8,128)(2,1)S(1)} all-to-all(bf16[16,256,128]{2,1,0:T(8,128)(2,1)S(1)} %shard_map.156), channel_id=1, replica_groups=mesh['batch'=16,'seq'=32] {'batch'}, dimensions={0} | all-to-all | bytes 2097152 | tf_op jit(solution)/shard_map/all_to_all | solution.py:565
  102.4 2.9 %shard_map.157 = (f32[32,64,128]{2,1,0:T(8,128)}, bf16[16,256,128]{2,1,0:T(8,128)(2,1)S(1)}) custom-call(bf16[16,256,128]{2,1,0:T(8,128)(2,1)S(1)} %all_to_all.20.f_ref, bf16[32,64,128]{2,1,0:T(8,128)(2,1)S(1)} %bitcast.15, f32[128,128]{1,0:T(8,128)S(1)} %copy-done.5), custom_call_target="tpu_custom_call" | custom-call | flops 1073741824 | bytes 5242880 | tf_op jit(solution)/shard_map/pallas_call | solution.py:411
  105.2 31.2 %all_to_all.21.y_ref = bf16[16,256,128]{2,1,0:T(8,128)(2,1)S(1)} all-to-all(bf16[16,256,128]{2,1,0:T(8,128)(2,1)S(1)} %get-tuple-element.19), channel_id=1, replica_groups=mesh['batch'=16,'seq'=32] {'batch'}, dimensions={0} | all-to-all | bytes 2097152 | tf_op jit(solution)/shard_map/all_to_all | solution.py:565
  136.4 2.9 %shard_map.158 = (bf16[512,1024]{1,0:T(8,128)(2,1)S(1)}, f32[64,128]{1,0:T(8,128)S(1)}) custom-call(bf16[16,256,128]{2,1,0:T(8,128)(2,1)S(1)} %all_to_all.21.y_ref, bf16[32,96,256]{2,1,0:T(8,128)(2,1)S(1)} %all-to-all-done.r_ref, bf16[64,128]{1,0:T(8,128)(2,1)S(1)} %collective-permute-done.rim_ref, f32[32,128]{1,0:T(8,128)S(1)} %pad.8.cols_ref, ...), custom_call_target="tpu_custom_call" | custom-call | flops 1073741824 | bytes 5242880 | tf_op jit(solution)/shard_map/pallas_call | solution.py:411
  139.3 1.9 %collective-permute-start.1 = (f32[64,128]{1,0:T(8,128)S(1)}, f32[64,128]{1,0:T(8,128)S(1)}, u32[]{:S(2)}, u32[]{:S(2)}) collective-permute-start(f32[64,128]{1,0:T(8,128)S(1)} %get-tuple-element.22), channel_id=1, source_target_pairs={{32,0},{64,32},{96,64},{128,96},{160,128},{192,160},{224,192},{256... | collective-permute-start | bytes 98312 | tf_op jit(solution)/shard_map/ppermute | solution.py:580
  141.2 4.0 %shard_map.159 = (bf16[32,72,256]{2,1,0:T(8,128)(2,1)}, f32[32,128]{1,0:T(8,128)S(1)}, bf16[896,128]{1,0:T(8,128)(2,1)S(1)}) custom-call(bf16[512,1024]{1,0:T(8,128)(2,1)S(1)} %get-tuple-element.20.d_ref, bf16[32,96,256]{2,1,0:T(8,128)(2,1)S(1)} %all-to-all-done.r_ref, bf16[64,128]{1,0:T(8,128)(2,1)S(1)} %collective-permute-done.rim_ref, ...), custom_call_target="tpu_custom_call" | custom-call | flops 33554432 | bytes 8388608 | tf_op jit(solution)/shard_map/pallas_call | solution.py:411
  145.3 1.4 shard_map.160
  146.7 5.5 %all-to-all-start.3 = ((bf16[32,72,256]{2,1,0:T(8,128)(2,1)}), bf16[32,72,256]{2,1,0:T(8,128)(2,1)S(1)}, u32[]{:S(2)}, u32[]{:S(2)}) async-start(bf16[32,72,256]{2,1,0:T(8,128)(2,1)} %get-tuple-element.25), calls=%async_computation.3 | async-start | bytes 2359296 | tf_op jit(solution)/shard_map/all_to_all | solution.py:565
  152.2 1.9 %collective-permute-start.2 = (f32[32,128]{1,0:T(8,128)S(1)}, f32[32,128]{1,0:T(8,128)S(1)}, u32[]{:S(2)}, u32[]{:S(2)}) collective-permute-start(f32[32,128]{1,0:T(8,128)S(1)} %get-tuple-element.30), channel_id=1, source_target_pairs={{0,32},{32,0},{64,96},{96,64},{128,160},{160,128},{192,224},{224,1... | collective-permute-start | bytes 49160 | tf_op jit(solution)/shard_map/ppermute | solution.py:590
  155.3 3.7 %collective-permute-start.3 = (f32[32,128]{1,0:T(8,128)S(1)}, f32[32,128]{1,0:T(8,128)S(1)}, u32[]{:S(2)}, u32[]{:S(2)}) collective-permute-start(f32[32,128]{1,0:T(8,128)S(1)} %add.29), channel_id=1, source_target_pairs={{0,64},{32,96},{64,0},{96,32},{128,192},{160,224},{192,128},{224,1... | collective-permute-start | bytes 49160 | tf_op jit(solution)/shard_map/ppermute | solution.py:590
  159.0 1.4 collective-permute-done.3
  160.4 1.9 %collective-permute-start.4 = (f32[32,128]{1,0:T(8,128)S(1)}, f32[32,128]{1,0:T(8,128)S(1)}, u32[]{:S(2)}, u32[]{:S(2)}) collective-permute-start(f32[32,128]{1,0:T(8,128)S(1)} %add.30), channel_id=1, source_target_pairs={{0,128},{32,160},{64,192},{96,224},{128,0},{160,32},{192,64},{224,... | collective-permute-start | bytes 49160 | tf_op jit(solution)/shard_map/ppermute | solution.py:590
  162.3 3.7 %collective-permute-done.4 = f32[32,128]{1,0:T(8,128)S(1)} collective-permute-done((f32[32,128]{1,0:T(8,128)S(1)}, f32[32,128]{1,0:T(8,128)S(1)}, u32[]{:S(2)}, u32[]{:S(2)}) %collective-permute-start.4) | collective-permute-done | bytes 16416 | tf_op jit(solution)/shard_map/ppermute | solution.py:590
  166.1 5.2 %collective-permute-start.5 = (f32[32,128]{1,0:T(8,128)S(1)}, f32[32,128]{1,0:T(8,128)S(1)}, u32[]{:S(2)}, u32[]{:S(2)}) collective-permute-start(f32[32,128]{1,0:T(8,128)S(1)} %add.31), channel_id=1, source_target_pairs={{0,256},{32,288},{64,320},{96,352},{128,384},{160,416},{192,448},{... | collective-permute-start | bytes 49160 | tf_op jit(solution)/shard_map/ppermute | solution.py:590
  171.6 2.9 %collective-permute-done.5 = f32[32,128]{1,0:T(8,128)S(1)} collective-permute-done((f32[32,128]{1,0:T(8,128)S(1)}, f32[32,128]{1,0:T(8,128)S(1)}, u32[]{:S(2)}, u32[]{:S(2)}) %collective-permute-start.5) | collective-permute-done | bytes 16416 | tf_op jit(solution)/shard_map/ppermute | solution.py:590
  176.6 6.1 %all-to-all-done.3.u_ref = bf16[32,72,256]{2,1,0:T(8,128)(2,1)S(1)} async-done(((bf16[32,72,256]{2,1,0:T(8,128)(2,1)}), bf16[32,72,256]{2,1,0:T(8,128)(2,1)S(1)}, u32[]{:S(2)}, u32[]{:S(2)}) %all-to-all-start.3) | async-done | bytes 1179680 | tf_op jit(solution)/shard_map/all_to_all | solution.py:565
  182.7 3.8 %shard_map.161 = (bf16[1024,256]{1,0:T(8,128)(2,1)}, bf16[32,32,256]{2,1,0:T(8,128)(2,1)}, bf16[1024,256]{1,0:T(8,128)(2,1)}) custom-call(bf16[32,72,256]{2,1,0:T(8,128)(2,1)S(1)} %all-to-all-done.3.u_ref, bf16[1024,256]{1,0:T(8,128)(2,1)S(1)} %copy-done.1, bf16[1024,256]{1,0:T(8,128)(2,1)S(1)} %copy-done.2, f32[1024,128]{1,0:T(8,128)S(1)} %pad.9.cols_ref, ...), custom_call_target="tpu_custom_call" | custom-call | flops 16777216 | bytes 6291456 | tf_op jit(solution)/shard_map/pallas_call | solution.py:411
  (37 shorter events, 4.0 us)
Async XLA Ops:
  4.0 57.3 %copy-start.6 = (f32[3,1024]{1,0:T(4,128)S(1)}, f32[3,1024]{1,0:T(4,128)}, u32[]{:S(2)}) copy-start(f32[3,1024]{1,0:T(4,128)} %param.14) | copy-start | bytes 36868
  4.1 57.3 %copy-start.7 = (f32[3,1024]{1,0:T(4,128)S(1)}, f32[3,1024]{1,0:T(4,128)}, u32[]{:S(2)}) copy-start(f32[3,1024]{1,0:T(4,128)} %param.13) | copy-start | bytes 36868
  4.1 57.3 %copy-start.8 = (f32[1024]{0:T(1024)S(1)}, f32[1024]{0:T(1024)}, u32[]{:S(2)}) copy-start(f32[1024]{0:T(1024)} %param.15) | copy-start | bytes 12292
  4.1 50.8 %all-to-all-start = ((bf16[32,96,256]{2,1,0:T(8,128)(2,1)}), bf16[32,96,256]{2,1,0:T(8,128)(2,1)S(1)}, u32[]{:S(2)}, u32[]{:S(2)}) async-start(bf16[32,96,256]{2,1,0:T(8,128)(2,1)} %shard_map.153), calls=%async_computation | async-start | bytes 3145728 | tf_op jit(solution)/shard_map/all_to_all | solution.py:565
  54.8 10.5 %collective-permute-start = (bf16[64,128]{1,0:T(8,128)(2,1)S(1)}, bf16[64,128]{1,0:T(8,128)(2,1)S(1)}, u32[]{:S(2)}, u32[]{:S(2)}) collective-permute-start(bf16[64,128]{1,0:T(8,128)(2,1)S(1)} %slice_bitcast_fusion), channel_id=1, source_target_pairs={{0,32},{32,64},{64,96},{96,128},{128,160},{160,192},{192,224},{224... | collective-permute-start | bytes 49160 | tf_op jit(solution)/shard_map/ppermute | solution.py:576
  61.5 1.6 copy-start
  63.3 2.1 %copy-start.3 = (f32[8,1024]{1,0:T(8,128)S(1)}, f32[8,1024]{1,0:T(8,128)}, u32[]{:S(2)}) copy-start(f32[8,1024]{1,0:T(8,128)} %tw_ref.3) | copy-start | bytes 98308
  67.6 34.7 %copy-start.4 = (bf16[32,128,64]{1,2,0:T(8,128)(2,1)S(1)}, bf16[32,128,64]{1,2,0:T(8,128)(2,1)}, u32[]{:S(2)}) copy-start(bf16[32,128,64]{1,2,0:T(8,128)(2,1)} %param.18) | copy-start | bytes 1572868
  67.6 34.7 %copy-start.5 = (f32[128,128]{1,0:T(8,128)S(1)}, f32[128,128]{1,0:T(8,128)}, u32[]{:S(2)}) copy-start(f32[128,128]{1,0:T(8,128)} %mix_ref.1) | copy-start | bytes 196612
  139.3 6.0 %collective-permute-start.1 = (f32[64,128]{1,0:T(8,128)S(1)}, f32[64,128]{1,0:T(8,128)S(1)}, u32[]{:S(2)}, u32[]{:S(2)}) collective-permute-start(f32[64,128]{1,0:T(8,128)S(1)} %get-tuple-element.22), channel_id=1, source_target_pairs={{32,0},{64,32},{96,64},{128,96},{160,128},{192,160},{224,192},{256... | collective-permute-start | bytes 98312 | tf_op jit(solution)/shard_map/ppermute | solution.py:580
  146.7 36.0 %copy-start.1 = (bf16[1024,256]{1,0:T(8,128)(2,1)S(1)}, bf16[1024,256]{1,0:T(8,128)(2,1)}, u32[]{:S(2)}) copy-start(bf16[1024,256]{1,0:T(8,128)(2,1)} %g_ref.1) | copy-start | bytes 1572868
  146.7 36.0 %copy-start.2 = (bf16[1024,256]{1,0:T(8,128)(2,1)S(1)}, bf16[1024,256]{1,0:T(8,128)(2,1)}, u32[]{:S(2)}) copy-start(bf16[1024,256]{1,0:T(8,128)(2,1)} %c_ref.1) | copy-start | bytes 1572868
  146.7 36.0 %all-to-all-start.3 = ((bf16[32,72,256]{2,1,0:T(8,128)(2,1)}), bf16[32,72,256]{2,1,0:T(8,128)(2,1)S(1)}, u32[]{:S(2)}, u32[]{:S(2)}) async-start(bf16[32,72,256]{2,1,0:T(8,128)(2,1)} %get-tuple-element.25), calls=%async_computation.3 | async-start | bytes 2359296 | tf_op jit(solution)/shard_map/all_to_all | solution.py:565
  152.2 3.1 %collective-permute-start.2 = (f32[32,128]{1,0:T(8,128)S(1)}, f32[32,128]{1,0:T(8,128)S(1)}, u32[]{:S(2)}, u32[]{:S(2)}) collective-permute-start(f32[32,128]{1,0:T(8,128)S(1)} %get-tuple-element.30), channel_id=1, source_target_pairs={{0,32},{32,0},{64,96},{96,64},{128,160},{160,128},{192,224},{224,1... | collective-permute-start | bytes 49160 | tf_op jit(solution)/shard_map/ppermute | solution.py:590
  155.3 5.1 %collective-permute-start.3 = (f32[32,128]{1,0:T(8,128)S(1)}, f32[32,128]{1,0:T(8,128)S(1)}, u32[]{:S(2)}, u32[]{:S(2)}) collective-permute-start(f32[32,128]{1,0:T(8,128)S(1)} %add.29), channel_id=1, source_target_pairs={{0,64},{32,96},{64,0},{96,32},{128,192},{160,224},{192,128},{224,1... | collective-permute-start | bytes 49160 | tf_op jit(solution)/shard_map/ppermute | solution.py:590
  160.4 5.7 %collective-permute-start.4 = (f32[32,128]{1,0:T(8,128)S(1)}, f32[32,128]{1,0:T(8,128)S(1)}, u32[]{:S(2)}, u32[]{:S(2)}) collective-permute-start(f32[32,128]{1,0:T(8,128)S(1)} %add.30), channel_id=1, source_target_pairs={{0,128},{32,160},{64,192},{96,224},{128,0},{160,32},{192,64},{224,... | collective-permute-start | bytes 49160 | tf_op jit(solution)/shard_map/ppermute | solution.py:590
  166.1 8.5 %collective-permute-start.5 = (f32[32,128]{1,0:T(8,128)S(1)}, f32[32,128]{1,0:T(8,128)S(1)}, u32[]{:S(2)}, u32[]{:S(2)}) collective-permute-start(f32[32,128]{1,0:T(8,128)S(1)} %add.31), channel_id=1, source_target_pairs={{0,256},{32,288},{64,320},{96,352},{128,384},{160,416},{192,448},{... | collective-permute-start | bytes 49160 | tf_op jit(solution)/shard_map/ppermute | solution.py:590

commit v6 on v4

--- a/solution.py
+++ b/solution.py
@@ -12,7 +12,7 @@
 BLOCK = 1024
 F32, BF16 = jnp.float32, jnp.bfloat16
 GRANT = 20 << 20
-PARTS = 4
+PARTS = 8
 
 
 def cas_table():
@@ -309,33 +309,35 @@
 def last_kernel(
     most_ref, d_ref, r_ref, rim_ref, next_ref, cols_ref, some_ref, heads_ref, out_ref, sums_ref, stage, edges, held, sems
 ):
-    finish(r_ref, d_ref, rim_ref, cols_ref, stage, held, sums_ref, 7, 1, next_ref, lambda i: None)
-    copies = [
-        pltpu.make_async_copy(stage, out_ref.at[28:32, 0:64, :], sems.at[0]),
-        pltpu.make_async_copy(edges, out_ref.at[:, 64:72, :], sems.at[1]),
-    ]
-    copies[0].start()
-    sums_ref[...] = sums_ref[...] + some_ref[...]
-    held[128:160, :] = next_ref[32:64, :].astype(BF16)
     line = lax.broadcasted_iota(jnp.int32, (8, 128), 0)
     lane = lanes((8, 128))
     after = ((line < 2) & (lane == line)).astype(F32).astype(BF16)
     before = ((line > 1) & (line < 4) & (lane == line + 124)).astype(F32).astype(BF16)
     dims = (((1,), (1,)), ((), ()))
-    edges[:, :, 128:256] = jnp.zeros((32, 8, 128), BF16)
-    for j in range(8):
-        if j < 6:
-            ahead = heads_ref[j * 128 + 32 : j * 128 + 160, :]
-        elif j == 6:
-            ahead = jnp.concatenate([heads_ref[800:896, :], held[0:32, :]], axis=0)
-        else:
-            ahead = held[32:160, :]
+
+    def edge_rows(j, ahead):
         pieces = [r_ref[p, 32:64, 128:256] if p >= 0 else rim_ref[32:64, :] for p in range(4 * j - 1, 4 * j + 3)]
         rows = lax.dot_general(after, ahead, dims, preferred_element_type=F32)
         rows += lax.dot_general(before, jnp.concatenate(pieces, axis=0), dims, preferred_element_type=F32)
         for p in range(4 * j, 4 * j + 4):
             edges[p, :, 0:128] = rows.astype(BF16)
+
+    edges[:, :, 128:256] = jnp.zeros((32, 8, 128), BF16)
+    copies = [
+        pltpu.make_async_copy(edges.at[0:24], out_ref.at[0:24, 64:72, :], sems.at[0]),
+        pltpu.make_async_copy(stage, out_ref.at[28:32, 0:64, :], sems.at[1]),
+        pltpu.make_async_copy(edges.at[24:32], out_ref.at[24:32, 64:72, :], sems.at[2]),
+    ]
+    for j in range(6):
+        edge_rows(j, heads_ref[j * 128 + 32 : j * 128 + 160, :])
+    copies[0].start()
+    finish(r_ref, d_ref, rim_ref, cols_ref, stage, held, sums_ref, 7, 1, next_ref, lambda i: None)
     copies[1].start()
+    held[128:160, :] = next_ref[32:64, :].astype(BF16)
+    edge_rows(6, jnp.concatenate([heads_ref[800:896, :], held[0:32, :]], axis=0))
+    edge_rows(7, held[32:160, :])
+    copies[2].start()
+    sums_ref[...] = sums_ref[...] + some_ref[...]
     for copy in copies:
         copy.wait()
 
@@ -483,7 +485,7 @@
             ((4, 64, 256), BF16),
             ((32, 8, 256), BF16),
             ((160, 128), BF16),
-            (pltpu.SemaphoreType.DMA((2,)), None),
+            (pltpu.SemaphoreType.DMA((3,)), None),
         ],
         1 << 22,
         1 << 20,

time: 186 us -> 186 us (level)
  no operation moved by 1% of the time
where the time goes in v6:
time: 186 us; the launch traced here: 185 us
  blocking collectives  65.9 us (35%)
  waiting for transfers between devices  52.2 us (28%)
  starting transfers between devices  40.4 us (22%)
  Pallas kernels  21.8 us (12%)
  local copies, waits for them, and re-layouts  4.07 us (2%)
    all_to_all x2, blocking collectives, exchange(): return lax.all_to_all(array, axis, 0, 0, tiled=True)  65.9 us
    all_to_all x2, waiting for transfers between devices, exchange(): return lax.all_to_all(array, axis, 0, 0, tiled=True)  43 us
    all_to_all x2, starting transfers between devices, exchange(): return lax.all_to_all(array, axis, 0, 0, tiled=True)  19.3 us
    pallas_call x7, Pallas kernels, call(): pl.pallas_call(kernel, **{'in_specs': [VMEM] * len(args), 'out_specs': [V...  19.2 us
    ppermute x4, starting transfers between devices, per_device(): lax.ppermute(sums, 'batch', [(i, i ^ step) for i in range(batch)])  12.7 us
    ppermute x4, waiting for transfers between devices, per_device(): lax.ppermute(sums, 'batch', [(i, i ^ step) for i in range(batch)])  9.2 us
    ppermute x1, starting transfers between devices, per_device(): lax.ppermute(r[31, :64, 128:], 'batch', [(i, i + 1) for i in range(batch...  6.46 us
  transfers between devices with their start and end apart: 8, of which 6 were waited for; matrix products, arithmetic and copies ran while one was open for 1% of the time, Pallas kernels for 3%

profile of v6, /device:TPU:1, one launch (start us, length us, event | category | flops | bytes accessed | tf_op | source)
XLA Modules:
  0.0 185.4 jit_solution(7759475658576882533)
XLA Ops:
  0.6 2.4 %shard_map.153 = bf16[32,96,256]{2,1,0:T(8,128)(2,1)} custom-call(bf16[32,32,256]{2,1,0:T(8,128)(2,1)} %bitcast.17, bf16[32,32,256]{2,1,0:T(8,128)(2,1)} %bitcast.13, bf16[32,32,256]{2,1,0:T(8,128)(2,1)} %bitcast.14), custom_call_target="tpu_custom_call" | custom-call | tf_op jit(solution)/shard_map/pallas_call | solution.py:528
  3.1 13.8 %all-to-all-start = ((bf16[32,96,256]{2,1,0:T(8,128)(2,1)}), bf16[32,96,256]{2,1,0:T(8,128)(2,1)S(1)}, u32[]{:S(2)}, u32[]{:S(2)}) async-start(bf16[32,96,256]{2,1,0:T(8,128)(2,1)} %shard_map.153), calls=%async_computation | async-start | bytes 3145728 | tf_op jit(solution)/shard_map/all_to_all | solution.py:554
  16.9 36.9 %all-to-all-done.r_ref = bf16[32,96,256]{2,1,0:T(8,128)(2,1)S(1)} async-done(((bf16[32,96,256]{2,1,0:T(8,128)(2,1)}), bf16[32,96,256]{2,1,0:T(8,128)(2,1)S(1)}, u32[]{:S(2)}, u32[]{:S(2)}) %all-to-all-start) | async-done | bytes 1572896 | tf_op jit(solution)/shard_map/all_to_all | solution.py:554
  53.9 6.5 %collective-permute-start = (bf16[64,128]{1,0:T(8,128)(2,1)S(1)}, bf16[64,128]{1,0:T(8,128)(2,1)S(1)}, u32[]{:S(2)}, u32[]{:S(2)}) collective-permute-start(bf16[64,128]{1,0:T(8,128)(2,1)S(1)} %slice_bitcast_fusion), channel_id=1, source_target_pairs={{0,32},{32,64},{64,96},{96,128},{128,160},{160,192},{192,224},{224... | collective-permute-start | bytes 49160 | tf_op jit(solution)/shard_map/ppermute | solution.py:565
  60.5 1.6 copy-done
  62.3 2.1 %shard_map.154.part_ref = bf16[512,1024]{1,0:T(8,128)(2,1)S(1)} custom-call(bf16[32,96,256]{2,1,0:T(8,128)(2,1)S(1)} %all-to-all-done.r_ref, f32[32,128]{1,0:T(8,128)S(1)} %pad.8.cols_ref), custom_call_target="tpu_custom_call" | custom-call | flops 16777216 | bytes 4194304 | tf_op jit(solution)/shard_map/pallas_call | solution.py:406
  64.4 2.2 %shard_map.156 = bf16[16,256,128]{2,1,0:T(8,128)(2,1)S(1)} custom-call(bf16[512,1024]{1,0:T(8,128)(2,1)S(1)} %shard_map.154.part_ref, bf16[32,96,256]{2,1,0:T(8,128)(2,1)S(1)} %all-to-all-done.r_ref, bf16[64,128]{1,0:T(8,128)(2,1)S(1)} %collective-permute-done.rim_ref, f32[32,128]{1,0:T(8,128)S(1)} %pad.8.cols_ref, f32[8,1024]{1,0:T(8,128)S(1)} %copy-done.3, ...), custom_call_target="tpu_custom_call" | custom-call | flops 1073741824 | bytes 5242880 | tf_op jit(solution)/shard_map/pallas_call | solution.py:406
  66.7 34.7 %all_to_all.20.f_ref = bf16[16,256,128]{2,1,0:T(8,128)(2,1)S(1)} all-to-all(bf16[16,256,128]{2,1,0:T(8,128)(2,1)S(1)} %shard_map.156), channel_id=1, replica_groups=mesh['batch'=16,'seq'=32] {'batch'}, dimensions={0} | all-to-all | bytes 2097152 | tf_op jit(solution)/shard_map/all_to_all | solution.py:554
  101.4 2.9 %shard_map.157 = (f32[32,64,128]{2,1,0:T(8,128)}, bf16[16,256,128]{2,1,0:T(8,128)(2,1)S(1)}) custom-call(bf16[16,256,128]{2,1,0:T(8,128)(2,1)S(1)} %all_to_all.20.f_ref, bf16[32,64,128]{2,1,0:T(8,128)(2,1)S(1)} %bitcast.15, f32[128,128]{1,0:T(8,128)S(1)} %copy-done.5), custom_call_target="tpu_custom_call" | custom-call | flops 1073741824 | bytes 5242880 | tf_op jit(solution)/shard_map/pallas_call | solution.py:406
  104.3 31.2 %all_to_all.21.y_ref = bf16[16,256,128]{2,1,0:T(8,128)(2,1)S(1)} all-to-all(bf16[16,256,128]{2,1,0:T(8,128)(2,1)S(1)} %get-tuple-element.19), channel_id=1, replica_groups=mesh['batch'=16,'seq'=32] {'batch'}, dimensions={0} | all-to-all | bytes 2097152 | tf_op jit(solution)/shard_map/all_to_all | solution.py:554
  135.5 2.9 %shard_map.158 = (bf16[512,1024]{1,0:T(8,128)(2,1)S(1)}, f32[64,128]{1,0:T(8,128)S(1)}) custom-call(bf16[16,256,128]{2,1,0:T(8,128)(2,1)S(1)} %all_to_all.21.y_ref, bf16[32,96,256]{2,1,0:T(8,128)(2,1)S(1)} %all-to-all-done.r_ref, bf16[64,128]{1,0:T(8,128)(2,1)S(1)} %collective-permute-done.rim_ref, f32[32,128]{1,0:T(8,128)S(1)} %pad.8.cols_ref, ...), custom_call_target="tpu_custom_call" | custom-call | flops 1073741824 | bytes 5242880 | tf_op jit(solution)/shard_map/pallas_call | solution.py:406
  138.4 1.9 %collective-permute-start.1 = (f32[64,128]{1,0:T(8,128)S(1)}, f32[64,128]{1,0:T(8,128)S(1)}, u32[]{:S(2)}, u32[]{:S(2)}) collective-permute-start(f32[64,128]{1,0:T(8,128)S(1)} %get-tuple-element.22), channel_id=1, source_target_pairs={{32,0},{64,32},{96,64},{128,96},{160,128},{192,160},{224,192},{256... | collective-permute-start | bytes 98312 | tf_op jit(solution)/shard_map/ppermute | solution.py:569
  140.3 4.0 %shard_map.159 = (bf16[32,72,256]{2,1,0:T(8,128)(2,1)}, f32[32,128]{1,0:T(8,128)S(1)}, bf16[896,128]{1,0:T(8,128)(2,1)S(1)}) custom-call(bf16[512,1024]{1,0:T(8,128)(2,1)S(1)} %get-tuple-element.20.d_ref, bf16[32,96,256]{2,1,0:T(8,128)(2,1)S(1)} %all-to-all-done.r_ref, bf16[64,128]{1,0:T(8,128)(2,1)S(1)} %collective-permute-done.rim_ref, ...), custom_call_target="tpu_custom_call" | custom-call | flops 33554432 | bytes 8388608 | tf_op jit(solution)/shard_map/pallas_call | solution.py:406
  144.3 1.4 shard_map.160
  145.7 5.5 %all-to-all-start.3 = ((bf16[32,72,256]{2,1,0:T(8,128)(2,1)}), bf16[32,72,256]{2,1,0:T(8,128)(2,1)S(1)}, u32[]{:S(2)}, u32[]{:S(2)}) async-start(bf16[32,72,256]{2,1,0:T(8,128)(2,1)} %get-tuple-element.25), calls=%async_computation.3 | async-start | bytes 2359296 | tf_op jit(solution)/shard_map/all_to_all | solution.py:554
  151.2 1.9 %collective-permute-start.2 = (f32[32,128]{1,0:T(8,128)S(1)}, f32[32,128]{1,0:T(8,128)S(1)}, u32[]{:S(2)}, u32[]{:S(2)}) collective-permute-start(f32[32,128]{1,0:T(8,128)S(1)} %get-tuple-element.30), channel_id=1, source_target_pairs={{0,32},{32,0},{64,96},{96,64},{128,160},{160,128},{192,224},{224,1... | collective-permute-start | bytes 49160 | tf_op jit(solution)/shard_map/ppermute | solution.py:579
  154.3 3.7 %collective-permute-start.3 = (f32[32,128]{1,0:T(8,128)S(1)}, f32[32,128]{1,0:T(8,128)S(1)}, u32[]{:S(2)}, u32[]{:S(2)}) collective-permute-start(f32[32,128]{1,0:T(8,128)S(1)} %add.29), channel_id=1, source_target_pairs={{0,64},{32,96},{64,0},{96,32},{128,192},{160,224},{192,128},{224,1... | collective-permute-start | bytes 49160 | tf_op jit(solution)/shard_map/ppermute | solution.py:579
  158.0 1.4 collective-permute-done.3
  159.4 1.9 %collective-permute-start.4 = (f32[32,128]{1,0:T(8,128)S(1)}, f32[32,128]{1,0:T(8,128)S(1)}, u32[]{:S(2)}, u32[]{:S(2)}) collective-permute-start(f32[32,128]{1,0:T(8,128)S(1)} %add.30), channel_id=1, source_target_pairs={{0,128},{32,160},{64,192},{96,224},{128,0},{160,32},{192,64},{224,... | collective-permute-start | bytes 49160 | tf_op jit(solution)/shard_map/ppermute | solution.py:579
  161.3 3.7 %collective-permute-done.4 = f32[32,128]{1,0:T(8,128)S(1)} collective-permute-done((f32[32,128]{1,0:T(8,128)S(1)}, f32[32,128]{1,0:T(8,128)S(1)}, u32[]{:S(2)}, u32[]{:S(2)}) %collective-permute-start.4) | collective-permute-done | bytes 16416 | tf_op jit(solution)/shard_map/ppermute | solution.py:579
  165.1 5.2 %collective-permute-start.5 = (f32[32,128]{1,0:T(8,128)S(1)}, f32[32,128]{1,0:T(8,128)S(1)}, u32[]{:S(2)}, u32[]{:S(2)}) collective-permute-start(f32[32,128]{1,0:T(8,128)S(1)} %add.31), channel_id=1, source_target_pairs={{0,256},{32,288},{64,320},{96,352},{128,384},{160,416},{192,448},{... | collective-permute-start | bytes 49160 | tf_op jit(solution)/shard_map/ppermute | solution.py:579
  170.6 2.9 %collective-permute-done.5 = f32[32,128]{1,0:T(8,128)S(1)} collective-permute-done((f32[32,128]{1,0:T(8,128)S(1)}, f32[32,128]{1,0:T(8,128)S(1)}, u32[]{:S(2)}, u32[]{:S(2)}) %collective-permute-start.5) | collective-permute-done | bytes 16416 | tf_op jit(solution)/shard_map/ppermute | solution.py:579
  175.6 6.1 %all-to-all-done.3.u_ref = bf16[32,72,256]{2,1,0:T(8,128)(2,1)S(1)} async-done(((bf16[32,72,256]{2,1,0:T(8,128)(2,1)}), bf16[32,72,256]{2,1,0:T(8,128)(2,1)S(1)}, u32[]{:S(2)}, u32[]{:S(2)}) %all-to-all-start.3) | async-done | bytes 1179680 | tf_op jit(solution)/shard_map/all_to_all | solution.py:554
  181.7 3.7 %shard_map.161 = (bf16[1024,256]{1,0:T(8,128)(2,1)}, bf16[32,32,256]{2,1,0:T(8,128)(2,1)}, bf16[1024,256]{1,0:T(8,128)(2,1)}) custom-call(bf16[32,72,256]{2,1,0:T(8,128)(2,1)S(1)} %all-to-all-done.3.u_ref, bf16[1024,256]{1,0:T(8,128)(2,1)S(1)} %copy-done.1, bf16[1024,256]{1,0:T(8,128)(2,1)S(1)} %copy-done.2, f32[1024,128]{1,0:T(8,128)S(1)} %pad.9.cols_ref, ...), custom_call_target="tpu_custom_call" | custom-call | flops 16777216 | bytes 6291456 | tf_op jit(solution)/shard_map/pallas_call | solution.py:406
  (37 shorter events, 4.0 us)
Async XLA Ops:
  3.1 57.3 %copy-start.6 = (f32[3,1024]{1,0:T(4,128)S(1)}, f32[3,1024]{1,0:T(4,128)}, u32[]{:S(2)}) copy-start(f32[3,1024]{1,0:T(4,128)} %param.14) | copy-start | bytes 36868
  3.1 57.3 %copy-start.7 = (f32[3,1024]{1,0:T(4,128)S(1)}, f32[3,1024]{1,0:T(4,128)}, u32[]{:S(2)}) copy-start(f32[3,1024]{1,0:T(4,128)} %param.13) | copy-start | bytes 36868
  3.1 57.3 %copy-start.8 = (f32[1024]{0:T(1024)S(1)}, f32[1024]{0:T(1024)}, u32[]{:S(2)}) copy-start(f32[1024]{0:T(1024)} %param.15) | copy-start | bytes 12292
  3.1 50.8 %all-to-all-start = ((bf16[32,96,256]{2,1,0:T(8,128)(2,1)}), bf16[32,96,256]{2,1,0:T(8,128)(2,1)S(1)}, u32[]{:S(2)}, u32[]{:S(2)}) async-start(bf16[32,96,256]{2,1,0:T(8,128)(2,1)} %shard_map.153), calls=%async_computation | async-start | bytes 3145728 | tf_op jit(solution)/shard_map/all_to_all | solution.py:554
  53.9 10.5 %collective-permute-start = (bf16[64,128]{1,0:T(8,128)(2,1)S(1)}, bf16[64,128]{1,0:T(8,128)(2,1)S(1)}, u32[]{:S(2)}, u32[]{:S(2)}) collective-permute-start(bf16[64,128]{1,0:T(8,128)(2,1)S(1)} %slice_bitcast_fusion), channel_id=1, source_target_pairs={{0,32},{32,64},{64,96},{96,128},{128,160},{160,192},{192,224},{224... | collective-permute-start | bytes 49160 | tf_op jit(solution)/shard_map/ppermute | solution.py:565
  60.5 1.6 copy-start
  62.3 2.1 %copy-start.3 = (f32[8,1024]{1,0:T(8,128)S(1)}, f32[8,1024]{1,0:T(8,128)}, u32[]{:S(2)}) copy-start(f32[8,1024]{1,0:T(8,128)} %tw_ref.3) | copy-start | bytes 98308
  66.6 34.7 %copy-start.4 = (bf16[32,128,64]{1,2,0:T(8,128)(2,1)S(1)}, bf16[32,128,64]{1,2,0:T(8,128)(2,1)}, u32[]{:S(2)}) copy-start(bf16[32,128,64]{1,2,0:T(8,128)(2,1)} %param.18) | copy-start | bytes 1572868
  66.7 34.7 %copy-start.5 = (f32[128,128]{1,0:T(8,128)S(1)}, f32[128,128]{1,0:T(8,128)}, u32[]{:S(2)}) copy-start(f32[128,128]{1,0:T(8,128)} %mix_ref.1) | copy-start | bytes 196612
  138.4 6.0 %collective-permute-start.1 = (f32[64,128]{1,0:T(8,128)S(1)}, f32[64,128]{1,0:T(8,128)S(1)}, u32[]{:S(2)}, u32[]{:S(2)}) collective-permute-start(f32[64,128]{1,0:T(8,128)S(1)} %get-tuple-element.22), channel_id=1, source_target_pairs={{32,0},{64,32},{96,64},{128,96},{160,128},{192,160},{224,192},{256... | collective-permute-start | bytes 98312 | tf_op jit(solution)/shard_map/ppermute | solution.py:569
  145.7 36.0 %copy-start.1 = (bf16[1024,256]{1,0:T(8,128)(2,1)S(1)}, bf16[1024,256]{1,0:T(8,128)(2,1)}, u32[]{:S(2)}) copy-start(bf16[1024,256]{1,0:T(8,128)(2,1)} %g_ref.1) | copy-start | bytes 1572868
  145.7 36.0 %copy-start.2 = (bf16[1024,256]{1,0:T(8,128)(2,1)S(1)}, bf16[1024,256]{1,0:T(8,128)(2,1)}, u32[]{:S(2)}) copy-start(bf16[1024,256]{1,0:T(8,128)(2,1)} %c_ref.1) | copy-start | bytes 1572868
  145.7 36.0 %all-to-all-start.3 = ((bf16[32,72,256]{2,1,0:T(8,128)(2,1)}), bf16[32,72,256]{2,1,0:T(8,128)(2,1)S(1)}, u32[]{:S(2)}, u32[]{:S(2)}) async-start(bf16[32,72,256]{2,1,0:T(8,128)(2,1)} %get-tuple-element.25), calls=%async_computation.3 | async-start | bytes 2359296 | tf_op jit(solution)/shard_map/all_to_all | solution.py:554
  151.2 3.1 %collective-permute-start.2 = (f32[32,128]{1,0:T(8,128)S(1)}, f32[32,128]{1,0:T(8,128)S(1)}, u32[]{:S(2)}, u32[]{:S(2)}) collective-permute-start(f32[32,128]{1,0:T(8,128)S(1)} %get-tuple-element.30), channel_id=1, source_target_pairs={{0,32},{32,0},{64,96},{96,64},{128,160},{160,128},{192,224},{224,1... | collective-permute-start | bytes 49160 | tf_op jit(solution)/shard_map/ppermute | solution.py:579
  154.3 5.1 %collective-permute-start.3 = (f32[32,128]{1,0:T(8,128)S(1)}, f32[32,128]{1,0:T(8,128)S(1)}, u32[]{:S(2)}, u32[]{:S(2)}) collective-permute-start(f32[32,128]{1,0:T(8,128)S(1)} %add.29), channel_id=1, source_target_pairs={{0,64},{32,96},{64,0},{96,32},{128,192},{160,224},{192,128},{224,1... | collective-permute-start | bytes 49160 | tf_op jit(solution)/shard_map/ppermute | solution.py:579
  159.4 5.7 %collective-permute-start.4 = (f32[32,128]{1,0:T(8,128)S(1)}, f32[32,128]{1,0:T(8,128)S(1)}, u32[]{:S(2)}, u32[]{:S(2)}) collective-permute-start(f32[32,128]{1,0:T(8,128)S(1)} %add.30), channel_id=1, source_target_pairs={{0,128},{32,160},{64,192},{96,224},{128,0},{160,32},{192,64},{224,... | collective-permute-start | bytes 49160 | tf_op jit(solution)/shard_map/ppermute | solution.py:579
  165.1 8.5 %collective-permute-start.5 = (f32[32,128]{1,0:T(8,128)S(1)}, f32[32,128]{1,0:T(8,128)S(1)}, u32[]{:S(2)}, u32[]{:S(2)}) collective-permute-start(f32[32,128]{1,0:T(8,128)S(1)} %add.31), channel_id=1, source_target_pairs={{0,256},{32,288},{64,320},{96,352},{128,384},{160,416},{192,448},{... | collective-permute-start | bytes 49160 | tf_op jit(solution)/shard_map/ppermute | solution.py:579

commit v7 on v6

--- a/solution.py
+++ b/solution.py
@@ -12,7 +12,7 @@
 BLOCK = 1024
 F32, BF16 = jnp.float32, jnp.bfloat16
 GRANT = 20 << 20
-PARTS = 8
+PARTS = 4
 
 
 def cas_table():
@@ -133,7 +133,7 @@
                 out_ref[d + 1, m * 16 : m * 16 + 16, :] = odd.astype(BF16)
         return 0
 
-    lax.fori_loop(0, 4, strip, 0)
+    lax.fori_loop(0, 4, strip, 0, unroll=True)
 
 
 def mix_kernel(f_ref, spec_ref, mix_ref, gs_ref, out_ref, wide_v, wide_g):
@@ -194,7 +194,7 @@
         out_ref[:, pl.ds(at, 256)] = sums.astype(BF16)
         return 0
 
-    lax.fori_loop(0, 4, strip, 0)
+    lax.fori_loop(0, 4, strip, 0, unroll=True)
 
     lane = lanes()
     cols = cols_ref[...]

time: 186 us -> 185 us (level)
  no operation moved by 1% of the time
where the time goes in v7:
time: 185 us; the launch traced here: 184 us
  blocking collectives  65.9 us (36%)
  waiting for transfers between devices  52.2 us (28%)
  starting transfers between devices  40.4 us (22%)
  Pallas kernels  20.2 us (11%)
  local copies, waits for them, and re-layouts  4.07 us (2%)
    all_to_all x2, blocking collectives, exchange(): return lax.all_to_all(array, axis, 0, 0, tiled=True)  65.9 us
    all_to_all x2, waiting for transfers between devices, exchange(): return lax.all_to_all(array, axis, 0, 0, tiled=True)  43 us
    all_to_all x2, starting transfers between devices, exchange(): return lax.all_to_all(array, axis, 0, 0, tiled=True)  19.3 us
    pallas_call x7, Pallas kernels, call(): pl.pallas_call(kernel, **{'in_specs': [VMEM] * len(args), 'out_specs': [V...  17.7 us
    ppermute x4, starting transfers between devices, per_device(): lax.ppermute(sums, 'batch', [(i, i ^ step) for i in range(batch)])  12.7 us
    ppermute x4, waiting for transfers between devices, per_device(): lax.ppermute(sums, 'batch', [(i, i ^ step) for i in range(batch)])  9.2 us
    ppermute x1, starting transfers between devices, per_device(): lax.ppermute(r[31, :64, 128:], 'batch', [(i, i + 1) for i in range(batch...  6.46 us
  transfers between devices with their start and end apart: 8, of which 6 were waited for; matrix products, arithmetic and copies ran while one was open for 1% of the time, Pallas kernels for 3%

profile of v7, /device:TPU:1, one launch (start us, length us, event | category | flops | bytes accessed | tf_op | source)
XLA Modules:
  0.0 183.9 jit_solution(1321954714166090457)
XLA Ops:
  0.6 2.4 %shard_map.153 = bf16[32,96,256]{2,1,0:T(8,128)(2,1)} custom-call(bf16[32,32,256]{2,1,0:T(8,128)(2,1)} %bitcast.17, bf16[32,32,256]{2,1,0:T(8,128)(2,1)} %bitcast.13, bf16[32,32,256]{2,1,0:T(8,128)(2,1)} %bitcast.14), custom_call_target="tpu_custom_call" | custom-call | tf_op jit(solution)/shard_map/pallas_call | solution.py:528
  3.0 13.8 %all-to-all-start = ((bf16[32,96,256]{2,1,0:T(8,128)(2,1)}), bf16[32,96,256]{2,1,0:T(8,128)(2,1)S(1)}, u32[]{:S(2)}, u32[]{:S(2)}) async-start(bf16[32,96,256]{2,1,0:T(8,128)(2,1)} %shard_map.153), calls=%async_computation | async-start | bytes 3145728 | tf_op jit(solution)/shard_map/all_to_all | solution.py:554
  16.9 36.9 %all-to-all-done.r_ref = bf16[32,96,256]{2,1,0:T(8,128)(2,1)S(1)} async-done(((bf16[32,96,256]{2,1,0:T(8,128)(2,1)}), bf16[32,96,256]{2,1,0:T(8,128)(2,1)S(1)}, u32[]{:S(2)}, u32[]{:S(2)}) %all-to-all-start) | async-done | bytes 1572896 | tf_op jit(solution)/shard_map/all_to_all | solution.py:554
  53.8 6.5 %collective-permute-start = (bf16[64,128]{1,0:T(8,128)(2,1)S(1)}, bf16[64,128]{1,0:T(8,128)(2,1)S(1)}, u32[]{:S(2)}, u32[]{:S(2)}) collective-permute-start(bf16[64,128]{1,0:T(8,128)(2,1)S(1)} %slice_bitcast_fusion), channel_id=1, source_target_pairs={{0,32},{32,64},{64,96},{96,128},{128,160},{160,192},{192,224},{224... | collective-permute-start | bytes 49160 | tf_op jit(solution)/shard_map/ppermute | solution.py:565
  60.5 1.6 copy-done
  62.3 2.1 %shard_map.154.part_ref = bf16[512,1024]{1,0:T(8,128)(2,1)S(1)} custom-call(bf16[32,96,256]{2,1,0:T(8,128)(2,1)S(1)} %all-to-all-done.r_ref, f32[32,128]{1,0:T(8,128)S(1)} %pad.8.cols_ref), custom_call_target="tpu_custom_call" | custom-call | flops 16777216 | bytes 4194304 | tf_op jit(solution)/shard_map/pallas_call | solution.py:406
  64.4 1.4 shard_map.156
  65.8 34.7 %all_to_all.20.f_ref = bf16[16,256,128]{2,1,0:T(8,128)(2,1)S(1)} all-to-all(bf16[16,256,128]{2,1,0:T(8,128)(2,1)S(1)} %shard_map.156), channel_id=1, replica_groups=mesh['batch'=16,'seq'=32] {'batch'}, dimensions={0} | all-to-all | bytes 2097152 | tf_op jit(solution)/shard_map/all_to_all | solution.py:554
  100.5 2.9 %shard_map.157 = (f32[32,64,128]{2,1,0:T(8,128)}, bf16[16,256,128]{2,1,0:T(8,128)(2,1)S(1)}) custom-call(bf16[16,256,128]{2,1,0:T(8,128)(2,1)S(1)} %all_to_all.20.f_ref, bf16[32,64,128]{2,1,0:T(8,128)(2,1)S(1)} %bitcast.15, f32[128,128]{1,0:T(8,128)S(1)} %copy-done.5), custom_call_target="tpu_custom_call" | custom-call | flops 1073741824 | bytes 5242880 | tf_op jit(solution)/shard_map/pallas_call | solution.py:406
  103.4 31.2 %all_to_all.21.y_ref = bf16[16,256,128]{2,1,0:T(8,128)(2,1)S(1)} all-to-all(bf16[16,256,128]{2,1,0:T(8,128)(2,1)S(1)} %get-tuple-element.19), channel_id=1, replica_groups=mesh['batch'=16,'seq'=32] {'batch'}, dimensions={0} | all-to-all | bytes 2097152 | tf_op jit(solution)/shard_map/all_to_all | solution.py:554
  134.6 2.2 %shard_map.158 = (bf16[512,1024]{1,0:T(8,128)(2,1)S(1)}, f32[64,128]{1,0:T(8,128)S(1)}) custom-call(bf16[16,256,128]{2,1,0:T(8,128)(2,1)S(1)} %all_to_all.21.y_ref, bf16[32,96,256]{2,1,0:T(8,128)(2,1)S(1)} %all-to-all-done.r_ref, bf16[64,128]{1,0:T(8,128)(2,1)S(1)} %collective-permute-done.rim_ref, f32[32,128]{1,0:T(8,128)S(1)} %pad.8.cols_ref, ...), custom_call_target="tpu_custom_call" | custom-call | flops 1073741824 | bytes 5242880 | tf_op jit(solution)/shard_map/pallas_call | solution.py:406
  136.8 1.9 %collective-permute-start.1 = (f32[64,128]{1,0:T(8,128)S(1)}, f32[64,128]{1,0:T(8,128)S(1)}, u32[]{:S(2)}, u32[]{:S(2)}) collective-permute-start(f32[64,128]{1,0:T(8,128)S(1)} %get-tuple-element.22), channel_id=1, source_target_pairs={{32,0},{64,32},{96,64},{128,96},{160,128},{192,160},{224,192},{256... | collective-permute-start | bytes 98312 | tf_op jit(solution)/shard_map/ppermute | solution.py:569
  138.8 4.0 %shard_map.159 = (bf16[32,72,256]{2,1,0:T(8,128)(2,1)}, f32[32,128]{1,0:T(8,128)S(1)}, bf16[896,128]{1,0:T(8,128)(2,1)S(1)}) custom-call(bf16[512,1024]{1,0:T(8,128)(2,1)S(1)} %get-tuple-element.20.d_ref, bf16[32,96,256]{2,1,0:T(8,128)(2,1)S(1)} %all-to-all-done.r_ref, bf16[64,128]{1,0:T(8,128)(2,1)S(1)} %collective-permute-done.rim_ref, ...), custom_call_target="tpu_custom_call" | custom-call | flops 33554432 | bytes 8388608 | tf_op jit(solution)/shard_map/pallas_call | solution.py:406
  142.8 1.4 shard_map.160
  144.2 5.5 %all-to-all-start.3 = ((bf16[32,72,256]{2,1,0:T(8,128)(2,1)}), bf16[32,72,256]{2,1,0:T(8,128)(2,1)S(1)}, u32[]{:S(2)}, u32[]{:S(2)}) async-start(bf16[32,72,256]{2,1,0:T(8,128)(2,1)} %get-tuple-element.25), calls=%async_computation.3 | async-start | bytes 2359296 | tf_op jit(solution)/shard_map/all_to_all | solution.py:554
  149.7 1.9 %collective-permute-start.2 = (f32[32,128]{1,0:T(8,128)S(1)}, f32[32,128]{1,0:T(8,128)S(1)}, u32[]{:S(2)}, u32[]{:S(2)}) collective-permute-start(f32[32,128]{1,0:T(8,128)S(1)} %get-tuple-element.30), channel_id=1, source_target_pairs={{0,32},{32,0},{64,96},{96,64},{128,160},{160,128},{192,224},{224,1... | collective-permute-start | bytes 49160 | tf_op jit(solution)/shard_map/ppermute | solution.py:579
  152.8 3.7 %collective-permute-start.3 = (f32[32,128]{1,0:T(8,128)S(1)}, f32[32,128]{1,0:T(8,128)S(1)}, u32[]{:S(2)}, u32[]{:S(2)}) collective-permute-start(f32[32,128]{1,0:T(8,128)S(1)} %add.29), channel_id=1, source_target_pairs={{0,64},{32,96},{64,0},{96,32},{128,192},{160,224},{192,128},{224,1... | collective-permute-start | bytes 49160 | tf_op jit(solution)/shard_map/ppermute | solution.py:579
  156.5 1.4 collective-permute-done.3
  157.9 1.9 %collective-permute-start.4 = (f32[32,128]{1,0:T(8,128)S(1)}, f32[32,128]{1,0:T(8,128)S(1)}, u32[]{:S(2)}, u32[]{:S(2)}) collective-permute-start(f32[32,128]{1,0:T(8,128)S(1)} %add.30), channel_id=1, source_target_pairs={{0,128},{32,160},{64,192},{96,224},{128,0},{160,32},{192,64},{224,... | collective-permute-start | bytes 49160 | tf_op jit(solution)/shard_map/ppermute | solution.py:579
  159.8 3.7 %collective-permute-done.4 = f32[32,128]{1,0:T(8,128)S(1)} collective-permute-done((f32[32,128]{1,0:T(8,128)S(1)}, f32[32,128]{1,0:T(8,128)S(1)}, u32[]{:S(2)}, u32[]{:S(2)}) %collective-permute-start.4) | collective-permute-done | bytes 16416 | tf_op jit(solution)/shard_map/ppermute | solution.py:579
  163.5 5.2 %collective-permute-start.5 = (f32[32,128]{1,0:T(8,128)S(1)}, f32[32,128]{1,0:T(8,128)S(1)}, u32[]{:S(2)}, u32[]{:S(2)}) collective-permute-start(f32[32,128]{1,0:T(8,128)S(1)} %add.31), channel_id=1, source_target_pairs={{0,256},{32,288},{64,320},{96,352},{128,384},{160,416},{192,448},{... | collective-permute-start | bytes 49160 | tf_op jit(solution)/shard_map/ppermute | solution.py:579
  169.1 2.9 %collective-permute-done.5 = f32[32,128]{1,0:T(8,128)S(1)} collective-permute-done((f32[32,128]{1,0:T(8,128)S(1)}, f32[32,128]{1,0:T(8,128)S(1)}, u32[]{:S(2)}, u32[]{:S(2)}) %collective-permute-start.5) | collective-permute-done | bytes 16416 | tf_op jit(solution)/shard_map/ppermute | solution.py:579
  174.1 6.1 %all-to-all-done.3.u_ref = bf16[32,72,256]{2,1,0:T(8,128)(2,1)S(1)} async-done(((bf16[32,72,256]{2,1,0:T(8,128)(2,1)}), bf16[32,72,256]{2,1,0:T(8,128)(2,1)S(1)}, u32[]{:S(2)}, u32[]{:S(2)}) %all-to-all-start.3) | async-done | bytes 1179680 | tf_op jit(solution)/shard_map/all_to_all | solution.py:554
  180.2 3.7 %shard_map.161 = (bf16[1024,256]{1,0:T(8,128)(2,1)}, bf16[32,32,256]{2,1,0:T(8,128)(2,1)}, bf16[1024,256]{1,0:T(8,128)(2,1)}) custom-call(bf16[32,72,256]{2,1,0:T(8,128)(2,1)S(1)} %all-to-all-done.3.u_ref, bf16[1024,256]{1,0:T(8,128)(2,1)S(1)} %copy-done.1, bf16[1024,256]{1,0:T(8,128)(2,1)S(1)} %copy-done.2, f32[1024,128]{1,0:T(8,128)S(1)} %pad.9.cols_ref, ...), custom_call_target="tpu_custom_call" | custom-call | flops 16777216 | bytes 6291456 | tf_op jit(solution)/shard_map/pallas_call | solution.py:406
  (37 shorter events, 4.0 us)
Async XLA Ops:
  3.0 57.3 %copy-start.6 = (f32[3,1024]{1,0:T(4,128)S(1)}, f32[3,1024]{1,0:T(4,128)}, u32[]{:S(2)}) copy-start(f32[3,1024]{1,0:T(4,128)} %param.14) | copy-start | bytes 36868
  3.0 57.3 %copy-start.7 = (f32[3,1024]{1,0:T(4,128)S(1)}, f32[3,1024]{1,0:T(4,128)}, u32[]{:S(2)}) copy-start(f32[3,1024]{1,0:T(4,128)} %param.13) | copy-start | bytes 36868
  3.0 57.3 %copy-start.8 = (f32[1024]{0:T(1024)S(1)}, f32[1024]{0:T(1024)}, u32[]{:S(2)}) copy-start(f32[1024]{0:T(1024)} %param.15) | copy-start | bytes 12292
  3.0 50.8 %all-to-all-start = ((bf16[32,96,256]{2,1,0:T(8,128)(2,1)}), bf16[32,96,256]{2,1,0:T(8,128)(2,1)S(1)}, u32[]{:S(2)}, u32[]{:S(2)}) async-start(bf16[32,96,256]{2,1,0:T(8,128)(2,1)} %shard_map.153), calls=%async_computation | async-start | bytes 3145728 | tf_op jit(solution)/shard_map/all_to_all | solution.py:554
  53.8 10.5 %collective-permute-start = (bf16[64,128]{1,0:T(8,128)(2,1)S(1)}, bf16[64,128]{1,0:T(8,128)(2,1)S(1)}, u32[]{:S(2)}, u32[]{:S(2)}) collective-permute-start(bf16[64,128]{1,0:T(8,128)(2,1)S(1)} %slice_bitcast_fusion), channel_id=1, source_target_pairs={{0,32},{32,64},{64,96},{96,128},{128,160},{160,192},{192,224},{224... | collective-permute-start | bytes 49160 | tf_op jit(solution)/shard_map/ppermute | solution.py:565
  60.5 1.6 copy-start
  62.2 2.1 %copy-start.3 = (f32[8,1024]{1,0:T(8,128)S(1)}, f32[8,1024]{1,0:T(8,128)}, u32[]{:S(2)}) copy-start(f32[8,1024]{1,0:T(8,128)} %tw_ref.3) | copy-start | bytes 98308
  65.8 34.7 %copy-start.4 = (bf16[32,128,64]{1,2,0:T(8,128)(2,1)S(1)}, bf16[32,128,64]{1,2,0:T(8,128)(2,1)}, u32[]{:S(2)}) copy-start(bf16[32,128,64]{1,2,0:T(8,128)(2,1)} %param.18) | copy-start | bytes 1572868
  65.8 34.7 %copy-start.5 = (f32[128,128]{1,0:T(8,128)S(1)}, f32[128,128]{1,0:T(8,128)}, u32[]{:S(2)}) copy-start(f32[128,128]{1,0:T(8,128)} %mix_ref.1) | copy-start | bytes 196612
  136.8 6.0 %collective-permute-start.1 = (f32[64,128]{1,0:T(8,128)S(1)}, f32[64,128]{1,0:T(8,128)S(1)}, u32[]{:S(2)}, u32[]{:S(2)}) collective-permute-start(f32[64,128]{1,0:T(8,128)S(1)} %get-tuple-element.22), channel_id=1, source_target_pairs={{32,0},{64,32},{96,64},{128,96},{160,128},{192,160},{224,192},{256... | collective-permute-start | bytes 98312 | tf_op jit(solution)/shard_map/ppermute | solution.py:569
  144.2 36.0 %copy-start.1 = (bf16[1024,256]{1,0:T(8,128)(2,1)S(1)}, bf16[1024,256]{1,0:T(8,128)(2,1)}, u32[]{:S(2)}) copy-start(bf16[1024,256]{1,0:T(8,128)(2,1)} %g_ref.1) | copy-start | bytes 1572868
  144.2 36.0 %copy-start.2 = (bf16[1024,256]{1,0:T(8,128)(2,1)S(1)}, bf16[1024,256]{1,0:T(8,128)(2,1)}, u32[]{:S(2)}) copy-start(bf16[1024,256]{1,0:T(8,128)(2,1)} %c_ref.1) | copy-start | bytes 1572868
  144.2 36.0 %all-to-all-start.3 = ((bf16[32,72,256]{2,1,0:T(8,128)(2,1)}), bf16[32,72,256]{2,1,0:T(8,128)(2,1)S(1)}, u32[]{:S(2)}, u32[]{:S(2)}) async-start(bf16[32,72,256]{2,1,0:T(8,128)(2,1)} %get-tuple-element.25), calls=%async_computation.3 | async-start | bytes 2359296 | tf_op jit(solution)/shard_map/all_to_all | solution.py:554
  149.7 3.1 %collective-permute-start.2 = (f32[32,128]{1,0:T(8,128)S(1)}, f32[32,128]{1,0:T(8,128)S(1)}, u32[]{:S(2)}, u32[]{:S(2)}) collective-permute-start(f32[32,128]{1,0:T(8,128)S(1)} %get-tuple-element.30), channel_id=1, source_target_pairs={{0,32},{32,0},{64,96},{96,64},{128,160},{160,128},{192,224},{224,1... | collective-permute-start | bytes 49160 | tf_op jit(solution)/shard_map/ppermute | solution.py:579
  152.8 5.1 %collective-permute-start.3 = (f32[32,128]{1,0:T(8,128)S(1)}, f32[32,128]{1,0:T(8,128)S(1)}, u32[]{:S(2)}, u32[]{:S(2)}) collective-permute-start(f32[32,128]{1,0:T(8,128)S(1)} %add.29), channel_id=1, source_target_pairs={{0,64},{32,96},{64,0},{96,32},{128,192},{160,224},{192,128},{224,1... | collective-permute-start | bytes 49160 | tf_op jit(solution)/shard_map/ppermute | solution.py:579
  157.9 5.7 %collective-permute-start.4 = (f32[32,128]{1,0:T(8,128)S(1)}, f32[32,128]{1,0:T(8,128)S(1)}, u32[]{:S(2)}, u32[]{:S(2)}) collective-permute-start(f32[32,128]{1,0:T(8,128)S(1)} %add.30), channel_id=1, source_target_pairs={{0,128},{32,160},{64,192},{96,224},{128,0},{160,32},{192,64},{224,... | collective-permute-start | bytes 49160 | tf_op jit(solution)/shard_map/ppermute | solution.py:579
  163.5 8.5 %collective-permute-start.5 = (f32[32,128]{1,0:T(8,128)S(1)}, f32[32,128]{1,0:T(8,128)S(1)}, u32[]{:S(2)}, u32[]{:S(2)}) collective-permute-start(f32[32,128]{1,0:T(8,128)S(1)} %add.31), channel_id=1, source_target_pairs={{0,256},{32,288},{64,320},{96,352},{128,384},{160,416},{192,448},{... | collective-permute-start | bytes 49160 | tf_op jit(solution)/shard_map/ppermute | solution.py:579
